TPU v7x, 768 devices: a whole 4x8x12 slice. The times are simulated.
768 devices in a mesh: dp: 16 (over y_lo, x), enode: 12 (over z), echip: 4 (over y_hi, core).
Axes of the slice: x: 4, y: 8 (y_hi: 2, y_lo: 4; y = y_hi * 4 + y_lo), z: 12, core: 2. Of those that a mesh axis runs over, the one named last changes fastest.
Arguments:
- hidden: bfloat16 [4608, 7168], P(('dp', 'enode', 'echip')), may hold values from -6 to 6
- grad_out: bfloat16 [4608, 7168], P(('dp', 'enode', 'echip')), may hold values from -6 to 6
- routes: int32 [16, 12, 4, 6, 2], P('dp', None, 'echip'), may hold values from 0 to 3, as said below
- combine: float32 [16, 12, 4, 6, 2], P('dp', None, 'echip'), may hold values from 0.1 to 0.7
- w_gate: bfloat16 [4, 7168, 1536], P('echip', None, 'enode'), may hold values from -0.0625 to 0.0625
- w_up: bfloat16 [4, 7168, 1536], P('echip', None, 'enode'), may hold values from -0.0625 to 0.0625
- w_down: bfloat16 [4, 1536, 7168], P('echip', 'enode'), may hold values from -0.15625 to 0.15625
Outputs:
- layer_out: bfloat16 [4608, 7168], P(('dp', 'enode', 'echip'))
- grad_in: bfloat16 [4608, 7168], P(('dp', 'enode', 'echip'))
- grad_gate: bfloat16 [4, 7168, 1536], P('echip', 'dp', 'enode')
- grad_up: bfloat16 [4, 7168, 1536], P('echip', 'dp', 'enode')
- grad_down: bfloat16 [4, 1536, 7168], P('echip', 'enode', 'dp')
Inputs may be any that keep to these rules, and one draw needn't show every extreme that they name: `routes`: each token names 2 different experts, and the 6 tokens of each device name every expert exactly 6 * 2 / 4 times.
All inputs are finite; a program needn't handle non-finite values.
Results may differ from a plain program's by a relative error of at most 0.015.
Values may be sent and summed in bfloat16 or wider, within the bound.
No kernel may reach another device: no remote copies, remote signals or barrier semaphores. Data moves between devices by JAX's collectives and lax.ppermute only.
A program may use at most 64 MiB of HBM per device.

v0:
```python
import jax
import jax.numpy as jnp
from jax import lax
from jax.sharding import PartitionSpec as P


def dispatch_plan(expert_ids, gate_wts, experts):
    token_count, topk_count = expert_ids.shape
    entry_count = token_count * topk_count
    flat_ids = expert_ids.reshape(entry_count)
    slot_count = entry_count // experts
    onehot = (flat_ids[:, None] == jnp.arange(experts)[None, :]).astype(jnp.int32)
    rank_in = jnp.sum((jnp.cumsum(onehot, axis=0) - 1) * onehot, axis=1)
    slot_of = flat_ids * slot_count + rank_in
    placing = (slot_of[:, None] == jnp.arange(experts * slot_count)[None, :]).astype(jnp.float32)
    owners = (
        (jnp.arange(entry_count) // topk_count)[:, None] == jnp.arange(token_count)[None, :]
    ).astype(jnp.float32)
    select = jnp.dot(placing.T, owners, precision=lax.Precision.HIGHEST)
    row_weight = jnp.dot(placing.T, gate_wts.reshape(entry_count), precision=lax.Precision.HIGHEST)
    return (select, row_weight, slot_count)


def make_rows(select, row_weight, tokens, cotangents):
    select_b = select.astype(jnp.bfloat16)
    send_tok = jnp.dot(select_b, tokens, preferred_element_type=jnp.float32).astype(jnp.bfloat16)
    picked_grad = jnp.dot(select_b, cotangents, preferred_element_type=jnp.float32)
    send_cot = (picked_grad * row_weight[:, None]).astype(jnp.bfloat16)
    return (send_tok, send_cot)


def expert_pass(token_rows, cot_rows, gate_mat, up_mat, down_mat):
    contract_last = (((1,), (1,)), ((), ()))
    gate_pre = jnp.dot(token_rows, gate_mat, preferred_element_type=jnp.float32)
    up_pre = jnp.dot(token_rows, up_mat, preferred_element_type=jnp.float32)
    sigmoid_gate = jax.nn.sigmoid(gate_pre)
    hid_b = (gate_pre * sigmoid_gate * up_pre).astype(jnp.bfloat16)
    part_out = jnp.dot(hid_b, down_mat, preferred_element_type=jnp.float32)
    hidden_grad = lax.dot_general(
        cot_rows, down_mat, contract_last, preferred_element_type=jnp.float32
    )
    dgate_b = (
        hidden_grad * up_pre * sigmoid_gate * (1.0 + gate_pre * (1.0 - sigmoid_gate))
    ).astype(jnp.bfloat16)
    dup_b = (hidden_grad * gate_pre * sigmoid_gate).astype(jnp.bfloat16)
    part_dx = lax.dot_general(dgate_b, gate_mat, contract_last, preferred_element_type=jnp.float32)
    part_dx = part_dx + lax.dot_general(
        dup_b, up_mat, contract_last, preferred_element_type=jnp.float32
    )
    return (part_out, part_dx, hid_b, dgate_b, dup_b)


def group_total(form, left, right):
    partial_value = jnp.einsum(form, left, right, preferred_element_type=jnp.float32)
    rounded = lax.optimization_barrier(partial_value.astype(jnp.bfloat16))
    return jnp.sum(rounded.astype(jnp.float32), axis=0).astype(jnp.bfloat16)


def local(hidden, grad_out, routes, combine, w_gate, w_up, w_down):
    experts = lax.axis_size("echip")
    node_count = lax.axis_size("enode")
    tok_count = hidden.shape[0]
    topk_count = routes.shape[4]
    model_width = hidden.shape[1]
    gate_mat = w_gate[0]
    up_mat = w_up[0]
    down_mat = w_down[0]
    col_ids = routes[0, :, 0].reshape(node_count * tok_count, topk_count)
    col_wts = combine[0, :, 0].reshape(node_count * tok_count, topk_count)
    select, row_weight, slot_count = dispatch_plan(col_ids, col_wts, experts)
    col_tokens, col_grads = (
        lax.all_gather(hidden, "enode", axis=0, tiled=True),
        lax.all_gather(grad_out, "enode", axis=0, tiled=True),
    )
    send_tok, send_cot = make_rows(select, row_weight, col_tokens, col_grads)
    got_tok, got_cot = (
        lax.all_to_all(
            send_tok.reshape(experts, slot_count, model_width),
            "echip",
            split_axis=0,
            concat_axis=0,
            tiled=True,
        ),
        lax.all_to_all(
            send_cot.reshape(experts, slot_count, model_width),
            "echip",
            split_axis=0,
            concat_axis=0,
            tiled=True,
        ),
    )
    token_rows = got_tok.reshape(experts * slot_count, model_width)
    cot_rows = got_cot.reshape(experts * slot_count, model_width)
    part_out, part_dx, hid_b, dgate_b, dup_b = expert_pass(
        token_rows, cot_rows, gate_mat, up_mat, down_mat
    )
    back_out, back_dx = (
        lax.all_to_all(
            part_out.astype(jnp.bfloat16).reshape(experts, slot_count, model_width),
            "echip",
            split_axis=0,
            concat_axis=0,
            tiled=True,
        ),
        lax.all_to_all(
            part_dx.astype(jnp.bfloat16).reshape(experts, slot_count, model_width),
            "echip",
            split_axis=0,
            concat_axis=0,
            tiled=True,
        ),
    )
    weighted = (
        back_out.reshape(experts * slot_count, model_width).astype(jnp.float32)
        * row_weight[:, None]
    )
    mixed_out = jnp.dot(select.T, weighted, precision=lax.Precision.HIGHEST)
    mixed_dx = jnp.dot(
        select.T,
        back_dx.reshape(experts * slot_count, model_width).astype(jnp.float32),
        precision=lax.Precision.HIGHEST,
    )
    layer_sum, grad_sum = (
        lax.psum_scatter(
            mixed_out.astype(jnp.bfloat16), "enode", scatter_dimension=0, tiled=True
        ).astype(jnp.float32),
        lax.psum_scatter(
            mixed_dx.astype(jnp.bfloat16), "enode", scatter_dimension=0, tiled=True
        ).astype(jnp.float32),
    )
    layer_out = layer_sum.astype(jnp.bfloat16)
    grad_in = grad_sum.astype(jnp.bfloat16)
    groups = lax.axis_size("dp")
    row_count = token_rows.shape[0]
    col_tok, col_cot = (
        lax.all_to_all(token_rows, "dp", split_axis=1, concat_axis=0, tiled=True),
        lax.all_to_all(cot_rows, "dp", split_axis=1, concat_axis=0, tiled=True),
    )
    all_dgate, all_dup, all_hid = (
        lax.all_gather(dgate_b, "dp", axis=0, tiled=True),
        lax.all_gather(dup_b, "dp", axis=0, tiled=True),
        lax.all_gather(hid_b, "dp", axis=0, tiled=True),
    )
    tok_groups = col_tok.reshape(groups, row_count, -1)
    cot_groups = col_cot.reshape(groups, row_count, -1)
    dgate_groups = all_dgate.reshape(groups, row_count, -1)
    dup_groups = all_dup.reshape(groups, row_count, -1)
    hid_groups = all_hid.reshape(groups, row_count, -1)
    grad_gate = group_total("grd,grf->gdf", tok_groups, dgate_groups)[None]
    grad_up = group_total("grd,grf->gdf", tok_groups, dup_groups)[None]
    grad_down = group_total("grf,grd->gfd", hid_groups, cot_groups)[None]
    return (layer_out, grad_in, grad_gate, grad_up, grad_down)


def solution(mesh):
    placed = (
        P(("dp", "enode", "echip"), None),
        P(("dp", "enode", "echip"), None),
        P("dp", None, "echip", None, None),
        P("dp", None, "echip", None, None),
        P("echip", None, "enode"),
        P("echip", None, "enode"),
        P("echip", "enode", None),
    )
    return jax.shard_map(
        local,
        mesh=mesh,
        in_specs=placed,
        out_specs=(
            P(("dp", "enode", "echip"), None),
            P(("dp", "enode", "echip"), None),
            P("echip", "dp", "enode"),
            P("echip", "dp", "enode"),
            P("echip", "enode", "dp"),
        ),
        check_vma=False,
    )
```

profile of v0, /device:TPU:2, one launch (start us, length us, event | category | flops | bytes accessed | tf_op | source)
XLA Modules:
  0.0 572.8 jit_solution(16405203838839608063)
XLA Ops:
  3.4 42.0 %all-gather = bf16[12,6,7168]{2,1,0:T(8,128)(2,1)S(1)} all-gather(bf16[1,6,7168]{2,1,0:T(8,128)(2,1)} %bitcast.77), channel_id=1, replica_groups=mesh['dp'=16,'enode'=12,'echip'=4] {'enode'}, dimensions={0}, use_global_device_ids=true | all-gather | bytes 1118208 | tf_op jit(solution)/shard_map/all_gather | solution.py:72
  47.1 3.2 convolution_convert_fusion.1
  50.3 2.8 reshape.91
  53.2 7.2 %all-to-all-start = ((bf16[4,36,7168]{2,1,0:T(8,128)(2,1)}), bf16[4,36,7168]{2,1,0:T(8,128)(2,1)}, u32[]{:S(2)}, u32[]{:S(2)}) async-start(bf16[4,36,7168]{2,1,0:T(8,128)(2,1)} %reshape.91), calls=%async_computation | async-start | bytes 4587520 | tf_op jit(solution)/shard_map/all_to_all | solution.py:77
  60.7 28.7 %all-gather.1 = bf16[12,6,7168]{2,1,0:T(8,128)(2,1)S(1)} all-gather(bf16[1,6,7168]{2,1,0:T(8,128)(2,1)S(1)} %bitcast.78), channel_id=1, replica_groups=mesh['dp'=16,'enode'=12,'echip'=4] {'enode'}, dimensions={0}, use_global_device_ids=true | all-gather | bytes 1118208 | tf_op jit(solution)/shard_map/all_gather | solution.py:73
  90.9 3.3 fusion.2
  94.2 2.8 reshape.94
  97.0 14.6 %all-to-all-done = bf16[4,36,7168]{2,1,0:T(8,128)(2,1)} async-done(((bf16[4,36,7168]{2,1,0:T(8,128)(2,1)}), bf16[4,36,7168]{2,1,0:T(8,128)(2,1)}, u32[]{:S(2)}, u32[]{:S(2)}) %all-to-all-start) | async-done | bytes 2064416 | tf_op jit(solution)/shard_map/all_to_all | solution.py:77
  111.7 4.5 all-to-all-start.2
  116.2 2.9 reshape.92
  119.1 3.0 fusion.16
  123.1 49.5 %all-to-all-done.2 = bf16[4,36,7168]{2,1,0:T(8,128)(2,1)} async-done(((bf16[4,36,7168]{2,1,0:T(8,128)(2,1)}), bf16[4,36,7168]{2,1,0:T(8,128)(2,1)}, u32[]{:S(2)}, u32[]{:S(2)}) %all-to-all-start.2) | async-done | bytes 2064416 | tf_op jit(solution)/shard_map/all_to_all | solution.py:84
  172.5 2.9 reshape.95
  175.4 2.3 multiply_convert_fusion
  177.7 2.0 convolution_convert_fusion
  179.7 2.8 reshape.93
  182.6 4.5 all-to-all-start.1
  187.1 2.3 fusion.18
  189.4 2.0 fusion.3
  191.4 2.8 reshape.96
  194.3 49.0 %all-to-all-done.1 = bf16[4,36,7168]{2,1,0:T(8,128)(2,1)} async-done(((bf16[4,36,7168]{2,1,0:T(8,128)(2,1)}), bf16[4,36,7168]{2,1,0:T(8,128)(2,1)}, u32[]{:S(2)}, u32[]{:S(2)}) %all-to-all-start.1) | async-done | bytes 2064416 | tf_op jit(solution)/shard_map/all_to_all | solution.py:98
  243.3 4.5 all-to-all-start.3
  247.8 5.3 all_to_all.43
  253.1 4.4 copy.25
  257.5 22.3 %all-to-all-done.3 = bf16[4,36,7168]{2,1,0:T(8,128)(2,1)} async-done(((bf16[4,36,7168]{2,1,0:T(8,128)(2,1)}), bf16[4,36,7168]{2,1,0:T(8,128)(2,1)}, u32[]{:S(2)}, u32[]{:S(2)}) %all-to-all-start.3) | async-done | bytes 2064416 | tf_op jit(solution)/shard_map/all_to_all | solution.py:105
  279.9 30.9 %all-to-all-start.5 = ((bf16[144,16,448]{2,0,1:T(8,128)(2,1)}), bf16[144,16,448]{2,0,1:T(8,128)(2,1)}, u32[]{:S(2)}, u32[]{:S(2)}) async-start(bf16[144,16,448]{2,0,1:T(8,128)(2,1)} %copy.25), calls=%async_computation.5 | async-start | bytes 4718592 | tf_op jit(solution)/shard_map/all_to_all | solution.py:137
  312.7 5.3 all_to_all.40
  318.0 4.5 copy.24
  322.4 65.7 %all_gather.18 = bf16[2304,128]{1,0:T(8,128)(2,1)S(1)} all-gather(bf16[144,128]{1,0:T(8,128)(2,1)S(1)} %get-tuple-element.9), channel_id=1, replica_groups=mesh['dp'=16,'enode'=12,'echip'=4] {'dp'}, dimensions={0}, use_global_device_ids=true | all-gather | bytes 626688 | tf_op jit(solution)/shard_map/all_gather | solution.py:141
  388.2 3.4 reshape.102
  391.6 2.9 reshape.97
  394.5 4.7 convolution_convert_fusion.2
  399.2 9.2 %all-to-all-start.4 = ((bf16[144,16,448]{2,0,1:T(8,128)(2,1)}), bf16[144,16,448]{2,0,1:T(8,128)(2,1)}, u32[]{:S(2)}, u32[]{:S(2)}) async-start(bf16[144,16,448]{2,0,1:T(8,128)(2,1)} %copy.24), calls=%async_computation.4 | async-start | bytes 4718592 | tf_op jit(solution)/shard_map/all_to_all | solution.py:136
  408.4 2.6 convolution_convert_fusion.3
  411.1 32.3 %fusion.40 = (bf16[8,7168]{1,0:T(8,128)(2,1)S(1)}, bf16[8,7168]{1,0:T(8,128)(2,1)S(1)}) fusion(bf16[72,7168]{1,0:T(8,128)(2,1)S(1)} %convolution_convert_fusion.2, bf16[72,7168]{1,0:T(8,128)(2,1)S(1)} %convolution_convert_fusion.3), kind=kCustom, calls=%all-reduce-scatter.2 | all-reduce-scatter fusion | flops 1376257 | bytes 2297856
  443.4 4.2 collective-permute-start.2
  447.7 40.8 %all_gather.17 = bf16[2304,128]{1,0:T(8,128)(2,1)S(1)} all-gather(bf16[144,128]{1,0:T(8,128)(2,1)S(1)} %copy-done.8), channel_id=1, replica_groups=mesh['dp'=16,'enode'=12,'echip'=4] {'dp'}, dimensions={0}, use_global_device_ids=true | all-gather | bytes 626688 | tf_op jit(solution)/shard_map/all_gather | solution.py:140
  488.5 3.8 collective-permute-start.1
  492.3 3.0 collective-permute-start
  495.3 5.0 collective-permute-start.4
  500.3 1.9 collective-permute-start.3
  502.2 1.9 collective-permute-start.5
  504.2 47.6 %all_gather.19 = bf16[2304,128]{1,0:T(8,128)(2,1)} all-gather(bf16[144,128]{1,0:T(8,128)(2,1)S(1)} %copy-done.6), channel_id=1, replica_groups=mesh['dp'=16,'enode'=12,'echip'=4] {'dp'}, dimensions={0}, use_global_device_ids=true | all-gather | bytes 626688 | tf_op jit(solution)/shard_map/all_gather | solution.py:142
  555.3 3.2 fusion.28
  558.5 4.2 fusion.25
  563.6 2.4 reduce_sum.47
  566.1 4.3 fusion.22
  570.4 2.4 reduce_sum.46
  (60 shorter events, 12.9 us)
Async XLA Ops:
  0.6 174.8 %copy-start = (bf16[1,128,7168]{2,1,0:T(8,128)(2,1)S(1)}, bf16[1,128,7168]{2,1,0:T(8,128)(2,1)}, u32[]{:S(2)}) copy-start(bf16[1,128,7168]{2,1,0:T(8,128)(2,1)} %param.13) | copy-start | bytes 5505028
  53.2 7.2 %copy-start.10 = (f32[1,12,1,6,2]{1,4,3,2,0:T(2,128)S(1)}, f32[1,12,1,6,2]{1,4,3,2,0:T(2,128)}, u32[]{:S(2)}) copy-start(f32[1,12,1,6,2]{1,4,3,2,0:T(2,128)} %param.10) | copy-start | bytes 1732
  53.2 7.5 %copy-start.9 = (bf16[6,7168]{1,0:T(8,128)(2,1)S(1)}, bf16[6,7168]{1,0:T(8,128)(2,1)}, u32[]{:S(2)}) copy-start(bf16[6,7168]{1,0:T(8,128)(2,1)} %param.8) | copy-start | bytes 258052
  53.2 58.5 %all-to-all-start = ((bf16[4,36,7168]{2,1,0:T(8,128)(2,1)}), bf16[4,36,7168]{2,1,0:T(8,128)(2,1)}, u32[]{:S(2)}, u32[]{:S(2)}) async-start(bf16[4,36,7168]{2,1,0:T(8,128)(2,1)} %reshape.91), calls=%async_computation | async-start | bytes 4587520 | tf_op jit(solution)/shard_map/all_to_all | solution.py:77
  111.7 60.9 %all-to-all-start.2 = ((bf16[4,36,7168]{2,1,0:T(8,128)(2,1)}), bf16[4,36,7168]{2,1,0:T(8,128)(2,1)}, u32[]{:S(2)}, u32[]{:S(2)}) async-start(bf16[4,36,7168]{2,1,0:T(8,128)(2,1)} %reshape.94), calls=%async_computation.2 | async-start | bytes 4587520 | tf_op jit(solution)/shard_map/all_to_all | solution.py:84
  119.1 3.0 copy-start.2
  119.1 3.3 copy-start.4
  177.7 4.9 copy-start.5
  177.7 9.3 %copy-start.7 = (bf16[144,128]{1,0:T(8,128)(2,1)}, bf16[144,128]{1,0:T(8,128)(2,1)S(1)}, u32[]{:S(2)}) copy-start(bf16[144,128]{1,0:T(8,128)(2,1)S(1)} %get-tuple-element.10) | copy-start | bytes 110596
  182.6 60.7 %all-to-all-start.1 = ((bf16[4,36,7168]{2,1,0:T(8,128)(2,1)}), bf16[4,36,7168]{2,1,0:T(8,128)(2,1)}, u32[]{:S(2)}, u32[]{:S(2)}) async-start(bf16[4,36,7168]{2,1,0:T(8,128)(2,1)} %reshape.93), calls=%async_computation.1 | async-start | bytes 4587520 | tf_op jit(solution)/shard_map/all_to_all | solution.py:98
  187.1 2.4 copy-start.3
  243.3 36.6 %all-to-all-start.3 = ((bf16[4,36,7168]{2,1,0:T(8,128)(2,1)}), bf16[4,36,7168]{2,1,0:T(8,128)(2,1)}, u32[]{:S(2)}, u32[]{:S(2)}) async-start(bf16[4,36,7168]{2,1,0:T(8,128)(2,1)} %reshape.96), calls=%async_computation.3 | async-start | bytes 4587520 | tf_op jit(solution)/shard_map/all_to_all | solution.py:105
  279.9 119.3 %all-to-all-start.5 = ((bf16[144,16,448]{2,0,1:T(8,128)(2,1)}), bf16[144,16,448]{2,0,1:T(8,128)(2,1)}, u32[]{:S(2)}, u32[]{:S(2)}) async-start(bf16[144,16,448]{2,0,1:T(8,128)(2,1)} %copy.25), calls=%async_computation.5 | async-start | bytes 4718592 | tf_op jit(solution)/shard_map/all_to_all | solution.py:137
  399.2 159.3 %all-to-all-start.4 = ((bf16[144,16,448]{2,0,1:T(8,128)(2,1)}), bf16[144,16,448]{2,0,1:T(8,128)(2,1)}, u32[]{:S(2)}, u32[]{:S(2)}) async-start(bf16[144,16,448]{2,0,1:T(8,128)(2,1)} %copy.24), calls=%async_computation.4 | async-start | bytes 4718592 | tf_op jit(solution)/shard_map/all_to_all | solution.py:136
  408.4 39.2 %copy-start.8 = (bf16[144,128]{1,0:T(8,128)(2,1)S(1)}, bf16[144,128]{1,0:T(8,128)(2,1)}, u32[]{:S(2)}) copy-start(bf16[144,128]{1,0:T(8,128)(2,1)} %copy-done.7) | copy-start | bytes 110596
  411.0 93.1 %copy-start.6 = (bf16[144,128]{1,0:T(8,128)(2,1)S(1)}, bf16[144,128]{1,0:T(8,128)(2,1)}, u32[]{:S(2)}) copy-start(bf16[144,128]{1,0:T(8,128)(2,1)} %copy-done.5) | copy-start | bytes 110596
  443.4 58.8 %collective-permute-start.2 = (bf16[6,7168]{1,0:T(8,128)(2,1)S(1)}, bf16[6,7168]{1,0:T(8,128)(2,1)S(1)}, u32[]{:S(2)}, u32[]{:S(2)}) collective-permute-start(bf16[6,7168]{1,0:T(8,128)(2,1)S(1)} %slice.14), channel_id=1, source_target_pairs={{0,12},{4,16},{8,20},{12,24},{16,28},{20,32},{24,36},{28,40},{32,4... | collective-permute-start | bytes 258056
  488.5 63.4 %collective-permute-start.1 = (bf16[8,7168]{1,0:T(8,128)(2,1)S(1)}, bf16[8,7168]{1,0:T(8,128)(2,1)S(1)}, u32[]{:S(2)}, u32[]{:S(2)}) collective-permute-start(bf16[8,7168]{1,0:T(8,128)(2,1)S(1)} %get-tuple-element.7), channel_id=1, source_target_pairs={{0,8},{4,12},{8,16},{12,20},{16,24},{20,28},{24,32},{28,36},{32,40... | collective-permute-start | bytes 344072
  492.3 59.5 %collective-permute-start = (bf16[8,7168]{1,0:T(8,128)(2,1)S(1)}, bf16[8,7168]{1,0:T(8,128)(2,1)S(1)}, u32[]{:S(2)}, u32[]{:S(2)}) collective-permute-start(bf16[8,7168]{1,0:T(8,128)(2,1)S(1)} %get-tuple-element.7), channel_id=1, source_target_pairs={{0,4},{4,8},{8,12},{12,16},{16,20},{20,24},{24,28},{28,32},{32,36}... | collective-permute-start | bytes 344072
  495.3 57.6 %collective-permute-start.4 = (bf16[8,7168]{1,0:T(8,128)(2,1)S(1)}, bf16[8,7168]{1,0:T(8,128)(2,1)S(1)}, u32[]{:S(2)}, u32[]{:S(2)}) collective-permute-start(bf16[8,7168]{1,0:T(8,128)(2,1)S(1)} %get-tuple-element.8), channel_id=1, source_target_pairs={{0,8},{4,12},{8,16},{12,20},{16,24},{20,28},{24,32},{28,36},{32,40... | collective-permute-start | bytes 344072
  500.3 52.6 %collective-permute-start.3 = (bf16[8,7168]{1,0:T(8,128)(2,1)S(1)}, bf16[8,7168]{1,0:T(8,128)(2,1)S(1)}, u32[]{:S(2)}, u32[]{:S(2)}) collective-permute-start(bf16[8,7168]{1,0:T(8,128)(2,1)S(1)} %get-tuple-element.8), channel_id=1, source_target_pairs={{0,4},{4,8},{8,12},{12,16},{16,20},{20,24},{24,28},{28,32},{32,36}... | collective-permute-start | bytes 344072
  502.2 50.6 %collective-permute-start.5 = (bf16[6,7168]{1,0:T(8,128)(2,1)S(1)}, bf16[6,7168]{1,0:T(8,128)(2,1)S(1)}, u32[]{:S(2)}, u32[]{:S(2)}) collective-permute-start(bf16[6,7168]{1,0:T(8,128)(2,1)S(1)} %slice.15), channel_id=1, source_target_pairs={{0,12},{4,16},{8,20},{12,24},{16,28},{20,32},{24,36},{28,40},{32,4... | collective-permute-start | bytes 258056
  566.1 6.8 %copy-start.1 = (bf16[1,128,7168]{2,1,0:T(8,128)(2,1)S(1)}, bf16[1,128,7168]{2,1,0:T(8,128)(2,1)}, u32[]{:S(2)}) copy-start(bf16[1,128,7168]{2,1,0:T(8,128)(2,1)} %param.13) | copy-start | bytes 5505028
where the time goes:
time: 574 us; the launch traced here: 573 us
  blocking collectives  257 us (45%)
  waiting for transfers between devices  136 us (24%)
  starting transfers between devices  80.7 us (14%)
  local copies, waits for them, and re-layouts  52.4 us (9%)
  matrix products  38.2 us (7%)
  other arithmetic  7.13 us (1%)
    all_gather x1, blocking collectives, local(): lax.all_gather(dup_b, 'dp', axis=0, tiled=True)  65.7 us
    all_to_all x1, waiting for transfers between devices, local(): lax.all_to_all(send_cot.reshape(experts, slot_count, model_width), 'echip...  49.5 us
    all_to_all x1, waiting for transfers between devices, local(): lax.all_to_all(part_out.astype(jnp.bfloat16).reshape(experts, slot_count,...  49 us
    all_gather x1, blocking collectives, local(): lax.all_gather(hid_b, 'dp', axis=0, tiled=True)  47.6 us
    all_gather x1, blocking collectives, local(): lax.all_gather(hidden, 'enode', axis=0, tiled=True)  42 us
    all_gather x1, blocking collectives, local(): lax.all_gather(dgate_b, 'dp', axis=0, tiled=True)  40.8 us
    unnamed x1, blocking collectives  32.3 us
    all_to_all x1, starting transfers between devices, local(): lax.all_to_all(cot_rows, 'dp', split_axis=1, concat_axis=0, tiled=True)  30.9 us
  transfers between devices with their start and end apart: 12, of which 4 were waited for; matrix products, arithmetic and copies ran while one was open for 15% of the time, Pallas kernels for 0%

commit v1 on v0

v1 whole, which is shorter than its diff:
```python
import jax
import jax.numpy as jnp
from jax import lax
from jax.sharding import Mesh, PartitionSpec as P


def slot_plan(expert_ids, gate_wts, experts):
    token_count, topk_count = expert_ids.shape
    entry_count = token_count * topk_count
    slots = entry_count // experts
    ids = expert_ids.reshape(entry_count)
    order = jnp.arange(entry_count)
    earlier = (ids[None, :] == ids[:, None]) & (order[None, :] < order[:, None])
    rank = jnp.sum(earlier.astype(jnp.int32), axis=1)
    row_of = ids * (2 * slots) + rank
    rows = jnp.arange(experts * 2 * slots)
    hit_tok = (rows[:, None] == row_of[None, :]).astype(jnp.float32)
    hit_cot = (rows[:, None] == (row_of + slots)[None, :]).astype(jnp.float32)
    wts = gate_wts.reshape(1, entry_count)
    pick_tok = jnp.sum(hit_tok.reshape(-1, token_count, topk_count), axis=2)
    pick_cot = jnp.sum(hit_cot.reshape(-1, token_count, topk_count), axis=2)
    mix_out = jnp.sum((hit_cot * wts).reshape(-1, token_count, topk_count), axis=2)
    cot_weight = jnp.sum(hit_cot * wts, axis=1)
    return pick_tok, pick_cot, mix_out, cot_weight, slots


def local(hidden, grad_out, routes, combine, w_gate, w_up, w_down):
    experts = lax.axis_size("yh") * lax.axis_size("c")
    width = hidden.shape[1]
    f_dev = w_gate.shape[2]
    node = lax.axis_index("z")
    ids = lax.dynamic_index_in_dim(routes[0, :, 0], node, 0, keepdims=False)
    wts = lax.dynamic_index_in_dim(combine[0, :, 0], node, 0, keepdims=False)
    pick_tok, pick_cot, mix_out, cot_weight, slots = slot_plan(ids, wts, experts)
    bf16 = jnp.bfloat16
    weights = jnp.concatenate([w_gate[0], w_up[0], w_down[0].T], axis=1)

    send_tok = jnp.dot(pick_tok.astype(bf16), hidden, preferred_element_type=jnp.float32)
    send_cot = jnp.dot(pick_cot.astype(bf16), grad_out, preferred_element_type=jnp.float32)
    send = (send_tok + send_cot * cot_weight[:, None]).astype(bf16)
    own = send.shape[0]
    got = lax.all_to_all(
        send.reshape(experts, own // experts, width), ("yh", "c"), split_axis=0, concat_axis=0, tiled=True
    ).reshape(own, width)
    rows = lax.all_gather(got, "z", axis=0, tiled=True)

    pre = jnp.dot(rows, weights, preferred_element_type=jnp.float32)
    gate_pre = pre[:, :f_dev]
    up_pre = pre[:, f_dev : 2 * f_dev]
    hidden_grad = jnp.roll(pre[:, 2 * f_dev :], -slots, axis=0)
    is_tok = ((jnp.arange(rows.shape[0]) % (2 * slots)) < slots)[:, None]
    sig = jax.nn.sigmoid(gate_pre)
    hid = gate_pre * sig * up_pre
    dgate = hidden_grad * up_pre * sig * (1.0 + gate_pre * (1.0 - sig))
    dup = hidden_grad * gate_pre * sig
    mids = jnp.concatenate(
        [
            jnp.where(is_tok, dgate, 0.0),
            jnp.where(is_tok, dup, 0.0),
            jnp.where(is_tok, 0.0, jnp.roll(hid, slots, axis=0)),
        ],
        axis=1,
    ).astype(bf16)

    shares = lax.dot_general(
        rows, mids, (((0,), (0,)), ((), ())), preferred_element_type=jnp.float32
    ).astype(bf16)
    parts = lax.dot_general(
        mids, weights, (((1,), (1,)), ((), ())), preferred_element_type=jnp.float32
    ).astype(bf16)
    summed = lax.psum_scatter(parts, "z", scatter_dimension=0, tiled=True)
    grads = lax.psum_scatter(shares, ("yl", "x"), scatter_dimension=0, tiled=True)
    back = lax.all_to_all(
        summed.reshape(experts, own // experts, width), ("yh", "c"), split_axis=0, concat_axis=0, tiled=True
    ).reshape(own, width).astype(jnp.float32)
    high = lax.Precision.HIGHEST
    layer_out = jnp.dot(mix_out.T, back, precision=high).astype(bf16)
    grad_in = jnp.dot(pick_tok.T, back, precision=high).astype(bf16)
    grad_gate = grads[None, :, :f_dev]
    grad_up = grads[None, :, f_dev : 2 * f_dev]
    grad_down = grads[:, 2 * f_dev :].T[None]
    return (layer_out, grad_in, grad_gate, grad_up, grad_down)


def solution(mesh):
    fine = Mesh(mesh.devices.reshape(4, 4, 12, 2, 2), ("yl", "x", "z", "yh", "c"))
    dp, echip = ("yl", "x"), ("yh", "c")
    every = dp + ("z",) + echip
    return jax.shard_map(
        local,
        mesh=fine,
        in_specs=(
            P(every, None),
            P(every, None),
            P(dp, None, echip, None, None),
            P(dp, None, echip, None, None),
            P(echip, None, "z"),
            P(echip, None, "z"),
            P(echip, "z", None),
        ),
        out_specs=(
            P(every, None),
            P(every, None),
            P(echip, dp, "z"),
            P(echip, dp, "z"),
            P(echip, "z", dp),
        ),
        check_vma=False,
    )
```

time: 574 us -> 296 us (0.52)
  the two profiles are of different devices: /device:TPU:2 before, /device:TPU:64 now
where the time goes in v1:
time: 296 us; the launch traced here: 295 us
  waiting for transfers between devices  206 us (70%)
  blocking collectives  41.1 us (14%)
  matrix products  21.2 us (7%)
  between operations  13.9 us (5%)
  local copies, waits for them, and re-layouts  12.5 us (4%)
    reduce_scatter x1, waiting for transfers between devices, local(): lax.psum_scatter(shares, ('yl', 'x'), scatter_dimension=0, tiled=True)  84.3 us
    all_gather x1, waiting for transfers between devices, local(): rows = lax.all_gather(got, 'z', axis=0, tiled=True)  63.8 us
    reduce_scatter x1, waiting for transfers between devices, local(): summed = lax.psum_scatter(parts, 'z', scatter_dimension=0, tiled=True)  57.4 us
    all_to_all x1, blocking collectives, local(): lax.all_to_all(send.reshape(experts, own // experts, width), ('yh', 'c'),...  20.8 us
    all_to_all x1, blocking collectives, local(): lax.all_to_all(summed.reshape(experts, own // experts, width), ('yh', 'c'...  20.3 us
    dot_general x1, matrix products, local(): lax.dot_general(rows, mids, (((0,), (0,)), ((), ())), preferred_element_t...  8.13 us
  transfers between devices with their start and end apart: 3, of which 3 were waited for; matrix products, arithmetic and copies ran while one was open for 6% of the time, Pallas kernels for 0%

profile of v1, /device:TPU:64, one launch (start us, length us, event | category | flops | bytes accessed | tf_op | source)
XLA Modules:
  0.0 295.1 jit_solution(14618037364466926284)
XLA Ops:
  7.2 0.0 copy-start
  7.2 0.0 copy-start.1
  7.2 0.0 all-gather.2.cloned.1.call-start
  7.2 1.1 fusion.17
  8.3 0.1 eq.53
  8.4 0.2 convert_reduce_fusion
  8.6 0.1 reduce_sum.48
  8.7 0.1 copy.45
  8.8 0.1 copy.38
  8.9 0.1 copy.39
  9.0 0.1 copy.42
  9.1 0.1 fusion.5
  9.2 0.8 fusion.16
  10.0 0.1 mul.74
  10.1 0.1 copy.40
  10.2 0.1 copy.41
  10.3 0.1 select_reduce_fusion
  10.4 0.1 convert_reduce_fusion.1
  10.5 0.0 copy-done
  10.5 0.3 fusion.8
  10.8 1.2 fusion.1
  12.0 0.1 reshape.97
  12.1 20.8 %all_to_all.10 = bf16[4,6,7168]{2,1,0:T(8,128)(2,1)S(1)} all-to-all(bf16[4,6,7168]{2,1,0:T(8,128)(2,1)S(1)} %reshape.97), channel_id=1, replica_groups=mesh['yl'=4,'x'=4,'z'=12,'yh'=2,'c'=2] {'yh','c'}, dimensions={0} | all-to-all | bytes 688128 | tf_op jit(solution)/shard_map/all_to_all | solution.py:42
  32.9 0.9 reshape.98
  33.8 0.0 all-gather.2.cloned.1.call-update
  33.8 0.0 reduce-scatter.3.cloned.1.call-start
  33.8 0.0 copy-done.1
  33.9 3.0 %copy.43 = bf16[1,7168,128]{1,2,0:T(8,128)(2,1)} copy(bf16[1,7168,128]{2,1,0:T(8,128)(2,1)S(1)} %copy-done.1) | data formatting | bytes 3670016 | tf_op args[4]
  36.8 2.8 copy.44
  39.6 63.8 %all-gather.2.cloned.1.call-done = bf16[288,7168]{1,0:T(8,128)(2,1)} async-done(((bf16[24,7168]{1,0:T(8,128)(2,1)}), bf16[288,7168]{1,0:T(8,128)(2,1)}) %all-gather.2.cloned.1.call-update) | async-done | bytes 4128784 | tf_op jit(solution)/shard_map/all_gather | solution.py:45
  103.5 5.7 %fusion.2 = f32[288,384]{1,0:T(8,128)S(1)} fusion(bf16[288,7168]{1,0:T(8,128)(2,1)} %all-gather.2.cloned.1.call-done, bf16[7168,128]{0,1:T(8,128)(2,1)} %bitcast.33, bf16[7168,128]{0,1:T(8,128)(2,1)S(1)} %bitcast.29, bf16[7168,128]{0,1:T(8,128)(2,1)} %bitcast.27), kind=kOutput, calls=%fused_computation.8 | convolution fusion | flops 1601961984 | bytes 10076160 | tf_op jit(solution)/shard_map/dot_general | solution.py:47
  109.2 0.1 multiply_multiply_fusion
  109.3 0.1 fusion.3
  109.4 0.1 select_convert_fusion.1
  109.5 0.0 copy-done.2
  109.6 3.9 %convolution_convert_fusion.1 = bf16[288,7168]{1,0:T(8,128)(2,1)} fusion(bf16[7168,128]{0,1:T(8,128)(2,1)S(1)} %bitcast.34, bf16[7168,128]{0,1:T(8,128)(2,1)S(1)} %bitcast.30, bf16[7168,128]{0,1:T(8,128)(2,1)S(1)} %bitcast.28, bf16[288,128]{1,0:T(8,128)(2,1)S(1)} %fusion.3, bf16[288,128]{1,0:T(8,128)(2,1)S(1)} %get-tuple-element.14, ...), kind=kOutput, calls=%fused_computation.1 | convolution fusion | flops 1604689920 | bytes 9854976 | tf_op jit(solution)/shard_map/dot_general | solution.py:68
  113.5 0.0 reduce-scatter.3.cloned.1.call-update
  113.5 0.0 reduce-scatter.5.cloned.1.call-start
  113.6 8.1 %convolution_convert_fusion = bf16[7168,384]{1,0:T(8,128)(2,1)} fusion(bf16[288,7168]{1,0:T(8,128)(2,1)} %all-gather.2.cloned.1.call-done, bf16[288,128]{1,0:T(8,128)(2,1)S(1)} %fusion.3, bf16[288,128]{1,0:T(8,128)(2,1)S(1)} %get-tuple-element.14, bf16[288,128]{1,0:T(8,128)(2,1)S(1)} %get-tuple-element.13), kind=kOutput, calls=%fused_computation | convolution fusion | flops 1588862976 | bytes 9854976 | tf_op jit(solution)/shard_map/dot_general | solution.py:65
  121.7 0.0 reduce-scatter.5.cloned.1.call-update
  121.7 57.4 %reduce-scatter.3.cloned.1.call-done = bf16[24,7168]{1,0:T(8,128)(2,1)} async-done(((bf16[288,7168]{1,0:T(8,128)(2,1)}), bf16[24,7168]{1,0:T(8,128)(2,1)}) %reduce-scatter.3.cloned.1.call-update) | async-done | bytes 344080 | tf_op jit(solution)/shard_map/reduce_scatter | solution.py:71
  179.1 1.1 reshape.99
  180.2 20.3 %all_to_all.11 = bf16[4,6,7168]{2,1,0:T(8,128)(2,1)S(1)} all-to-all(bf16[4,6,7168]{2,1,0:T(8,128)(2,1)S(1)} %reshape.99), channel_id=1, replica_groups=mesh['yl'=4,'x'=4,'z'=12,'yh'=2,'c'=2] {'yh','c'}, dimensions={0} | all-to-all | bytes 688128 | tf_op jit(solution)/shard_map/all_to_all | solution.py:73
  200.6 0.1 reshape.100
  200.7 0.9 convolution_convert_fusion.2
  201.6 0.9 convolution_convert_fusion.3
  202.6 84.3 %reduce-scatter.5.cloned.1.call-done = bf16[448,384]{1,0:T(8,128)(2,1)} async-done(((bf16[7168,384]{1,0:T(8,128)(2,1)}), bf16[448,384]{1,0:T(8,128)(2,1)}) %reduce-scatter.5.cloned.1.call-update) | async-done | bytes 344080 | tf_op jit(solution)/shard_map/reduce_scatter | solution.py:72
  286.8 1.7 slice_bitcast_fusion
  (9 shorter events, 0.1 us)
Async XLA Ops:
  7.2 3.3 %copy-start = (bf16[6,7168]{1,0:T(8,128)(2,1)S(1)}, bf16[6,7168]{1,0:T(8,128)(2,1)}, u32[]{:S(2)}) copy-start(bf16[6,7168]{1,0:T(8,128)(2,1)} %param.7) | copy-start | bytes 258052
  7.2 26.7 %copy-start.1 = (bf16[1,7168,128]{2,1,0:T(8,128)(2,1)S(1)}, bf16[1,7168,128]{2,1,0:T(8,128)(2,1)}, u32[]{:S(2)}) copy-start(bf16[1,7168,128]{2,1,0:T(8,128)(2,1)} %param.11) | copy-start | bytes 5505028
  7.2 96.3 %all-gather.2.cloned.1.call-start = ((), (), s32[]{:S(2)}) async-start(), calls=%async_computation.4 | async-start | bytes 4472832 | tf_op jit(solution)/shard_map/all_gather | solution.py:45
  33.8 145.3 %reduce-scatter.3.cloned.1.call-start = ((), (), s32[]{:S(2)}) async-start(), calls=%async_computation.5 | async-start | bytes 4472832 | tf_op jit(solution)/shard_map/reduce_scatter | solution.py:71
  103.5 6.1 %copy-start.2 = (bf16[1,7168,128]{1,2,0:T(8,128)(2,1)S(1)}, bf16[1,7168,128]{1,2,0:T(8,128)(2,1)}, u32[]{:S(2)}) copy-start(bf16[1,7168,128]{1,2,0:T(8,128)(2,1)} %copy.43) | copy-start | bytes 5505028
  103.5 6.1 %copy-start.3 = (bf16[1,128,7168]{2,1,0:T(8,128)(2,1)S(1)}, bf16[1,128,7168]{2,1,0:T(8,128)(2,1)}, u32[]{:S(2)}) copy-start(bf16[1,128,7168]{2,1,0:T(8,128)(2,1)} %param.13) | copy-start | bytes 5505028
  113.5 173.3 %reduce-scatter.5.cloned.1.call-start = ((), (), s32[]{:S(2)}) async-start(), calls=%async_computation.6 | async-start | bytes 5849088 | tf_op jit(solution)/shard_map/reduce_scatter | solution.py:72
Sparse Core Ops, SparseCore 0:
  33.9 69.4 all-gather.1
  113.6 65.4 reduce-scatter.2
  182.3 104.5 reduce-scatter.4

commit v2 on v1

--- a/solution.py
+++ b/solution.py
@@ -22,6 +22,45 @@
     mix_out = jnp.sum((hit_cot * wts).reshape(-1, token_count, topk_count), axis=2)
     cot_weight = jnp.sum(hit_cot * wts, axis=1)
     return pick_tok, pick_cot, mix_out, cot_weight, slots
+
+
+def shift(value, axis, step):
+    size = lax.axis_size(axis)
+    return lax.ppermute(value, axis, [(i, (i + step) % size) for i in range(size)])
+
+
+def total(*terms):
+    return sum(term.astype(jnp.float32) for term in terms).astype(jnp.bfloat16)
+
+
+def scatter_shares(shares, pieces):
+    nx, ny = lax.axis_size("x"), lax.axis_size("yl")
+    px, py = lax.axis_index("x"), lax.axis_index("yl")
+    grid = shares.reshape(ny, nx, shares.shape[0] // (nx * ny), shares.shape[1])
+    rows = grid.shape[2] // pieces
+    low, high = slice(0, ny // 2), slice(ny // 2, ny)
+    done = []
+    for piece in range(pieces):
+        part = grid[:, :, piece * rows : (piece + 1) * rows]
+
+        def chunk(step, half):
+            return lax.dynamic_index_in_dim(part[half], (px + step) % nx, 1, keepdims=False)
+
+        far_low = shift(chunk(2, low), "x", 1)
+        far_high = shift(chunk(2, high), "x", -1)
+        near_high = shift(chunk(1, high), "x", 1)
+        near_low = shift(chunk(-1, low), "x", -1)
+        rest_low = shift(total(chunk(1, low), far_low), "x", 1)
+        rest_high = shift(total(chunk(-1, high), far_high), "x", -1)
+        mine = jnp.concatenate(
+            [total(chunk(0, low), near_low, rest_low), total(chunk(0, high), near_high, rest_high)], axis=0
+        )
+
+        def target(step):
+            return lax.dynamic_index_in_dim(mine, (py + step) % ny, 0, keepdims=False)
+
+        done.append(total(target(0), *[shift(target(step), "yl", step) for step in range(1, ny)]))
+    return jnp.concatenate(done, axis=0)
 
 
 def local(hidden, grad_out, routes, combine, w_gate, w_up, w_down):
@@ -69,7 +108,7 @@
         mids, weights, (((1,), (1,)), ((), ())), preferred_element_type=jnp.float32
     ).astype(bf16)
     summed = lax.psum_scatter(parts, "z", scatter_dimension=0, tiled=True)
-    grads = lax.psum_scatter(shares, ("yl", "x"), scatter_dimension=0, tiled=True)
+    grads = scatter_shares(shares, 2)
     back = lax.all_to_all(
         summed.reshape(experts, own // experts, width), ("yh", "c"), split_axis=0, concat_axis=0, tiled=True
     ).reshape(own, width).astype(jnp.float32)

time: 296 us -> 225 us (0.76)
  the two profiles are of different devices: /device:TPU:64 before, /device:TPU:8 now
where the time goes in v2:
time: 225 us; the launch traced here: 224 us
  waiting for transfers between devices  82.9 us (37%)
  starting transfers between devices  66.5 us (30%)
  blocking collectives  22.9 us (10%)
  matrix products  18.9 us (8%)
  between operations  14.7 us (7%)
  local copies, waits for them, and re-layouts  13.9 us (6%)
  other arithmetic  3.94 us (2%)
    all_gather x1, waiting for transfers between devices, local(): rows = lax.all_gather(got, 'z', axis=0, tiled=True)  62.1 us
    ppermute x18, starting transfers between devices, shift(): lax.ppermute(value, axis, [(i, (i + step) % size) for i in range(size)])  61.2 us
    all_to_all x1, blocking collectives, local(): lax.all_to_all(send.reshape(experts, own // experts, width), ('yh', 'c'),...  22.9 us
    ppermute x18, waiting for transfers between devices, shift(): lax.ppermute(value, axis, [(i, (i + step) % size) for i in range(size)])  12.8 us
    all_to_all x1, waiting for transfers between devices, local(): lax.all_to_all(summed.reshape(experts, own // experts, width), ('yh', 'c'...  7.94 us
    unnamed x13, local copies, waits for them, and re-layouts  7.09 us
    dot_general x1, matrix products, local(): lax.dot_general(rows, mids, (((0,), (0,)), ((), ())), preferred_element_t...  5.74 us
    dot_general x1, matrix products, local(): pre = jnp.dot(rows, weights, preferred_element_type=jnp.float32)  5.73 us
  transfers between devices with their start and end apart: 21, of which 6 were waited for; matrix products, arithmetic and copies ran while one was open for 8% of the time, Pallas kernels for 0%

profile of v2, /device:TPU:8, one launch (start us, length us, event | category | flops | bytes accessed | tf_op | source)
XLA Modules:
  0.0 223.6 jit_solution(13615890083432252139)
XLA Ops:
  7.2 0.9 fusion.56
  8.3 0.2 convert_reduce_fusion
  8.8 0.9 fusion.55
  10.3 0.3 fusion.47
  10.7 1.3 fusion.1
  12.1 22.9 %all_to_all.10 = bf16[4,6,7168]{2,1,0:T(8,128)(2,1)S(1)} all-to-all(bf16[4,6,7168]{2,1,0:T(8,128)(2,1)S(1)} %reshape.120), channel_id=1, replica_groups=mesh['yl'=4,'x'=4,'z'=12,'yh'=2,'c'=2] {'yh','c'}, dimensions={0} | all-to-all | bytes 688128 | tf_op jit(solution)/shard_map/all_to_all | solution.py:81
  35.0 0.9 reshape.121
  36.0 2.9 %copy.56 = bf16[1,7168,128]{1,2,0:T(8,128)(2,1)} copy(bf16[1,7168,128]{2,1,0:T(8,128)(2,1)S(1)} %copy-done.1) | data formatting | bytes 3670016 | tf_op args[5]
  39.0 4.0 %copy.55 = bf16[1,7168,128]{1,2,0:T(8,128)(2,1)} copy(bf16[1,7168,128]{2,1,0:T(8,128)(2,1)} %param.11) | data formatting | bytes 3670016 | tf_op args[4]
  43.0 62.1 %all-gather.2.cloned.1.call-done = bf16[288,7168]{1,0:T(8,128)(2,1)} async-done(((bf16[24,7168]{1,0:T(8,128)(2,1)}), bf16[288,7168]{1,0:T(8,128)(2,1)}) %all-gather.2.cloned.1.call-update) | async-done | bytes 4128784 | tf_op jit(solution)/shard_map/all_gather | solution.py:84
  105.2 5.7 %fusion.2 = f32[288,384]{1,0:T(8,128)S(1)} fusion(bf16[288,7168]{1,0:T(8,128)(2,1)} %all-gather.2.cloned.1.call-done, bf16[7168,128]{0,1:T(8,128)(2,1)} %bitcast.129, bf16[7168,128]{0,1:T(8,128)(2,1)S(1)} %bitcast.123, bf16[7168,128]{0,1:T(8,128)(2,1)} %bitcast.125), kind=kOutput, calls=%fused_computation.8 | convolution fusion | flops 1601961984 | bytes 10076160 | tf_op jit(solution)/shard_map/dot_general | solution.py:86
  111.2 3.9 %convolution_convert_fusion.1 = bf16[288,7168]{1,0:T(8,128)(2,1)} fusion(bf16[7168,128]{0,1:T(8,128)(2,1)S(1)} %bitcast.130, bf16[7168,128]{0,1:T(8,128)(2,1)S(1)} %bitcast.124, bf16[7168,128]{0,1:T(8,128)(2,1)S(1)} %bitcast.126, bf16[288,128]{1,0:T(8,128)(2,1)S(1)} %fusion.37, bf16[288,128]{1,0:T(8,128)(2,1)S(1)} %get-tuple-element.32, ...), kind=kOutput, calls=%fused_computation.1 | convolution fusion | flops 1604689920 | bytes 9854976 | tf_op jit(solution)/shard_map/dot_general | solution.py:107
  115.3 5.7 %convolution_convert_fusion = bf16[7168,384]{1,0:T(8,128)(2,1)S(1)} fusion(bf16[288,7168]{1,0:T(8,128)(2,1)} %all-gather.2.cloned.1.call-done, bf16[288,128]{1,0:T(8,128)(2,1)S(1)} %fusion.37, bf16[288,128]{1,0:T(8,128)(2,1)S(1)} %get-tuple-element.32, bf16[288,128]{1,0:T(8,128)(2,1)S(1)} %get-tuple-element.31), kind=kOutput, calls=%fused_computation | convolution fusion | flops 1588862976 | bytes 9854976 | tf_op jit(solution)/shard_map/dot_general | solution.py:104
  121.0 0.8 fusion.57
  121.9 3.4 %collective-permute-start.10 = (bf16[2,224,384]{2,1,0:T(8,128)(2,1)S(1)}, bf16[2,224,384]{2,1,0:T(8,128)(2,1)S(1)}, u32[]{:S(2)}, u32[]{:S(2)}) collective-permute-start(bf16[2,224,384]{2,1,0:T(8,128)(2,1)S(1)} %get-tuple-element.20), channel_id=1, source_target_pairs={{0,48},{48,96},{96,144},{144,0},{1,49},{49,97},{97,145},{145,1},{2... | collective-permute-start | bytes 1032200 | tf_op jit(solution)/shard_map/ppermute | solution.py:29
  125.3 3.7 %collective-permute-start.9 = (bf16[2,224,384]{2,1,0:T(8,128)(2,1)S(1)}, bf16[2,224,384]{2,1,0:T(8,128)(2,1)S(1)}, u32[]{:S(2)}, u32[]{:S(2)}) collective-permute-start(bf16[2,224,384]{2,1,0:T(8,128)(2,1)S(1)} %get-tuple-element.19), channel_id=1, source_target_pairs={{0,144},{48,0},{96,48},{144,96},{1,145},{49,1},{97,49},{145,97},{2... | collective-permute-start | bytes 1032200 | tf_op jit(solution)/shard_map/ppermute | solution.py:29
  129.1 3.4 %collective-permute-start.13 = (bf16[2,224,384]{2,1,0:T(8,128)(2,1)S(1)}, bf16[2,224,384]{2,1,0:T(8,128)(2,1)S(1)}, u32[]{:S(2)}, u32[]{:S(2)}) collective-permute-start(bf16[2,224,384]{2,1,0:T(8,128)(2,1)S(1)} %get-tuple-element.18), channel_id=1, source_target_pairs={{0,144},{48,0},{96,48},{144,96},{1,145},{49,1},{97,49},{145,97},{2... | collective-permute-start | bytes 1032200 | tf_op jit(solution)/shard_map/ppermute | solution.py:29
  132.5 2.5 %collective-permute-start.12 = (bf16[2,224,384]{2,1,0:T(8,128)(2,1)S(1)}, bf16[2,224,384]{2,1,0:T(8,128)(2,1)S(1)}, u32[]{:S(2)}, u32[]{:S(2)}) collective-permute-start(bf16[2,224,384]{2,1,0:T(8,128)(2,1)S(1)} %get-tuple-element.17), channel_id=1, source_target_pairs={{0,48},{48,96},{96,144},{144,0},{1,49},{49,97},{97,145},{145,1},{2... | collective-permute-start | bytes 1032200 | tf_op jit(solution)/shard_map/ppermute | solution.py:29
  135.1 2.2 collective-permute-start.1
  137.4 4.9 %collective-permute-start = (bf16[2,224,384]{2,1,0:T(8,128)(2,1)S(1)}, bf16[2,224,384]{2,1,0:T(8,128)(2,1)S(1)}, u32[]{:S(2)}, u32[]{:S(2)}) collective-permute-start(bf16[2,224,384]{2,1,0:T(8,128)(2,1)S(1)} %get-tuple-element.23), channel_id=1, source_target_pairs={{0,144},{48,0},{96,48},{144,96},{1,145},{49,1},{97,49},{145,97},{2... | collective-permute-start | bytes 1032200 | tf_op jit(solution)/shard_map/ppermute | solution.py:29
  142.4 1.1 collective-permute-done.13
  143.5 3.7 %collective-permute-start.4 = (bf16[2,224,384]{2,1,0:T(8,128)(2,1)S(1)}, bf16[2,224,384]{2,1,0:T(8,128)(2,1)S(1)}, u32[]{:S(2)}, u32[]{:S(2)}) collective-permute-start(bf16[2,224,384]{2,1,0:T(8,128)(2,1)S(1)} %get-tuple-element.22), channel_id=1, source_target_pairs={{0,144},{48,0},{96,48},{144,96},{1,145},{49,1},{97,49},{145,97},{2... | collective-permute-start | bytes 1032200 | tf_op jit(solution)/shard_map/ppermute | solution.py:29
  147.3 0.7 collective-permute-done.1
  148.0 2.2 collective-permute-start.11
  150.3 4.1 %collective-permute-done.4 = bf16[2,224,384]{2,1,0:T(8,128)(2,1)S(1)} collective-permute-done((bf16[2,224,384]{2,1,0:T(8,128)(2,1)S(1)}, bf16[2,224,384]{2,1,0:T(8,128)(2,1)S(1)}, u32[]{:S(2)}, u32[]{:S(2)}) %collective-permute-start.4) | collective-permute-done | bytes 344096 | tf_op jit(solution)/shard_map/ppermute | solution.py:29
  154.5 4.9 %collective-permute-start.14 = (bf16[2,224,384]{2,1,0:T(8,128)(2,1)S(1)}, bf16[2,224,384]{2,1,0:T(8,128)(2,1)S(1)}, u32[]{:S(2)}, u32[]{:S(2)}) collective-permute-start(bf16[2,224,384]{2,1,0:T(8,128)(2,1)S(1)} %fusion.3), channel_id=1, source_target_pairs={{0,144},{48,0},{96,48},{144,96},{1,145},{49,1},{97,49},{145,97},{2... | collective-permute-start | bytes 1032200 | tf_op jit(solution)/shard_map/ppermute | solution.py:29
  159.5 1.9 collective-permute-start.3
  161.4 2.4 %collective-permute-start.2 = (bf16[2,224,384]{2,1,0:T(8,128)(2,1)S(1)}, bf16[2,224,384]{2,1,0:T(8,128)(2,1)S(1)}, u32[]{:S(2)}, u32[]{:S(2)}) collective-permute-start(bf16[2,224,384]{2,1,0:T(8,128)(2,1)S(1)} %fusion.12), channel_id=1, source_target_pairs={{0,48},{48,96},{96,144},{144,0},{1,49},{49,97},{97,145},{145,1},{2... | collective-permute-start | bytes 1032200 | tf_op jit(solution)/shard_map/ppermute | solution.py:29
  163.8 0.1 fusion.8
  164.0 4.6 %collective-permute-start.5 = (bf16[2,224,384]{2,1,0:T(8,128)(2,1)S(1)}, bf16[2,224,384]{2,1,0:T(8,128)(2,1)S(1)}, u32[]{:S(2)}, u32[]{:S(2)}) collective-permute-start(bf16[2,224,384]{2,1,0:T(8,128)(2,1)S(1)} %fusion.9), channel_id=1, source_target_pairs={{0,144},{48,0},{96,48},{144,96},{1,145},{49,1},{97,49},{145,97},{2... | collective-permute-start | bytes 1032200 | tf_op jit(solution)/shard_map/ppermute | solution.py:29
  168.6 0.1 fusion.5
  168.8 0.2 fusion.26
  169.0 2.4 %collective-permute-start.17 = (bf16[224,384]{1,0:T(8,128)(2,1)S(1)}, bf16[224,384]{1,0:T(8,128)(2,1)S(1)}, u32[]{:S(2)}, u32[]{:S(2)}) collective-permute-start(bf16[224,384]{1,0:T(8,128)(2,1)S(1)} %get-tuple-element.27), channel_id=1, source_target_pairs={{0,576},{192,0},{384,192},{576,384},{1,577},{193,1},{385,193},{577... | collective-permute-start | bytes 516104 | tf_op jit(solution)/shard_map/ppermute | solution.py:29
  171.5 4.3 %collective-permute-start.16 = (bf16[224,384]{1,0:T(8,128)(2,1)S(1)}, bf16[224,384]{1,0:T(8,128)(2,1)S(1)}, u32[]{:S(2)}, u32[]{:S(2)}) collective-permute-start(bf16[224,384]{1,0:T(8,128)(2,1)S(1)} %get-tuple-element.26), channel_id=1, source_target_pairs={{0,384},{192,576},{384,0},{576,192},{1,385},{193,577},{385,1},{577... | collective-permute-start | bytes 516104 | tf_op jit(solution)/shard_map/ppermute | solution.py:29
  175.8 4.3 %collective-permute-start.15 = (bf16[224,384]{1,0:T(8,128)(2,1)S(1)}, bf16[224,384]{1,0:T(8,128)(2,1)S(1)}, u32[]{:S(2)}, u32[]{:S(2)}) collective-permute-start(bf16[224,384]{1,0:T(8,128)(2,1)S(1)} %get-tuple-element.25), channel_id=1, source_target_pairs={{0,192},{192,384},{384,576},{576,0},{1,193},{193,385},{385,577},{5... | collective-permute-start | bytes 516104 | tf_op jit(solution)/shard_map/ppermute | solution.py:29
  180.4 1.0 fusion.34
  181.4 1.9 collective-permute-start.8
  183.3 3.6 %collective-permute-start.7 = (bf16[224,384]{1,0:T(8,128)(2,1)}, bf16[224,384]{1,0:T(8,128)(2,1)S(1)}, u32[]{:S(2)}, u32[]{:S(2)}) collective-permute-start(bf16[224,384]{1,0:T(8,128)(2,1)} %get-tuple-element.29), channel_id=1, source_target_pairs={{0,384},{192,576},{384,0},{576,192},{1,385},{193,577},{385,1},{577... | collective-permute-start | bytes 516104 | tf_op jit(solution)/shard_map/ppermute | solution.py:29
  187.0 1.9 reshape.122
  188.9 5.2 %all-to-all-start.1 = ((bf16[4,6,7168]{2,1,0:T(8,128)(2,1)}), bf16[4,6,7168]{2,1,0:T(8,128)(2,1)S(1)}, u32[]{:S(2)}, u32[]{:S(2)}) async-start(bf16[4,6,7168]{2,1,0:T(8,128)(2,1)} %reshape.122), calls=%async_computation.2 | async-start | bytes 917504 | tf_op jit(solution)/shard_map/all_to_all | solution.py:112
  194.1 4.8 %collective-permute-start.6 = (bf16[224,384]{1,0:T(8,128)(2,1)S(1)}, bf16[224,384]{1,0:T(8,128)(2,1)S(1)}, u32[]{:S(2)}, u32[]{:S(2)}) collective-permute-start(bf16[224,384]{1,0:T(8,128)(2,1)S(1)} %get-tuple-element.28), channel_id=1, source_target_pairs={{0,192},{192,384},{384,576},{576,0},{1,193},{193,385},{385,577},{5... | collective-permute-start | bytes 516104 | tf_op jit(solution)/shard_map/ppermute | solution.py:29
  199.0 0.2 fusion.17
  199.1 6.8 %collective-permute-done.6 = bf16[224,384]{1,0:T(8,128)(2,1)S(1)} collective-permute-done((bf16[224,384]{1,0:T(8,128)(2,1)S(1)}, bf16[224,384]{1,0:T(8,128)(2,1)S(1)}, u32[]{:S(2)}, u32[]{:S(2)}) %collective-permute-start.6) | collective-permute-done | bytes 172064 | tf_op jit(solution)/shard_map/ppermute | solution.py:29
  205.9 0.1 fusion.20
  206.1 0.7 fusion.42
  206.8 7.9 %all-to-all-done.1 = bf16[4,6,7168]{2,1,0:T(8,128)(2,1)S(1)} async-done(((bf16[4,6,7168]{2,1,0:T(8,128)(2,1)}), bf16[4,6,7168]{2,1,0:T(8,128)(2,1)S(1)}, u32[]{:S(2)}, u32[]{:S(2)}) %all-to-all-start.1) | async-done | bytes 344096 | tf_op jit(solution)/shard_map/all_to_all | solution.py:112
  214.9 0.9 convolution_convert_fusion.2
  215.8 0.9 convolution_convert_fusion.3
  (62 shorter events, 2.9 us)
Async XLA Ops:
  7.2 3.1 %copy-start = (bf16[6,7168]{1,0:T(8,128)(2,1)S(1)}, bf16[6,7168]{1,0:T(8,128)(2,1)}, u32[]{:S(2)}) copy-start(bf16[6,7168]{1,0:T(8,128)(2,1)} %param.7) | copy-start | bytes 258052
  7.2 98.0 %all-gather.2.cloned.1.call-start = ((), (), s32[]{:S(2)}) async-start(), calls=%async_computation.3 | async-start | bytes 4472832 | tf_op jit(solution)/shard_map/all_gather | solution.py:84
  10.6 25.4 %copy-start.1 = (bf16[1,7168,128]{2,1,0:T(8,128)(2,1)S(1)}, bf16[1,7168,128]{2,1,0:T(8,128)(2,1)}, u32[]{:S(2)}) copy-start(bf16[1,7168,128]{2,1,0:T(8,128)(2,1)} %param.12) | copy-start | bytes 5505028
  36.0 151.0 %reduce-scatter.2.cloned.1.call-start = ((), (), s32[]{:S(2)}) async-start(), calls=%async_computation.4 | async-start | bytes 4472832 | tf_op jit(solution)/shard_map/reduce_scatter | solution.py:110
  39.0 66.2 %copy-start.2 = (bf16[1,7168,128]{1,2,0:T(8,128)(2,1)S(1)}, bf16[1,7168,128]{1,2,0:T(8,128)(2,1)}, u32[]{:S(2)}) copy-start(bf16[1,7168,128]{1,2,0:T(8,128)(2,1)} %copy.56) | copy-start | bytes 5505028
  105.2 6.1 %copy-start.3 = (bf16[1,7168,128]{1,2,0:T(8,128)(2,1)S(1)}, bf16[1,7168,128]{1,2,0:T(8,128)(2,1)}, u32[]{:S(2)}) copy-start(bf16[1,7168,128]{1,2,0:T(8,128)(2,1)} %copy.55) | copy-start | bytes 5505028
  105.2 6.1 %copy-start.4 = (bf16[1,128,7168]{2,1,0:T(8,128)(2,1)S(1)}, bf16[1,128,7168]{2,1,0:T(8,128)(2,1)}, u32[]{:S(2)}) copy-start(bf16[1,128,7168]{2,1,0:T(8,128)(2,1)} %param.13) | copy-start | bytes 5505028
  121.9 15.4 %collective-permute-start.10 = (bf16[2,224,384]{2,1,0:T(8,128)(2,1)S(1)}, bf16[2,224,384]{2,1,0:T(8,128)(2,1)S(1)}, u32[]{:S(2)}, u32[]{:S(2)}) collective-permute-start(bf16[2,224,384]{2,1,0:T(8,128)(2,1)S(1)} %get-tuple-element.20), channel_id=1, source_target_pairs={{0,48},{48,96},{96,144},{144,0},{1,49},{49,97},{97,145},{145,1},{2... | collective-permute-start | bytes 1032200 | tf_op jit(solution)/shard_map/ppermute | solution.py:29
  125.3 34.2 %collective-permute-start.9 = (bf16[2,224,384]{2,1,0:T(8,128)(2,1)S(1)}, bf16[2,224,384]{2,1,0:T(8,128)(2,1)S(1)}, u32[]{:S(2)}, u32[]{:S(2)}) collective-permute-start(bf16[2,224,384]{2,1,0:T(8,128)(2,1)S(1)} %get-tuple-element.19), channel_id=1, source_target_pairs={{0,144},{48,0},{96,48},{144,96},{1,145},{49,1},{97,49},{145,97},{2... | collective-permute-start | bytes 1032200 | tf_op jit(solution)/shard_map/ppermute | solution.py:29
  129.1 14.4 %collective-permute-start.13 = (bf16[2,224,384]{2,1,0:T(8,128)(2,1)S(1)}, bf16[2,224,384]{2,1,0:T(8,128)(2,1)S(1)}, u32[]{:S(2)}, u32[]{:S(2)}) collective-permute-start(bf16[2,224,384]{2,1,0:T(8,128)(2,1)S(1)} %get-tuple-element.18), channel_id=1, source_target_pairs={{0,144},{48,0},{96,48},{144,96},{1,145},{49,1},{97,49},{145,97},{2... | collective-permute-start | bytes 1032200 | tf_op jit(solution)/shard_map/ppermute | solution.py:29
  132.5 31.5 %collective-permute-start.12 = (bf16[2,224,384]{2,1,0:T(8,128)(2,1)S(1)}, bf16[2,224,384]{2,1,0:T(8,128)(2,1)S(1)}, u32[]{:S(2)}, u32[]{:S(2)}) collective-permute-start(bf16[2,224,384]{2,1,0:T(8,128)(2,1)S(1)} %get-tuple-element.17), channel_id=1, source_target_pairs={{0,48},{48,96},{96,144},{144,0},{1,49},{49,97},{97,145},{145,1},{2... | collective-permute-start | bytes 1032200 | tf_op jit(solution)/shard_map/ppermute | solution.py:29
  135.1 12.9 %collective-permute-start.1 = (bf16[2,224,384]{2,1,0:T(8,128)(2,1)S(1)}, bf16[2,224,384]{2,1,0:T(8,128)(2,1)S(1)}, u32[]{:S(2)}, u32[]{:S(2)}) collective-permute-start(bf16[2,224,384]{2,1,0:T(8,128)(2,1)S(1)} %get-tuple-element.24), channel_id=1, source_target_pairs={{0,48},{48,96},{96,144},{144,0},{1,49},{49,97},{97,145},{145,1},{2... | collective-permute-start | bytes 1032200 | tf_op jit(solution)/shard_map/ppermute | solution.py:29
  137.4 34.1 %collective-permute-start = (bf16[2,224,384]{2,1,0:T(8,128)(2,1)S(1)}, bf16[2,224,384]{2,1,0:T(8,128)(2,1)S(1)}, u32[]{:S(2)}, u32[]{:S(2)}) collective-permute-start(bf16[2,224,384]{2,1,0:T(8,128)(2,1)S(1)} %get-tuple-element.23), channel_id=1, source_target_pairs={{0,144},{48,0},{96,48},{144,96},{1,145},{49,1},{97,49},{145,97},{2... | collective-permute-start | bytes 1032200 | tf_op jit(solution)/shard_map/ppermute | solution.py:29
  143.5 11.0 %collective-permute-start.4 = (bf16[2,224,384]{2,1,0:T(8,128)(2,1)S(1)}, bf16[2,224,384]{2,1,0:T(8,128)(2,1)S(1)}, u32[]{:S(2)}, u32[]{:S(2)}) collective-permute-start(bf16[2,224,384]{2,1,0:T(8,128)(2,1)S(1)} %get-tuple-element.22), channel_id=1, source_target_pairs={{0,144},{48,0},{96,48},{144,96},{1,145},{49,1},{97,49},{145,97},{2... | collective-permute-start | bytes 1032200 | tf_op jit(solution)/shard_map/ppermute | solution.py:29
  148.0 13.4 %collective-permute-start.11 = (bf16[2,224,384]{2,1,0:T(8,128)(2,1)S(1)}, bf16[2,224,384]{2,1,0:T(8,128)(2,1)S(1)}, u32[]{:S(2)}, u32[]{:S(2)}) collective-permute-start(bf16[2,224,384]{2,1,0:T(8,128)(2,1)S(1)} %fusion.6), channel_id=1, source_target_pairs={{0,48},{48,96},{96,144},{144,0},{1,49},{49,97},{97,145},{145,1},{2... | collective-permute-start | bytes 1032200 | tf_op jit(solution)/shard_map/ppermute | solution.py:29
  154.5 14.2 %collective-permute-start.14 = (bf16[2,224,384]{2,1,0:T(8,128)(2,1)S(1)}, bf16[2,224,384]{2,1,0:T(8,128)(2,1)S(1)}, u32[]{:S(2)}, u32[]{:S(2)}) collective-permute-start(bf16[2,224,384]{2,1,0:T(8,128)(2,1)S(1)} %fusion.3), channel_id=1, source_target_pairs={{0,144},{48,0},{96,48},{144,96},{1,145},{49,1},{97,49},{145,97},{2... | collective-permute-start | bytes 1032200 | tf_op jit(solution)/shard_map/ppermute | solution.py:29
  159.5 20.8 %collective-permute-start.3 = (bf16[2,224,384]{2,1,0:T(8,128)(2,1)S(1)}, bf16[2,224,384]{2,1,0:T(8,128)(2,1)S(1)}, u32[]{:S(2)}, u32[]{:S(2)}) collective-permute-start(bf16[2,224,384]{2,1,0:T(8,128)(2,1)S(1)} %get-tuple-element.21), channel_id=1, source_target_pairs={{0,48},{48,96},{96,144},{144,0},{1,49},{49,97},{97,145},{145,1},{2... | collective-permute-start | bytes 1032200 | tf_op jit(solution)/shard_map/ppermute | solution.py:29
  161.4 14.4 %collective-permute-start.2 = (bf16[2,224,384]{2,1,0:T(8,128)(2,1)S(1)}, bf16[2,224,384]{2,1,0:T(8,128)(2,1)S(1)}, u32[]{:S(2)}, u32[]{:S(2)}) collective-permute-start(bf16[2,224,384]{2,1,0:T(8,128)(2,1)S(1)} %fusion.12), channel_id=1, source_target_pairs={{0,48},{48,96},{96,144},{144,0},{1,49},{49,97},{97,145},{145,1},{2... | collective-permute-start | bytes 1032200 | tf_op jit(solution)/shard_map/ppermute | solution.py:29
  164.0 16.3 %collective-permute-start.5 = (bf16[2,224,384]{2,1,0:T(8,128)(2,1)S(1)}, bf16[2,224,384]{2,1,0:T(8,128)(2,1)S(1)}, u32[]{:S(2)}, u32[]{:S(2)}) collective-permute-start(bf16[2,224,384]{2,1,0:T(8,128)(2,1)S(1)} %fusion.9), channel_id=1, source_target_pairs={{0,144},{48,0},{96,48},{144,96},{1,145},{49,1},{97,49},{145,97},{2... | collective-permute-start | bytes 1032200 | tf_op jit(solution)/shard_map/ppermute | solution.py:29
  169.0 25.1 %collective-permute-start.17 = (bf16[224,384]{1,0:T(8,128)(2,1)S(1)}, bf16[224,384]{1,0:T(8,128)(2,1)S(1)}, u32[]{:S(2)}, u32[]{:S(2)}) collective-permute-start(bf16[224,384]{1,0:T(8,128)(2,1)S(1)} %get-tuple-element.27), channel_id=1, source_target_pairs={{0,576},{192,0},{384,192},{576,384},{1,577},{193,1},{385,193},{577... | collective-permute-start | bytes 516104 | tf_op jit(solution)/shard_map/ppermute | solution.py:29
  171.5 27.4 %collective-permute-start.16 = (bf16[224,384]{1,0:T(8,128)(2,1)S(1)}, bf16[224,384]{1,0:T(8,128)(2,1)S(1)}, u32[]{:S(2)}, u32[]{:S(2)}) collective-permute-start(bf16[224,384]{1,0:T(8,128)(2,1)S(1)} %get-tuple-element.26), channel_id=1, source_target_pairs={{0,384},{192,576},{384,0},{576,192},{1,385},{193,577},{385,1},{577... | collective-permute-start | bytes 516104 | tf_op jit(solution)/shard_map/ppermute | solution.py:29
  175.8 23.1 %collective-permute-start.15 = (bf16[224,384]{1,0:T(8,128)(2,1)S(1)}, bf16[224,384]{1,0:T(8,128)(2,1)S(1)}, u32[]{:S(2)}, u32[]{:S(2)}) collective-permute-start(bf16[224,384]{1,0:T(8,128)(2,1)S(1)} %get-tuple-element.25), channel_id=1, source_target_pairs={{0,192},{192,384},{384,576},{576,0},{1,193},{193,385},{385,577},{5... | collective-permute-start | bytes 516104 | tf_op jit(solution)/shard_map/ppermute | solution.py:29
  181.4 17.7 %collective-permute-start.8 = (bf16[224,384]{1,0:T(8,128)(2,1)}, bf16[224,384]{1,0:T(8,128)(2,1)S(1)}, u32[]{:S(2)}, u32[]{:S(2)}) collective-permute-start(bf16[224,384]{1,0:T(8,128)(2,1)} %get-tuple-element.30), channel_id=1, source_target_pairs={{0,576},{192,0},{384,192},{576,384},{1,577},{193,1},{385,193},{577... | collective-permute-start | bytes 516104 | tf_op jit(solution)/shard_map/ppermute | solution.py:29
  183.3 15.8 %collective-permute-start.7 = (bf16[224,384]{1,0:T(8,128)(2,1)}, bf16[224,384]{1,0:T(8,128)(2,1)S(1)}, u32[]{:S(2)}, u32[]{:S(2)}) collective-permute-start(bf16[224,384]{1,0:T(8,128)(2,1)} %get-tuple-element.29), channel_id=1, source_target_pairs={{0,384},{192,576},{384,0},{576,192},{1,385},{193,577},{385,1},{577... | collective-permute-start | bytes 516104 | tf_op jit(solution)/shard_map/ppermute | solution.py:29
  188.9 25.9 %all-to-all-start.1 = ((bf16[4,6,7168]{2,1,0:T(8,128)(2,1)}), bf16[4,6,7168]{2,1,0:T(8,128)(2,1)S(1)}, u32[]{:S(2)}, u32[]{:S(2)}) async-start(bf16[4,6,7168]{2,1,0:T(8,128)(2,1)} %reshape.122), calls=%async_computation.2 | async-start | bytes 917504 | tf_op jit(solution)/shard_map/all_to_all | solution.py:112
  194.1 11.8 %collective-permute-start.6 = (bf16[224,384]{1,0:T(8,128)(2,1)S(1)}, bf16[224,384]{1,0:T(8,128)(2,1)S(1)}, u32[]{:S(2)}, u32[]{:S(2)}) collective-permute-start(bf16[224,384]{1,0:T(8,128)(2,1)S(1)} %get-tuple-element.28), channel_id=1, source_target_pairs={{0,192},{192,384},{384,576},{576,0},{1,193},{193,385},{385,577},{5... | collective-permute-start | bytes 516104 | tf_op jit(solution)/shard_map/ppermute | solution.py:29
Sparse Core Ops, SparseCore 0:
  36.1 69.0 all-gather.1
  115.3 65.8 reduce-scatter.1

commit v3 on v1

--- a/solution.py
+++ b/solution.py
@@ -24,10 +24,81 @@
     return pick_tok, pick_cot, mix_out, cot_weight, slots
 
 
+def shift(value, axis, step):
+    size = lax.axis_size(axis)
+    return lax.ppermute(value, axis, [(i, (i + step) % size) for i in range(size)])
+
+
+def total(*terms):
+    return sum(term.astype(jnp.float32) for term in terms).astype(jnp.bfloat16)
+
+
+def ring_gather(value, axis, ups):
+    size = lax.axis_size(axis)
+    blocks = {0: value}
+    up = down = value
+    for step in range(1, max(ups, size - 1 - ups) + 1):
+        if step <= ups:
+            up = shift(up, axis, 1)
+            blocks[size - step] = up
+        if step <= size - 1 - ups:
+            down = shift(down, axis, -1)
+            blocks[step] = down
+    return jnp.concatenate([blocks[k] for k in range(size)], axis=0)
+
+
+def ring_scatter(value, axis, ups):
+    size = lax.axis_size(axis)
+    rows = value.shape[0] // size
+    blocks = [value[k * rows : (k + 1) * rows] for k in range(size)]
+    downs = size - 1 - ups
+    up, down = blocks[ups], blocks[size - downs]
+    left_up, left_down = ups, downs
+    while left_up or left_down:
+        if left_up >= left_down:
+            up = shift(up, axis, 1)
+            left_up -= 1
+            if left_up:
+                up = total(up, blocks[left_up])
+        else:
+            down = shift(down, axis, -1)
+            left_down -= 1
+            if left_down:
+                down = total(down, blocks[size - left_down])
+    return total(blocks[0], up, down)
+
+
+def scatter_shares(low, high):
+    nx, ny = lax.axis_size("x"), lax.axis_size("yl")
+    px, py = lax.axis_index("x"), lax.axis_index("yl")
+    low = low.reshape(ny // 2, nx, -1, low.shape[1])
+    high = high.reshape(ny // 2, nx, -1, high.shape[1])
+
+    def chunk(step, half):
+        return lax.dynamic_index_in_dim(half, (px + step) % nx, 1, keepdims=False)
+
+    far_low = shift(chunk(2, low), "x", 1)
+    far_high = shift(chunk(2, high), "x", -1)
+    near_high = shift(chunk(1, high), "x", 1)
+    near_low = shift(chunk(-1, low), "x", -1)
+    rest_low = shift(total(chunk(1, low), far_low), "x", 1)
+    rest_high = shift(total(chunk(-1, high), far_high), "x", -1)
+    mine = jnp.concatenate(
+        [total(chunk(0, low), near_low, rest_low), total(chunk(0, high), near_high, rest_high)], axis=0
+    )
+
+    def target(step):
+        return lax.dynamic_index_in_dim(mine, (py + step) % ny, 0, keepdims=False)
+
+    return total(target(0), *[shift(target(step), "yl", step) for step in range(1, ny)])
+
+
 def local(hidden, grad_out, routes, combine, w_gate, w_up, w_down):
     experts = lax.axis_size("yh") * lax.axis_size("c")
     width = hidden.shape[1]
+    half = width // 2
     f_dev = w_gate.shape[2]
+    nodes = lax.axis_size("z")
     node = lax.axis_index("z")
     ids = lax.dynamic_index_in_dim(routes[0, :, 0], node, 0, keepdims=False)
     wts = lax.dynamic_index_in_dim(combine[0, :, 0], node, 0, keepdims=False)
@@ -42,13 +113,16 @@
     got = lax.all_to_all(
         send.reshape(experts, own // experts, width), ("yh", "c"), split_axis=0, concat_axis=0, tiled=True
     ).reshape(own, width)
-    rows = lax.all_gather(got, "z", axis=0, tiled=True)
+    ups = (nodes - 1) // 2
+    rows_low = ring_gather(got[:, :half], "z", ups)
+    rows_high = ring_gather(got[:, half:], "z", nodes - 1 - ups)
 
-    pre = jnp.dot(rows, weights, preferred_element_type=jnp.float32)
+    pre = jnp.dot(rows_low, weights[:half], preferred_element_type=jnp.float32)
+    pre = pre + jnp.dot(rows_high, weights[half:], preferred_element_type=jnp.float32)
     gate_pre = pre[:, :f_dev]
     up_pre = pre[:, f_dev : 2 * f_dev]
     hidden_grad = jnp.roll(pre[:, 2 * f_dev :], -slots, axis=0)
-    is_tok = ((jnp.arange(rows.shape[0]) % (2 * slots)) < slots)[:, None]
+    is_tok = ((jnp.arange(pre.shape[0]) % (2 * slots)) < slots)[:, None]
     sig = jax.nn.sigmoid(gate_pre)
     hid = gate_pre * sig * up_pre
     dgate = hidden_grad * up_pre * sig * (1.0 + gate_pre * (1.0 - sig))
@@ -62,14 +136,24 @@
         axis=1,
     ).astype(bf16)
 
-    shares = lax.dot_general(
-        rows, mids, (((0,), (0,)), ((), ())), preferred_element_type=jnp.float32
-    ).astype(bf16)
-    parts = lax.dot_general(
-        mids, weights, (((1,), (1,)), ((), ())), preferred_element_type=jnp.float32
-    ).astype(bf16)
-    summed = lax.psum_scatter(parts, "z", scatter_dimension=0, tiled=True)
-    grads = lax.psum_scatter(shares, ("yl", "x"), scatter_dimension=0, tiled=True)
+    def parts(block):
+        return lax.dot_general(
+            mids, block, (((1,), (1,)), ((), ())), preferred_element_type=jnp.float32
+        ).astype(bf16)
+
+    def shares(rows):
+        return lax.dot_general(
+            rows, mids, (((0,), (0,)), ((), ())), preferred_element_type=jnp.float32
+        ).astype(bf16)
+
+    summed = jnp.concatenate(
+        [
+            ring_scatter(parts(weights[:half]), "z", ups),
+            ring_scatter(parts(weights[half:]), "z", nodes - 1 - ups),
+        ],
+        axis=1,
+    )
+    grads = scatter_shares(shares(rows_low), shares(rows_high))
     back = lax.all_to_all(
         summed.reshape(experts, own // experts, width), ("yh", "c"), split_axis=0, concat_axis=0, tiled=True
     ).reshape(own, width).astype(jnp.float32)

time: 296 us -> 314 us (1.061)
  the two profiles are of different devices: /device:TPU:64 before, /device:TPU:1 now
where the time goes in v3:
time: 314 us; the launch traced here: 312 us
  starting transfers between devices  212 us (68%)
  waiting for transfers between devices  40.6 us (13%)
  local copies, waits for them, and re-layouts  27.8 us (9%)
  matrix products  15.2 us (5%)
  other arithmetic  14.5 us (5%)
    ppermute x53, starting transfers between devices, shift(): lax.ppermute(value, axis, [(i, (i + step) % size) for i in range(size)])  175 us
    ppermute x53, waiting for transfers between devices, shift(): lax.ppermute(value, axis, [(i, (i + step) % size) for i in range(size)])  36.3 us
    all_to_all x1, starting transfers between devices, local(): lax.all_to_all(summed.reshape(experts, own // experts, width), ('yh', 'c'...  22.8 us
    unnamed x35, local copies, waits for them, and re-layouts  17.8 us
    all_to_all x1, starting transfers between devices, local(): lax.all_to_all(send.reshape(experts, own // experts, width), ('yh', 'c'),...  13.9 us
    convert_element_type x17, other arithmetic, total(): sum((term.astype(jnp.float32) for term in terms)).astype(jnp.bfloat16)  7.64 us
  transfers between devices with their start and end apart: 55, of which 12 were waited for; matrix products, arithmetic and copies ran while one was open for 13% of the time, Pallas kernels for 0%

profile of v3, /device:TPU:1, one launch (start us, length us, event | category | flops | bytes accessed | tf_op | source)
XLA Modules:
  0.0 311.8 jit_solution(3892179663461466066)
XLA Ops:
  6.8 13.9 %all-to-all-start = ((bf16[4,6,7168]{2,1,0:T(8,128)(2,1)}), bf16[4,6,7168]{2,1,0:T(8,128)(2,1)S(1)}, u32[]{:S(2)}, u32[]{:S(2)}) async-start(bf16[4,6,7168]{2,1,0:T(8,128)(2,1)} %reshape.113), calls=%async_computation | async-start | bytes 917504 | tf_op jit(solution)/shard_map/all_to_all | solution.py:113
  20.7 2.8 copy.56
  23.5 3.9 %copy.55 = bf16[1,7168,128]{1,2,0:T(8,128)(2,1)} copy(bf16[1,7168,128]{2,1,0:T(8,128)(2,1)} %param.11) | data formatting | bytes 3670016 | tf_op args[4]
  27.4 4.3 %all-to-all-done = bf16[4,6,7168]{2,1,0:T(8,128)(2,1)S(1)} async-done(((bf16[4,6,7168]{2,1,0:T(8,128)(2,1)}), bf16[4,6,7168]{2,1,0:T(8,128)(2,1)S(1)}, u32[]{:S(2)}, u32[]{:S(2)}) %all-to-all-start) | async-done | bytes 344096 | tf_op jit(solution)/shard_map/all_to_all | solution.py:113
  32.7 10.7 %collective-permute-start.11 = (bf16[24,3584]{1,0:T(8,128)(2,1)S(1)}, bf16[24,3584]{1,0:T(8,128)(2,1)S(1)}, u32[]{:S(2)}, u32[]{:S(2)}) collective-permute-start(bf16[24,3584]{1,0:T(8,128)(2,1)S(1)} %get-tuple-element.48), channel_id=1, source_target_pairs={{0,44},{4,0},{8,4},{12,8},{16,12},{20,16},{24,20},{28,24},{32,28},... | collective-permute-start | bytes 516104 | tf_op jit(solution)/shard_map/ppermute | solution.py:29
  43.4 5.0 %pad_maximum_fusion = bf16[7168,384]{0,1:T(8,128)(2,1)} fusion(bf16[7168,128]{0,1:T(8,128)(2,1)} %bitcast.78, bf16[7168,128]{0,1:T(8,128)(2,1)S(1)} %bitcast.70, bf16[7168,128]{0,1:T(8,128)(2,1)} %bitcast.71), kind=kLoop, calls=%fused_computation.7 | loop fusion | flops 16515072 | bytes 11010048 | tf_op jit(solution)/shard_map/concatenate | solution.py:107
  50.4 4.6 %collective-permute-start = (bf16[24,3584]{1,0:T(8,128)(2,1)S(1)}, bf16[24,3584]{1,0:T(8,128)(2,1)S(1)}, u32[]{:S(2)}, u32[]{:S(2)}) collective-permute-start(bf16[24,3584]{1,0:T(8,128)(2,1)S(1)} %get-tuple-element.45), channel_id=1, source_target_pairs={{0,44},{4,0},{8,4},{12,8},{16,12},{20,16},{24,20},{28,24},{32,28},... | collective-permute-start | bytes 516104 | tf_op jit(solution)/shard_map/ppermute | solution.py:29
  55.0 1.9 collective-permute-start.6
  56.9 4.6 %collective-permute-start.12 = (bf16[24,3584]{1,0:T(8,128)(2,1)S(1)}, bf16[24,3584]{1,0:T(8,128)(2,1)S(1)}, u32[]{:S(2)}, u32[]{:S(2)}) collective-permute-start(bf16[24,3584]{1,0:T(8,128)(2,1)S(1)} %collective-permute-done.11), channel_id=1, source_target_pairs={{0,44},{4,0},{8,4},{12,8},{16,12},{20,16},{24,20},{28,24},{32,28},... | collective-permute-start | bytes 516104 | tf_op jit(solution)/shard_map/ppermute | solution.py:29
  64.1 4.6 %collective-permute-start.1 = (bf16[24,3584]{1,0:T(8,128)(2,1)S(1)}, bf16[24,3584]{1,0:T(8,128)(2,1)S(1)}, u32[]{:S(2)}, u32[]{:S(2)}) collective-permute-start(bf16[24,3584]{1,0:T(8,128)(2,1)S(1)} %collective-permute-done), channel_id=1, source_target_pairs={{0,44},{4,0},{8,4},{12,8},{16,12},{20,16},{24,20},{28,24},{32,28},... | collective-permute-start | bytes 516104 | tf_op jit(solution)/shard_map/ppermute | solution.py:29
  69.4 2.2 collective-permute-start.7
  71.5 4.6 %collective-permute-start.13 = (bf16[24,3584]{1,0:T(8,128)(2,1)S(1)}, bf16[24,3584]{1,0:T(8,128)(2,1)S(1)}, u32[]{:S(2)}, u32[]{:S(2)}) collective-permute-start(bf16[24,3584]{1,0:T(8,128)(2,1)S(1)} %collective-permute-done.12), channel_id=1, source_target_pairs={{0,44},{4,0},{8,4},{12,8},{16,12},{20,16},{24,20},{28,24},{32,28},... | collective-permute-start | bytes 516104 | tf_op jit(solution)/shard_map/ppermute | solution.py:29
  78.7 4.6 %collective-permute-start.2 = (bf16[24,3584]{1,0:T(8,128)(2,1)S(1)}, bf16[24,3584]{1,0:T(8,128)(2,1)S(1)}, u32[]{:S(2)}, u32[]{:S(2)}) collective-permute-start(bf16[24,3584]{1,0:T(8,128)(2,1)S(1)} %collective-permute-done.1), channel_id=1, source_target_pairs={{0,44},{4,0},{8,4},{12,8},{16,12},{20,16},{24,20},{28,24},{32,28},... | collective-permute-start | bytes 516104 | tf_op jit(solution)/shard_map/ppermute | solution.py:29
  85.9 4.6 %collective-permute-start.14 = (bf16[24,3584]{1,0:T(8,128)(2,1)S(1)}, bf16[24,3584]{1,0:T(8,128)(2,1)S(1)}, u32[]{:S(2)}, u32[]{:S(2)}) collective-permute-start(bf16[24,3584]{1,0:T(8,128)(2,1)S(1)} %collective-permute-done.13), channel_id=1, source_target_pairs={{0,44},{4,0},{8,4},{12,8},{16,12},{20,16},{24,20},{28,24},{32,28},... | collective-permute-start | bytes 516104 | tf_op jit(solution)/shard_map/ppermute | solution.py:29
  93.1 4.6 %collective-permute-start.3 = (bf16[24,3584]{1,0:T(8,128)(2,1)S(1)}, bf16[24,3584]{1,0:T(8,128)(2,1)S(1)}, u32[]{:S(2)}, u32[]{:S(2)}) collective-permute-start(bf16[24,3584]{1,0:T(8,128)(2,1)S(1)} %collective-permute-done.2), channel_id=1, source_target_pairs={{0,44},{4,0},{8,4},{12,8},{16,12},{20,16},{24,20},{28,24},{32,28},... | collective-permute-start | bytes 516104 | tf_op jit(solution)/shard_map/ppermute | solution.py:29
  100.3 4.6 %collective-permute-start.15 = (bf16[24,3584]{1,0:T(8,128)(2,1)S(1)}, bf16[24,3584]{1,0:T(8,128)(2,1)S(1)}, u32[]{:S(2)}, u32[]{:S(2)}) collective-permute-start(bf16[24,3584]{1,0:T(8,128)(2,1)S(1)} %collective-permute-done.14), channel_id=1, source_target_pairs={{0,44},{4,0},{8,4},{12,8},{16,12},{20,16},{24,20},{28,24},{32,28},... | collective-permute-start | bytes 516104 | tf_op jit(solution)/shard_map/ppermute | solution.py:29
  107.5 4.6 %collective-permute-start.4 = (bf16[24,3584]{1,0:T(8,128)(2,1)S(1)}, bf16[24,3584]{1,0:T(8,128)(2,1)S(1)}, u32[]{:S(2)}, u32[]{:S(2)}) collective-permute-start(bf16[24,3584]{1,0:T(8,128)(2,1)S(1)} %collective-permute-done.3), channel_id=1, source_target_pairs={{0,44},{4,0},{8,4},{12,8},{16,12},{20,16},{24,20},{28,24},{32,28},... | collective-permute-start | bytes 516104 | tf_op jit(solution)/shard_map/ppermute | solution.py:29
  114.7 1.9 collective-permute-start.21
  116.7 4.8 %collective-permute-start.5 = (bf16[24,3584]{1,0:T(8,128)(2,1)S(1)}, bf16[24,3584]{1,0:T(8,128)(2,1)S(1)}, u32[]{:S(2)}, u32[]{:S(2)}) collective-permute-start(bf16[24,3584]{1,0:T(8,128)(2,1)S(1)} %collective-permute-done.4), channel_id=1, source_target_pairs={{0,44},{4,0},{8,4},{12,8},{16,12},{20,16},{24,20},{28,24},{32,28},... | collective-permute-start | bytes 516104 | tf_op jit(solution)/shard_map/ppermute | solution.py:29
  127.8 3.0 fusion.3
  138.9 1.9 collective-permute-start.33
  140.8 4.6 %collective-permute-start.39 = (bf16[24,3584]{1,0:T(8,128)(2,1)S(1)}, bf16[24,3584]{1,0:T(8,128)(2,1)S(1)}, u32[]{:S(2)}, u32[]{:S(2)}) collective-permute-start(bf16[24,3584]{1,0:T(8,128)(2,1)S(1)} %get-tuple-element.36), channel_id=1, source_target_pairs={{0,44},{4,0},{8,4},{12,8},{16,12},{20,16},{24,20},{28,24},{32,28},... | collective-permute-start | bytes 516104 | tf_op jit(solution)/shard_map/ppermute | solution.py:29
  145.4 1.9 collective-permute-start.22
  147.3 4.6 %collective-permute-start.27 = (bf16[24,3584]{1,0:T(8,128)(2,1)S(1)}, bf16[24,3584]{1,0:T(8,128)(2,1)S(1)}, u32[]{:S(2)}, u32[]{:S(2)}) collective-permute-start(bf16[24,3584]{1,0:T(8,128)(2,1)S(1)} %get-tuple-element.26), channel_id=1, source_target_pairs={{0,44},{4,0},{8,4},{12,8},{16,12},{20,16},{24,20},{28,24},{32,28},... | collective-permute-start | bytes 516104 | tf_op jit(solution)/shard_map/ppermute | solution.py:29
  152.9 3.1 collective-permute-start.45
  157.0 3.4 %collective-permute-start.44 = (bf16[2,448,384]{2,1,0:T(8,128)(2,1)}, bf16[2,448,384]{2,1,0:T(8,128)(2,1)}, u32[]{:S(2)}, u32[]{:S(2)}) collective-permute-start(bf16[2,448,384]{2,1,0:T(8,128)(2,1)} %get-tuple-element.15), channel_id=1, source_target_pairs={{0,144},{48,0},{96,48},{144,96},{1,145},{49,1},{97,49},{145,97},{2... | collective-permute-start | bytes 2064392 | tf_op jit(solution)/shard_map/ppermute | solution.py:29
  160.5 1.9 collective-permute-start.34
  162.5 3.2 %collective-permute-start.48 = (bf16[2,448,384]{2,1,0:T(8,128)(2,1)S(1)}, bf16[2,448,384]{2,1,0:T(8,128)(2,1)S(1)}, u32[]{:S(2)}, u32[]{:S(2)}) collective-permute-start(bf16[2,448,384]{2,1,0:T(8,128)(2,1)S(1)} %get-tuple-element.14), channel_id=1, source_target_pairs={{0,144},{48,0},{96,48},{144,96},{1,145},{49,1},{97,49},{145,97},{2... | collective-permute-start | bytes 2064392 | tf_op jit(solution)/shard_map/ppermute | solution.py:29
  165.6 2.5 collective-permute-done.34
  168.1 2.1 collective-permute-start.28
  170.3 3.2 %collective-permute-start.35 = (bf16[24,3584]{1,0:T(8,128)(2,1)S(1)}, bf16[24,3584]{1,0:T(8,128)(2,1)S(1)}, u32[]{:S(2)}, u32[]{:S(2)}) collective-permute-start(bf16[24,3584]{1,0:T(8,128)(2,1)S(1)} %get-tuple-element.33), channel_id=1, source_target_pairs={{0,4},{4,8},{8,12},{12,16},{16,20},{20,24},{24,28},{28,32},{32,36}... | collective-permute-start | bytes 516104 | tf_op jit(solution)/shard_map/ppermute | solution.py:29
  174.7 2.9 collective-permute-start.40
  181.2 3.9 %collective-permute-start.29 = (bf16[24,3584]{1,0:T(8,128)(2,1)S(1)}, bf16[24,3584]{1,0:T(8,128)(2,1)S(1)}, u32[]{:S(2)}, u32[]{:S(2)}) collective-permute-start(bf16[24,3584]{1,0:T(8,128)(2,1)S(1)} %get-tuple-element.24), channel_id=1, source_target_pairs={{0,44},{4,0},{8,4},{12,8},{16,12},{20,16},{24,20},{28,24},{32,28},... | collective-permute-start | bytes 516104 | tf_op jit(solution)/shard_map/ppermute | solution.py:29
  187.9 4.6 %collective-permute-start.41 = (bf16[24,3584]{1,0:T(8,128)(2,1)S(1)}, bf16[24,3584]{1,0:T(8,128)(2,1)S(1)}, u32[]{:S(2)}, u32[]{:S(2)}) collective-permute-start(bf16[24,3584]{1,0:T(8,128)(2,1)S(1)} %get-tuple-element.32), channel_id=1, source_target_pairs={{0,44},{4,0},{8,4},{12,8},{16,12},{20,16},{24,20},{28,24},{32,28},... | collective-permute-start | bytes 516104 | tf_op jit(solution)/shard_map/ppermute | solution.py:29
  195.2 1.9 collective-permute-start.24
  197.3 4.6 %collective-permute-start.30 = (bf16[24,3584]{1,0:T(8,128)(2,1)S(1)}, bf16[24,3584]{1,0:T(8,128)(2,1)S(1)}, u32[]{:S(2)}, u32[]{:S(2)}) collective-permute-start(bf16[24,3584]{1,0:T(8,128)(2,1)S(1)} %get-tuple-element.22), channel_id=1, source_target_pairs={{0,44},{4,0},{8,4},{12,8},{16,12},{20,16},{24,20},{28,24},{32,28},... | collective-permute-start | bytes 516104 | tf_op jit(solution)/shard_map/ppermute | solution.py:29
  204.9 4.6 %collective-permute-start.42 = (bf16[24,3584]{1,0:T(8,128)(2,1)S(1)}, bf16[24,3584]{1,0:T(8,128)(2,1)S(1)}, u32[]{:S(2)}, u32[]{:S(2)}) collective-permute-start(bf16[24,3584]{1,0:T(8,128)(2,1)S(1)} %get-tuple-element.30), channel_id=1, source_target_pairs={{0,44},{4,0},{8,4},{12,8},{16,12},{20,16},{24,20},{28,24},{32,28},... | collective-permute-start | bytes 516104 | tf_op jit(solution)/shard_map/ppermute | solution.py:29
  209.6 1.9 collective-permute-start.25
  212.5 4.6 %collective-permute-start.31 = (bf16[24,3584]{1,0:T(8,128)(2,1)S(1)}, bf16[24,3584]{1,0:T(8,128)(2,1)S(1)}, u32[]{:S(2)}, u32[]{:S(2)}) collective-permute-start(bf16[24,3584]{1,0:T(8,128)(2,1)S(1)} %get-tuple-element.20), channel_id=1, source_target_pairs={{0,44},{4,0},{8,4},{12,8},{16,12},{20,16},{24,20},{28,24},{32,28},... | collective-permute-start | bytes 516104 | tf_op jit(solution)/shard_map/ppermute | solution.py:29
  217.1 3.7 %collective-permute-start.46 = (bf16[2,448,384]{2,1,0:T(8,128)(2,1)}, bf16[2,448,384]{2,1,0:T(8,128)(2,1)}, u32[]{:S(2)}, u32[]{:S(2)}) collective-permute-start(bf16[2,448,384]{2,1,0:T(8,128)(2,1)} %fusion.11), channel_id=1, source_target_pairs={{0,48},{48,96},{96,144},{144,0},{1,49},{49,97},{97,145},{145,1},{2... | collective-permute-start | bytes 2064392 | tf_op jit(solution)/shard_map/ppermute | solution.py:29
  222.8 3.6 %collective-permute-start.38 = (bf16[24,3584]{1,0:T(8,128)(2,1)S(1)}, bf16[24,3584]{1,0:T(8,128)(2,1)S(1)}, u32[]{:S(2)}, u32[]{:S(2)}) collective-permute-start(bf16[24,3584]{1,0:T(8,128)(2,1)S(1)} %get-tuple-element.27), channel_id=1, source_target_pairs={{0,4},{4,8},{8,12},{12,16},{16,20},{20,24},{24,28},{28,32},{32,36}... | collective-permute-start | bytes 516104 | tf_op jit(solution)/shard_map/ppermute | solution.py:29
  228.2 1.9 collective-permute-start.32
  230.2 3.3 %collective-permute-start.26 = (bf16[24,3584]{1,0:T(8,128)(2,1)S(1)}, bf16[24,3584]{1,0:T(8,128)(2,1)S(1)}, u32[]{:S(2)}, u32[]{:S(2)}) collective-permute-start(bf16[24,3584]{1,0:T(8,128)(2,1)S(1)} %get-tuple-element.17), channel_id=1, source_target_pairs={{0,4},{4,8},{8,12},{12,16},{16,20},{20,24},{24,28},{28,32},{32,36}... | collective-permute-start | bytes 516104 | tf_op jit(solution)/shard_map/ppermute | solution.py:29
  234.7 3.1 collective-permute-start.49
  238.8 22.8 %all-to-all-start.1 = ((bf16[4,6,7168]{2,1,0:T(8,128)(2,1)}), bf16[4,6,7168]{2,1,0:T(8,128)(2,1)}, u32[]{:S(2)}, u32[]{:S(2)}) async-start(bf16[4,6,7168]{2,1,0:T(8,128)(2,1)} %reshape.115), calls=%async_computation.1 | async-start | bytes 917504 | tf_op jit(solution)/shard_map/all_to_all | solution.py:157
  265.4 9.5 %collective-permute-start.52 = (bf16[448,384]{1,0:T(8,128)(2,1)S(1)}, bf16[448,384]{1,0:T(8,128)(2,1)S(1)}, u32[]{:S(2)}, u32[]{:S(2)}) collective-permute-start(bf16[448,384]{1,0:T(8,128)(2,1)S(1)} %get-tuple-element.39), channel_id=1, source_target_pairs={{0,576},{192,0},{384,192},{576,384},{1,577},{193,1},{385,193},{577... | collective-permute-start | bytes 1032200 | tf_op jit(solution)/shard_map/ppermute | solution.py:29
  276.8 2.2 collective-permute-start.50
  283.7 26.1 %collective-permute-done.51 = bf16[448,384]{1,0:T(8,128)(2,1)S(1)} collective-permute-done((bf16[448,384]{1,0:T(8,128)(2,1)S(1)}, bf16[448,384]{1,0:T(8,128)(2,1)S(1)}, u32[]{:S(2)}, u32[]{:S(2)}) %collective-permute-start.51) | collective-permute-done | bytes 344096 | tf_op jit(solution)/shard_map/ppermute | solution.py:29
  (162 shorter events, 77.2 us)
Async XLA Ops:
  6.8 25.0 %all-to-all-start = ((bf16[4,6,7168]{2,1,0:T(8,128)(2,1)}), bf16[4,6,7168]{2,1,0:T(8,128)(2,1)S(1)}, u32[]{:S(2)}, u32[]{:S(2)}) async-start(bf16[4,6,7168]{2,1,0:T(8,128)(2,1)} %reshape.113), calls=%async_computation | async-start | bytes 917504 | tf_op jit(solution)/shard_map/all_to_all | solution.py:113
  32.7 24.2 %collective-permute-start.11 = (bf16[24,3584]{1,0:T(8,128)(2,1)S(1)}, bf16[24,3584]{1,0:T(8,128)(2,1)S(1)}, u32[]{:S(2)}, u32[]{:S(2)}) collective-permute-start(bf16[24,3584]{1,0:T(8,128)(2,1)S(1)} %get-tuple-element.48), channel_id=1, source_target_pairs={{0,44},{4,0},{8,4},{12,8},{16,12},{20,16},{24,20},{28,24},{32,28},... | collective-permute-start | bytes 516104 | tf_op jit(solution)/shard_map/ppermute | solution.py:29
  48.5 13.7 %collective-permute-start.16 = (bf16[24,3584]{1,0:T(8,128)(2,1)S(1)}, bf16[24,3584]{1,0:T(8,128)(2,1)S(1)}, u32[]{:S(2)}, u32[]{:S(2)}) collective-permute-start(bf16[24,3584]{1,0:T(8,128)(2,1)S(1)} %get-tuple-element.48), channel_id=1, source_target_pairs={{0,4},{4,8},{8,12},{12,16},{16,20},{20,24},{24,28},{28,32},{32,36}... | collective-permute-start | bytes 516104 | tf_op jit(solution)/shard_map/ppermute | solution.py:29
  50.4 13.7 %collective-permute-start = (bf16[24,3584]{1,0:T(8,128)(2,1)S(1)}, bf16[24,3584]{1,0:T(8,128)(2,1)S(1)}, u32[]{:S(2)}, u32[]{:S(2)}) collective-permute-start(bf16[24,3584]{1,0:T(8,128)(2,1)S(1)} %get-tuple-element.45), channel_id=1, source_target_pairs={{0,44},{4,0},{8,4},{12,8},{16,12},{20,16},{24,20},{28,24},{32,28},... | collective-permute-start | bytes 516104 | tf_op jit(solution)/shard_map/ppermute | solution.py:29
  55.0 14.4 %collective-permute-start.6 = (bf16[24,3584]{1,0:T(8,128)(2,1)S(1)}, bf16[24,3584]{1,0:T(8,128)(2,1)S(1)}, u32[]{:S(2)}, u32[]{:S(2)}) collective-permute-start(bf16[24,3584]{1,0:T(8,128)(2,1)S(1)} %get-tuple-element.45), channel_id=1, source_target_pairs={{0,4},{4,8},{8,12},{12,16},{16,20},{20,24},{24,28},{28,32},{32,36}... | collective-permute-start | bytes 516104 | tf_op jit(solution)/shard_map/ppermute | solution.py:29
  56.9 14.6 %collective-permute-start.12 = (bf16[24,3584]{1,0:T(8,128)(2,1)S(1)}, bf16[24,3584]{1,0:T(8,128)(2,1)S(1)}, u32[]{:S(2)}, u32[]{:S(2)}) collective-permute-start(bf16[24,3584]{1,0:T(8,128)(2,1)S(1)} %collective-permute-done.11), channel_id=1, source_target_pairs={{0,44},{4,0},{8,4},{12,8},{16,12},{20,16},{24,20},{28,24},{32,28},... | collective-permute-start | bytes 516104 | tf_op jit(solution)/shard_map/ppermute | solution.py:29
  62.2 14.7 %collective-permute-start.17 = (bf16[24,3584]{1,0:T(8,128)(2,1)S(1)}, bf16[24,3584]{1,0:T(8,128)(2,1)S(1)}, u32[]{:S(2)}, u32[]{:S(2)}) collective-permute-start(bf16[24,3584]{1,0:T(8,128)(2,1)S(1)} %collective-permute-done.16), channel_id=1, source_target_pairs={{0,4},{4,8},{8,12},{12,16},{16,20},{20,24},{24,28},{28,32},{32,36}... | collective-permute-start | bytes 516104 | tf_op jit(solution)/shard_map/ppermute | solution.py:29
  64.1 14.6 %collective-permute-start.1 = (bf16[24,3584]{1,0:T(8,128)(2,1)S(1)}, bf16[24,3584]{1,0:T(8,128)(2,1)S(1)}, u32[]{:S(2)}, u32[]{:S(2)}) collective-permute-start(bf16[24,3584]{1,0:T(8,128)(2,1)S(1)} %collective-permute-done), channel_id=1, source_target_pairs={{0,44},{4,0},{8,4},{12,8},{16,12},{20,16},{24,20},{28,24},{32,28},... | collective-permute-start | bytes 516104 | tf_op jit(solution)/shard_map/ppermute | solution.py:29
  69.4 14.7 %collective-permute-start.7 = (bf16[24,3584]{1,0:T(8,128)(2,1)S(1)}, bf16[24,3584]{1,0:T(8,128)(2,1)S(1)}, u32[]{:S(2)}, u32[]{:S(2)}) collective-permute-start(bf16[24,3584]{1,0:T(8,128)(2,1)S(1)} %collective-permute-done.6), channel_id=1, source_target_pairs={{0,4},{4,8},{8,12},{12,16},{16,20},{20,24},{24,28},{28,32},{32,36}... | collective-permute-start | bytes 516104 | tf_op jit(solution)/shard_map/ppermute | solution.py:29
  71.5 14.4 %collective-permute-start.13 = (bf16[24,3584]{1,0:T(8,128)(2,1)S(1)}, bf16[24,3584]{1,0:T(8,128)(2,1)S(1)}, u32[]{:S(2)}, u32[]{:S(2)}) collective-permute-start(bf16[24,3584]{1,0:T(8,128)(2,1)S(1)} %collective-permute-done.12), channel_id=1, source_target_pairs={{0,44},{4,0},{8,4},{12,8},{16,12},{20,16},{24,20},{28,24},{32,28},... | collective-permute-start | bytes 516104 | tf_op jit(solution)/shard_map/ppermute | solution.py:29
  76.8 14.4 %collective-permute-start.18 = (bf16[24,3584]{1,0:T(8,128)(2,1)S(1)}, bf16[24,3584]{1,0:T(8,128)(2,1)S(1)}, u32[]{:S(2)}, u32[]{:S(2)}) collective-permute-start(bf16[24,3584]{1,0:T(8,128)(2,1)S(1)} %collective-permute-done.17), channel_id=1, source_target_pairs={{0,4},{4,8},{8,12},{12,16},{16,20},{20,24},{24,28},{28,32},{32,36}... | collective-permute-start | bytes 516104 | tf_op jit(solution)/shard_map/ppermute | solution.py:29
  78.7 14.4 %collective-permute-start.2 = (bf16[24,3584]{1,0:T(8,128)(2,1)S(1)}, bf16[24,3584]{1,0:T(8,128)(2,1)S(1)}, u32[]{:S(2)}, u32[]{:S(2)}) collective-permute-start(bf16[24,3584]{1,0:T(8,128)(2,1)S(1)} %collective-permute-done.1), channel_id=1, source_target_pairs={{0,44},{4,0},{8,4},{12,8},{16,12},{20,16},{24,20},{28,24},{32,28},... | collective-permute-start | bytes 516104 | tf_op jit(solution)/shard_map/ppermute | solution.py:29
  84.0 14.4 %collective-permute-start.8 = (bf16[24,3584]{1,0:T(8,128)(2,1)S(1)}, bf16[24,3584]{1,0:T(8,128)(2,1)S(1)}, u32[]{:S(2)}, u32[]{:S(2)}) collective-permute-start(bf16[24,3584]{1,0:T(8,128)(2,1)S(1)} %collective-permute-done.7), channel_id=1, source_target_pairs={{0,4},{4,8},{8,12},{12,16},{16,20},{20,24},{24,28},{28,32},{32,36}... | collective-permute-start | bytes 516104 | tf_op jit(solution)/shard_map/ppermute | solution.py:29
  85.9 14.4 %collective-permute-start.14 = (bf16[24,3584]{1,0:T(8,128)(2,1)S(1)}, bf16[24,3584]{1,0:T(8,128)(2,1)S(1)}, u32[]{:S(2)}, u32[]{:S(2)}) collective-permute-start(bf16[24,3584]{1,0:T(8,128)(2,1)S(1)} %collective-permute-done.13), channel_id=1, source_target_pairs={{0,44},{4,0},{8,4},{12,8},{16,12},{20,16},{24,20},{28,24},{32,28},... | collective-permute-start | bytes 516104 | tf_op jit(solution)/shard_map/ppermute | solution.py:29
  91.2 14.4 %collective-permute-start.19 = (bf16[24,3584]{1,0:T(8,128)(2,1)S(1)}, bf16[24,3584]{1,0:T(8,128)(2,1)S(1)}, u32[]{:S(2)}, u32[]{:S(2)}) collective-permute-start(bf16[24,3584]{1,0:T(8,128)(2,1)S(1)} %collective-permute-done.18), channel_id=1, source_target_pairs={{0,4},{4,8},{8,12},{12,16},{16,20},{20,24},{24,28},{28,32},{32,36}... | collective-permute-start | bytes 516104 | tf_op jit(solution)/shard_map/ppermute | solution.py:29
  93.1 14.4 %collective-permute-start.3 = (bf16[24,3584]{1,0:T(8,128)(2,1)S(1)}, bf16[24,3584]{1,0:T(8,128)(2,1)S(1)}, u32[]{:S(2)}, u32[]{:S(2)}) collective-permute-start(bf16[24,3584]{1,0:T(8,128)(2,1)S(1)} %collective-permute-done.2), channel_id=1, source_target_pairs={{0,44},{4,0},{8,4},{12,8},{16,12},{20,16},{24,20},{28,24},{32,28},... | collective-permute-start | bytes 516104 | tf_op jit(solution)/shard_map/ppermute | solution.py:29
  98.4 14.4 %collective-permute-start.9 = (bf16[24,3584]{1,0:T(8,128)(2,1)S(1)}, bf16[24,3584]{1,0:T(8,128)(2,1)S(1)}, u32[]{:S(2)}, u32[]{:S(2)}) collective-permute-start(bf16[24,3584]{1,0:T(8,128)(2,1)S(1)} %collective-permute-done.8), channel_id=1, source_target_pairs={{0,4},{4,8},{8,12},{12,16},{16,20},{20,24},{24,28},{28,32},{32,36}... | collective-permute-start | bytes 516104 | tf_op jit(solution)/shard_map/ppermute | solution.py:29
  100.3 21.8 %collective-permute-start.15 = (bf16[24,3584]{1,0:T(8,128)(2,1)S(1)}, bf16[24,3584]{1,0:T(8,128)(2,1)S(1)}, u32[]{:S(2)}, u32[]{:S(2)}) collective-permute-start(bf16[24,3584]{1,0:T(8,128)(2,1)S(1)} %collective-permute-done.14), channel_id=1, source_target_pairs={{0,44},{4,0},{8,4},{12,8},{16,12},{20,16},{24,20},{28,24},{32,28},... | collective-permute-start | bytes 516104 | tf_op jit(solution)/shard_map/ppermute | solution.py:29
  105.6 9.1 %collective-permute-start.20 = (bf16[24,3584]{1,0:T(8,128)(2,1)S(1)}, bf16[24,3584]{1,0:T(8,128)(2,1)S(1)}, u32[]{:S(2)}, u32[]{:S(2)}) collective-permute-start(bf16[24,3584]{1,0:T(8,128)(2,1)S(1)} %collective-permute-done.19), channel_id=1, source_target_pairs={{0,4},{4,8},{8,12},{12,16},{16,20},{20,24},{24,28},{28,32},{32,36}... | collective-permute-start | bytes 516104 | tf_op jit(solution)/shard_map/ppermute | solution.py:29
  107.5 9.1 %collective-permute-start.4 = (bf16[24,3584]{1,0:T(8,128)(2,1)S(1)}, bf16[24,3584]{1,0:T(8,128)(2,1)S(1)}, u32[]{:S(2)}, u32[]{:S(2)}) collective-permute-start(bf16[24,3584]{1,0:T(8,128)(2,1)S(1)} %collective-permute-done.3), channel_id=1, source_target_pairs={{0,44},{4,0},{8,4},{12,8},{16,12},{20,16},{24,20},{28,24},{32,28},... | collective-permute-start | bytes 516104 | tf_op jit(solution)/shard_map/ppermute | solution.py:29
  112.8 18.0 %collective-permute-start.10 = (bf16[24,3584]{1,0:T(8,128)(2,1)S(1)}, bf16[24,3584]{1,0:T(8,128)(2,1)S(1)}, u32[]{:S(2)}, u32[]{:S(2)}) collective-permute-start(bf16[24,3584]{1,0:T(8,128)(2,1)S(1)} %collective-permute-done.9), channel_id=1, source_target_pairs={{0,4},{4,8},{8,12},{12,16},{16,20},{20,24},{24,28},{28,32},{32,36}... | collective-permute-start | bytes 516104 | tf_op jit(solution)/shard_map/ppermute | solution.py:29
  114.7 8.2 %collective-permute-start.21 = (bf16[24,3584]{1,0:T(8,128)(2,1)S(1)}, bf16[24,3584]{1,0:T(8,128)(2,1)S(1)}, u32[]{:S(2)}, u32[]{:S(2)}) collective-permute-start(bf16[24,3584]{1,0:T(8,128)(2,1)S(1)} %collective-permute-done.20), channel_id=1, source_target_pairs={{0,4},{4,8},{8,12},{12,16},{16,20},{20,24},{24,28},{28,32},{32,36}... | collective-permute-start | bytes 516104 | tf_op jit(solution)/shard_map/ppermute | solution.py:29
  116.7 10.4 %collective-permute-start.5 = (bf16[24,3584]{1,0:T(8,128)(2,1)S(1)}, bf16[24,3584]{1,0:T(8,128)(2,1)S(1)}, u32[]{:S(2)}, u32[]{:S(2)}) collective-permute-start(bf16[24,3584]{1,0:T(8,128)(2,1)S(1)} %collective-permute-done.4), channel_id=1, source_target_pairs={{0,44},{4,0},{8,4},{12,8},{16,12},{20,16},{24,20},{28,24},{32,28},... | collective-permute-start | bytes 516104 | tf_op jit(solution)/shard_map/ppermute | solution.py:29
  138.9 18.2 %collective-permute-start.33 = (bf16[24,3584]{1,0:T(8,128)(2,1)S(1)}, bf16[24,3584]{1,0:T(8,128)(2,1)S(1)}, u32[]{:S(2)}, u32[]{:S(2)}) collective-permute-start(bf16[24,3584]{1,0:T(8,128)(2,1)S(1)} %get-tuple-element.35), channel_id=1, source_target_pairs={{0,4},{4,8},{8,12},{12,16},{16,20},{20,24},{24,28},{28,32},{32,36}... | collective-permute-start | bytes 516104 | tf_op jit(solution)/shard_map/ppermute | solution.py:29
  140.8 21.7 %collective-permute-start.39 = (bf16[24,3584]{1,0:T(8,128)(2,1)S(1)}, bf16[24,3584]{1,0:T(8,128)(2,1)S(1)}, u32[]{:S(2)}, u32[]{:S(2)}) collective-permute-start(bf16[24,3584]{1,0:T(8,128)(2,1)S(1)} %get-tuple-element.36), channel_id=1, source_target_pairs={{0,44},{4,0},{8,4},{12,8},{16,12},{20,16},{24,20},{28,24},{32,28},... | collective-permute-start | bytes 516104 | tf_op jit(solution)/shard_map/ppermute | solution.py:29
  145.4 24.9 %collective-permute-start.22 = (bf16[24,3584]{1,0:T(8,128)(2,1)S(1)}, bf16[24,3584]{1,0:T(8,128)(2,1)S(1)}, u32[]{:S(2)}, u32[]{:S(2)}) collective-permute-start(bf16[24,3584]{1,0:T(8,128)(2,1)S(1)} %get-tuple-element.25), channel_id=1, source_target_pairs={{0,4},{4,8},{8,12},{12,16},{16,20},{20,24},{24,28},{28,32},{32,36}... | collective-permute-start | bytes 516104 | tf_op jit(solution)/shard_map/ppermute | solution.py:29
  147.3 13.1 %collective-permute-start.27 = (bf16[24,3584]{1,0:T(8,128)(2,1)S(1)}, bf16[24,3584]{1,0:T(8,128)(2,1)S(1)}, u32[]{:S(2)}, u32[]{:S(2)}) collective-permute-start(bf16[24,3584]{1,0:T(8,128)(2,1)S(1)} %get-tuple-element.26), channel_id=1, source_target_pairs={{0,44},{4,0},{8,4},{12,8},{16,12},{20,16},{24,20},{28,24},{32,28},... | collective-permute-start | bytes 516104 | tf_op jit(solution)/shard_map/ppermute | solution.py:29
  152.9 44.4 %collective-permute-start.45 = (bf16[2,448,384]{2,1,0:T(8,128)(2,1)S(1)}, bf16[2,448,384]{2,1,0:T(8,128)(2,1)S(1)}, u32[]{:S(2)}, u32[]{:S(2)}) collective-permute-start(bf16[2,448,384]{2,1,0:T(8,128)(2,1)S(1)} %get-tuple-element.16), channel_id=1, source_target_pairs={{0,48},{48,96},{96,144},{144,0},{1,49},{49,97},{97,145},{145,1},{2... | collective-permute-start | bytes 2064392 | tf_op jit(solution)/shard_map/ppermute | solution.py:29
  157.0 104.6 %collective-permute-start.44 = (bf16[2,448,384]{2,1,0:T(8,128)(2,1)}, bf16[2,448,384]{2,1,0:T(8,128)(2,1)}, u32[]{:S(2)}, u32[]{:S(2)}) collective-permute-start(bf16[2,448,384]{2,1,0:T(8,128)(2,1)} %get-tuple-element.15), channel_id=1, source_target_pairs={{0,144},{48,0},{96,48},{144,96},{1,145},{49,1},{97,49},{145,97},{2... | collective-permute-start | bytes 2064392 | tf_op jit(solution)/shard_map/ppermute | solution.py:29
  160.5 7.7 %collective-permute-start.34 = (bf16[24,3584]{1,0:T(8,128)(2,1)S(1)}, bf16[24,3584]{1,0:T(8,128)(2,1)S(1)}, u32[]{:S(2)}, u32[]{:S(2)}) collective-permute-start(bf16[24,3584]{1,0:T(8,128)(2,1)S(1)} %add_convert_fusion.9), channel_id=1, source_target_pairs={{0,4},{4,8},{8,12},{12,16},{16,20},{20,24},{24,28},{28,32},{32,36}... | collective-permute-start | bytes 516104 | tf_op jit(solution)/shard_map/ppermute | solution.py:29
  162.5 47.1 %collective-permute-start.48 = (bf16[2,448,384]{2,1,0:T(8,128)(2,1)S(1)}, bf16[2,448,384]{2,1,0:T(8,128)(2,1)S(1)}, u32[]{:S(2)}, u32[]{:S(2)}) collective-permute-start(bf16[2,448,384]{2,1,0:T(8,128)(2,1)S(1)} %get-tuple-element.14), channel_id=1, source_target_pairs={{0,144},{48,0},{96,48},{144,96},{1,145},{49,1},{97,49},{145,97},{2... | collective-permute-start | bytes 2064392 | tf_op jit(solution)/shard_map/ppermute | solution.py:29
  170.3 8.3 %collective-permute-start.35 = (bf16[24,3584]{1,0:T(8,128)(2,1)S(1)}, bf16[24,3584]{1,0:T(8,128)(2,1)S(1)}, u32[]{:S(2)}, u32[]{:S(2)}) collective-permute-start(bf16[24,3584]{1,0:T(8,128)(2,1)S(1)} %get-tuple-element.33), channel_id=1, source_target_pairs={{0,4},{4,8},{8,12},{12,16},{16,20},{20,24},{24,28},{28,32},{32,36}... | collective-permute-start | bytes 516104 | tf_op jit(solution)/shard_map/ppermute | solution.py:29
  178.6 7.3 %collective-permute-start.23 = (bf16[24,3584]{1,0:T(8,128)(2,1)S(1)}, bf16[24,3584]{1,0:T(8,128)(2,1)S(1)}, u32[]{:S(2)}, u32[]{:S(2)}) collective-permute-start(bf16[24,3584]{1,0:T(8,128)(2,1)S(1)} %get-tuple-element.23), channel_id=1, source_target_pairs={{0,4},{4,8},{8,12},{12,16},{16,20},{20,24},{24,28},{28,32},{32,36}... | collective-permute-start | bytes 516104 | tf_op jit(solution)/shard_map/ppermute | solution.py:29
  193.3 69.9 %collective-permute-start.47 = (bf16[2,448,384]{2,1,0:T(8,128)(2,1)}, bf16[2,448,384]{2,1,0:T(8,128)(2,1)}, u32[]{:S(2)}, u32[]{:S(2)}) collective-permute-start(bf16[2,448,384]{2,1,0:T(8,128)(2,1)} %get-tuple-element.13), channel_id=1, source_target_pairs={{0,48},{48,96},{96,144},{144,0},{1,49},{49,97},{97,145},{145,1},{2... | collective-permute-start | bytes 2064392 | tf_op jit(solution)/shard_map/ppermute | solution.py:29
  195.2 7.7 %collective-permute-start.24 = (bf16[24,3584]{1,0:T(8,128)(2,1)S(1)}, bf16[24,3584]{1,0:T(8,128)(2,1)S(1)}, u32[]{:S(2)}, u32[]{:S(2)}) collective-permute-start(bf16[24,3584]{1,0:T(8,128)(2,1)S(1)} %get-tuple-element.21), channel_id=1, source_target_pairs={{0,4},{4,8},{8,12},{12,16},{16,20},{20,24},{24,28},{28,32},{32,36}... | collective-permute-start | bytes 516104 | tf_op jit(solution)/shard_map/ppermute | solution.py:29
  197.3 7.6 %collective-permute-start.30 = (bf16[24,3584]{1,0:T(8,128)(2,1)S(1)}, bf16[24,3584]{1,0:T(8,128)(2,1)S(1)}, u32[]{:S(2)}, u32[]{:S(2)}) collective-permute-start(bf16[24,3584]{1,0:T(8,128)(2,1)S(1)} %get-tuple-element.22), channel_id=1, source_target_pairs={{0,44},{4,0},{8,4},{12,8},{16,12},{20,16},{24,20},{28,24},{32,28},... | collective-permute-start | bytes 516104 | tf_op jit(solution)/shard_map/ppermute | solution.py:29
  203.0 9.6 %collective-permute-start.37 = (bf16[24,3584]{1,0:T(8,128)(2,1)S(1)}, bf16[24,3584]{1,0:T(8,128)(2,1)S(1)}, u32[]{:S(2)}, u32[]{:S(2)}) collective-permute-start(bf16[24,3584]{1,0:T(8,128)(2,1)S(1)} %get-tuple-element.29), channel_id=1, source_target_pairs={{0,4},{4,8},{8,12},{12,16},{16,20},{20,24},{24,28},{28,32},{32,36}... | collective-permute-start | bytes 516104 | tf_op jit(solution)/shard_map/ppermute | solution.py:29
  204.9 12.2 %collective-permute-start.42 = (bf16[24,3584]{1,0:T(8,128)(2,1)S(1)}, bf16[24,3584]{1,0:T(8,128)(2,1)S(1)}, u32[]{:S(2)}, u32[]{:S(2)}) collective-permute-start(bf16[24,3584]{1,0:T(8,128)(2,1)S(1)} %get-tuple-element.30), channel_id=1, source_target_pairs={{0,44},{4,0},{8,4},{12,8},{16,12},{20,16},{24,20},{28,24},{32,28},... | collective-permute-start | bytes 516104 | tf_op jit(solution)/shard_map/ppermute | solution.py:29
  209.6 11.3 %collective-permute-start.25 = (bf16[24,3584]{1,0:T(8,128)(2,1)S(1)}, bf16[24,3584]{1,0:T(8,128)(2,1)S(1)}, u32[]{:S(2)}, u32[]{:S(2)}) collective-permute-start(bf16[24,3584]{1,0:T(8,128)(2,1)S(1)} %get-tuple-element.19), channel_id=1, source_target_pairs={{0,4},{4,8},{8,12},{12,16},{16,20},{20,24},{24,28},{28,32},{32,36}... | collective-permute-start | bytes 516104 | tf_op jit(solution)/shard_map/ppermute | solution.py:29
  212.5 10.3 %collective-permute-start.31 = (bf16[24,3584]{1,0:T(8,128)(2,1)S(1)}, bf16[24,3584]{1,0:T(8,128)(2,1)S(1)}, u32[]{:S(2)}, u32[]{:S(2)}) collective-permute-start(bf16[24,3584]{1,0:T(8,128)(2,1)S(1)} %get-tuple-element.20), channel_id=1, source_target_pairs={{0,44},{4,0},{8,4},{12,8},{16,12},{20,16},{24,20},{28,24},{32,28},... | collective-permute-start | bytes 516104 | tf_op jit(solution)/shard_map/ppermute | solution.py:29
  217.1 44.5 %collective-permute-start.46 = (bf16[2,448,384]{2,1,0:T(8,128)(2,1)}, bf16[2,448,384]{2,1,0:T(8,128)(2,1)}, u32[]{:S(2)}, u32[]{:S(2)}) collective-permute-start(bf16[2,448,384]{2,1,0:T(8,128)(2,1)} %fusion.11), channel_id=1, source_target_pairs={{0,48},{48,96},{96,144},{144,0},{1,49},{49,97},{97,145},{145,1},{2... | collective-permute-start | bytes 2064392 | tf_op jit(solution)/shard_map/ppermute | solution.py:29
  222.8 7.4 %collective-permute-start.38 = (bf16[24,3584]{1,0:T(8,128)(2,1)S(1)}, bf16[24,3584]{1,0:T(8,128)(2,1)S(1)}, u32[]{:S(2)}, u32[]{:S(2)}) collective-permute-start(bf16[24,3584]{1,0:T(8,128)(2,1)S(1)} %get-tuple-element.27), channel_id=1, source_target_pairs={{0,4},{4,8},{8,12},{12,16},{16,20},{20,24},{24,28},{28,32},{32,36}... | collective-permute-start | bytes 516104 | tf_op jit(solution)/shard_map/ppermute | solution.py:29
  230.2 7.6 %collective-permute-start.26 = (bf16[24,3584]{1,0:T(8,128)(2,1)S(1)}, bf16[24,3584]{1,0:T(8,128)(2,1)S(1)}, u32[]{:S(2)}, u32[]{:S(2)}) collective-permute-start(bf16[24,3584]{1,0:T(8,128)(2,1)S(1)} %get-tuple-element.17), channel_id=1, source_target_pairs={{0,4},{4,8},{8,12},{12,16},{16,20},{20,24},{24,28},{28,32},{32,36}... | collective-permute-start | bytes 516104 | tf_op jit(solution)/shard_map/ppermute | solution.py:29
  234.7 28.5 %collective-permute-start.49 = (bf16[2,448,384]{2,1,0:T(8,128)(2,1)}, bf16[2,448,384]{2,1,0:T(8,128)(2,1)}, u32[]{:S(2)}, u32[]{:S(2)}) collective-permute-start(bf16[2,448,384]{2,1,0:T(8,128)(2,1)} %fusion.8), channel_id=1, source_target_pairs={{0,144},{48,0},{96,48},{144,96},{1,145},{49,1},{97,49},{145,97},{2... | collective-permute-start | bytes 2064392 | tf_op jit(solution)/shard_map/ppermute | solution.py:29
  238.8 40.2 %all-to-all-start.1 = ((bf16[4,6,7168]{2,1,0:T(8,128)(2,1)}), bf16[4,6,7168]{2,1,0:T(8,128)(2,1)}, u32[]{:S(2)}, u32[]{:S(2)}) async-start(bf16[4,6,7168]{2,1,0:T(8,128)(2,1)} %reshape.115), calls=%async_computation.1 | async-start | bytes 917504 | tf_op jit(solution)/shard_map/all_to_all | solution.py:157
  265.4 18.3 %collective-permute-start.52 = (bf16[448,384]{1,0:T(8,128)(2,1)S(1)}, bf16[448,384]{1,0:T(8,128)(2,1)S(1)}, u32[]{:S(2)}, u32[]{:S(2)}) collective-permute-start(bf16[448,384]{1,0:T(8,128)(2,1)S(1)} %get-tuple-element.39), channel_id=1, source_target_pairs={{0,576},{192,0},{384,192},{576,384},{1,577},{193,1},{385,193},{577... | collective-permute-start | bytes 1032200 | tf_op jit(solution)/shard_map/ppermute | solution.py:29
  274.9 34.9 %collective-permute-start.51 = (bf16[448,384]{1,0:T(8,128)(2,1)S(1)}, bf16[448,384]{1,0:T(8,128)(2,1)S(1)}, u32[]{:S(2)}, u32[]{:S(2)}) collective-permute-start(bf16[448,384]{1,0:T(8,128)(2,1)S(1)} %get-tuple-element.38), channel_id=1, source_target_pairs={{0,384},{192,576},{384,0},{576,192},{1,385},{193,577},{385,1},{577... | collective-permute-start | bytes 1032200 | tf_op jit(solution)/shard_map/ppermute | solution.py:29
  276.8 33.0 %collective-permute-start.50 = (bf16[448,384]{1,0:T(8,128)(2,1)S(1)}, bf16[448,384]{1,0:T(8,128)(2,1)}, u32[]{:S(2)}, u32[]{:S(2)}) collective-permute-start(bf16[448,384]{1,0:T(8,128)(2,1)S(1)} %get-tuple-element.37), channel_id=1, source_target_pairs={{0,192},{192,384},{384,576},{576,0},{1,193},{193,385},{385,577},{5... | collective-permute-start | bytes 1032200 | tf_op jit(solution)/shard_map/ppermute | solution.py:29
  (13 other events, 189.8 us)

commit v4 on v2

--- a/solution.py
+++ b/solution.py
@@ -33,37 +33,37 @@
     return sum(term.astype(jnp.float32) for term in terms).astype(jnp.bfloat16)
 
 
-def scatter_shares(shares, pieces):
+def scatter_shares(shares, cuts):
     nx, ny = lax.axis_size("x"), lax.axis_size("yl")
     px, py = lax.axis_index("x"), lax.axis_index("yl")
     grid = shares.reshape(ny, nx, shares.shape[0] // (nx * ny), shares.shape[1])
-    rows = grid.shape[2] // pieces
     low, high = slice(0, ny // 2), slice(ny // 2, ny)
+    edges = (0,) + cuts + (grid.shape[2],)
     done = []
-    for piece in range(pieces):
-        part = grid[:, :, piece * rows : (piece + 1) * rows]
+    for piece in range(len(edges) - 1):
+        part = grid[:, :, edges[piece] : edges[piece + 1]]
 
         def chunk(step, half):
             return lax.dynamic_index_in_dim(part[half], (px + step) % nx, 1, keepdims=False)
 
-        far_low = shift(chunk(2, low), "x", 1)
-        far_high = shift(chunk(2, high), "x", -1)
-        near_high = shift(chunk(1, high), "x", 1)
-        near_low = shift(chunk(-1, low), "x", -1)
-        rest_low = shift(total(chunk(1, low), far_low), "x", 1)
-        rest_high = shift(total(chunk(-1, high), far_high), "x", -1)
+        right = shift(jnp.concatenate([chunk(2, low), chunk(1, high)], axis=0), "x", 1)
+        left = shift(jnp.concatenate([chunk(2, high), chunk(-1, low)], axis=0), "x", -1)
+        rests = lax.optimization_barrier((total(chunk(1, low), right[low]), total(chunk(-1, high), left[low])))
+        rest_low = shift(rests[0], "x", 1)
+        rest_high = shift(rests[1], "x", -1)
         mine = jnp.concatenate(
-            [total(chunk(0, low), near_low, rest_low), total(chunk(0, high), near_high, rest_high)], axis=0
+            [total(chunk(0, low), left[high], rest_low), total(chunk(0, high), right[high], rest_high)], axis=0
         )
 
         def target(step):
             return lax.dynamic_index_in_dim(mine, (py + step) % ny, 0, keepdims=False)
 
-        done.append(total(target(0), *[shift(target(step), "yl", step) for step in range(1, ny)]))
+        others = [shift(target(step), "yl", step) for step in (2, 1, 3)]
+        done.append(total(target(0), *others))
     return jnp.concatenate(done, axis=0)
 
 
-def local(hidden, grad_out, routes, combine, w_gate, w_up, w_down):
+def layer(hidden, grad_out, routes, combine, w_gate, w_up, w_down):
     experts = lax.axis_size("yh") * lax.axis_size("c")
     width = hidden.shape[1]
     f_dev = w_gate.shape[2]
@@ -72,22 +72,28 @@
     wts = lax.dynamic_index_in_dim(combine[0, :, 0], node, 0, keepdims=False)
     pick_tok, pick_cot, mix_out, cot_weight, slots = slot_plan(ids, wts, experts)
     bf16 = jnp.bfloat16
-    weights = jnp.concatenate([w_gate[0], w_up[0], w_down[0].T], axis=1)
+    weights = lax.optimization_barrier(jnp.concatenate([w_gate[0], w_up[0], w_down[0].T], axis=1))
 
     send_tok = jnp.dot(pick_tok.astype(bf16), hidden, preferred_element_type=jnp.float32)
     send_cot = jnp.dot(pick_cot.astype(bf16), grad_out, preferred_element_type=jnp.float32)
     send = (send_tok + send_cot * cot_weight[:, None]).astype(bf16)
     own = send.shape[0]
-    got = lax.all_to_all(
-        send.reshape(experts, own // experts, width), ("yh", "c"), split_axis=0, concat_axis=0, tiled=True
-    ).reshape(own, width)
-    rows = lax.all_gather(got, "z", axis=0, tiled=True)
+    wide = 3 * width // 4
 
-    pre = jnp.dot(rows, weights, preferred_element_type=jnp.float32)
+    def exchange(block):
+        return lax.all_to_all(
+            block.reshape(experts, own // experts, block.shape[1]), ("yh", "c"), split_axis=0, concat_axis=0, tiled=True
+        ).reshape(block.shape)
+
+    rows_wide = lax.all_gather(exchange(send[:, :wide]), "z", axis=0, tiled=True)
+    rows_rest = lax.all_gather(exchange(send[:, wide:]), "z", axis=0, tiled=True)
+
+    pre = jnp.dot(rows_rest, weights[wide:], preferred_element_type=jnp.float32)
+    pre = pre + jnp.dot(rows_wide, weights[:wide], preferred_element_type=jnp.float32)
     gate_pre = pre[:, :f_dev]
     up_pre = pre[:, f_dev : 2 * f_dev]
     hidden_grad = jnp.roll(pre[:, 2 * f_dev :], -slots, axis=0)
-    is_tok = ((jnp.arange(rows.shape[0]) % (2 * slots)) < slots)[:, None]
+    is_tok = ((jnp.arange(pre.shape[0]) % (2 * slots)) < slots)[:, None]
     sig = jax.nn.sigmoid(gate_pre)
     hid = gate_pre * sig * up_pre
     dgate = hidden_grad * up_pre * sig * (1.0 + gate_pre * (1.0 - sig))
@@ -101,17 +107,21 @@
         axis=1,
     ).astype(bf16)
 
-    shares = lax.dot_general(
-        rows, mids, (((0,), (0,)), ((), ())), preferred_element_type=jnp.float32
-    ).astype(bf16)
+    shares = jnp.concatenate(
+        [
+            lax.dot_general(
+                block, mids, (((0,), (0,)), ((), ())), preferred_element_type=jnp.float32
+            ).astype(bf16)
+            for block in (rows_wide, rows_rest)
+        ],
+        axis=0,
+    )
     parts = lax.dot_general(
         mids, weights, (((1,), (1,)), ((), ())), preferred_element_type=jnp.float32
     ).astype(bf16)
     summed = lax.psum_scatter(parts, "z", scatter_dimension=0, tiled=True)
-    grads = scatter_shares(shares, 2)
-    back = lax.all_to_all(
-        summed.reshape(experts, own // experts, width), ("yh", "c"), split_axis=0, concat_axis=0, tiled=True
-    ).reshape(own, width).astype(jnp.float32)
+    grads = scatter_shares(shares, (shares.shape[0] * 4 // (7 * 16),))
+    back = exchange(summed).astype(jnp.float32)
     high = lax.Precision.HIGHEST
     layer_out = jnp.dot(mix_out.T, back, precision=high).astype(bf16)
     grad_in = jnp.dot(pick_tok.T, back, precision=high).astype(bf16)
@@ -126,7 +136,7 @@
     dp, echip = ("yl", "x"), ("yh", "c")
     every = dp + ("z",) + echip
     return jax.shard_map(
-        local,
+        layer,
         mesh=fine,
         in_specs=(
             P(every, None),

time: 225 us -> 238 us (1.058)
  the two profiles are of different devices: /device:TPU:8 before, /device:TPU:1 now
where the time goes in v4:
time: 238 us; the launch traced here: 237 us
  blocking collectives  64.6 us (27%)
  starting transfers between devices  64.4 us (27%)
  waiting for transfers between devices  33.7 us (14%)
  other arithmetic  23.6 us (10%)
  matrix products  21.3 us (9%)
  local copies, waits for them, and re-layouts  14.7 us (6%)
  between operations  14.7 us (6%)
    ppermute x14, starting transfers between devices, shift(): lax.ppermute(value, axis, [(i, (i + step) % size) for i in range(size)])  45.5 us
    all_gather x1, blocking collectives, layer(): lax.all_gather(exchange(send[:, wide:]), 'z', axis=0, tiled=True)  41.8 us
    ppermute x14, waiting for transfers between devices, shift(): lax.ppermute(value, axis, [(i, (i + step) % size) for i in range(size)])  26.1 us
    all_to_all x1, blocking collectives, exchange(): lax.all_to_all(block.reshape(experts, own // experts, block.shape[1]), ('...  22.8 us
    all_to_all x2, starting transfers between devices, exchange(): lax.all_to_all(block.reshape(experts, own // experts, block.shape[1]), ('...  18.9 us
    convert_element_type x10, other arithmetic, total(): sum((term.astype(jnp.float32) for term in terms)).astype(jnp.bfloat16)  10.7 us
    unnamed x25, local copies, waits for them, and re-layouts  7.63 us
    all_gather x1, waiting for transfers between devices, layer(): lax.all_gather(exchange(send[:, :wide]), 'z', axis=0, tiled=True)  7.48 us
  transfers between devices with their start and end apart: 18, of which 4 were waited for; matrix products, arithmetic and copies ran while one was open for 15% of the time, Pallas kernels for 0%

profile of v4, /device:TPU:1, one launch (start us, length us, event | category | flops | bytes accessed | tf_op | source)
XLA Modules:
  0.0 236.9 jit_solution(10318458234591119938)
XLA Ops:
  7.2 0.9 fusion.59
  11.2 1.2 fusion.1
  12.6 22.8 %all_to_all.15 = bf16[4,6,5376]{2,1,0:T(8,128)(2,1)S(1)} all-to-all(bf16[4,6,5376]{2,1,0:T(8,128)(2,1)S(1)} %reshape.128), channel_id=1, replica_groups=mesh['yl'=4,'x'=4,'z'=12,'yh'=2,'c'=2] {'yh','c'}, dimensions={0} | all-to-all | bytes 516096 | tf_op jit(solution)/shard_map/all_to_all | solution.py:84
  36.9 5.1 %all-to-all-start = ((bf16[4,6,1792]{2,1,0:T(8,128)(2,1)}), bf16[4,6,1792]{2,1,0:T(8,128)(2,1)S(1)}, u32[]{:S(2)}, u32[]{:S(2)}) async-start(bf16[4,6,1792]{2,1,0:T(8,128)(2,1)} %reshape.126), calls=%async_computation | async-start | bytes 229376 | tf_op jit(solution)/shard_map/all_to_all | solution.py:84
  42.0 2.8 %copy.56 = bf16[1,7168,128]{1,2,0:T(8,128)(2,1)S(1)} copy(bf16[1,7168,128]{2,1,0:T(8,128)(2,1)} %param.12) | data formatting | bytes 3670016 | tf_op args[5]
  44.8 3.9 %copy.55 = bf16[1,7168,128]{1,2,0:T(8,128)(2,1)} copy(bf16[1,7168,128]{2,1,0:T(8,128)(2,1)} %param.11) | data formatting | bytes 3670016 | tf_op args[4]
  48.7 5.1 %pad_maximum_fusion = bf16[7168,384]{0,1:T(8,128)(2,1)} fusion(bf16[7168,128]{0,1:T(8,128)(2,1)} %bitcast.129, bf16[7168,128]{0,1:T(8,128)(2,1)S(1)} %bitcast.127, bf16[7168,128]{0,1:T(8,128)(2,1)} %bitcast.128), kind=kLoop, calls=%fused_computation.7 | loop fusion | flops 16515072 | bytes 11010048 | tf_op jit(solution)/shard_map/concatenate | solution.py:75
  53.9 41.8 %all_gather.6 = bf16[288,1792]{1,0:T(8,128)(2,1)S(1)} all-gather(bf16[24,1792]{1,0:T(8,128)(2,1)S(1)} %reshape.127), channel_id=1, replica_groups=mesh['yl'=4,'x'=4,'z'=12,'yh'=2,'c'=2] {'z'}, dimensions={0}, use_global_device_ids=true | all-gather | bytes 1118208 | tf_op jit(solution)/shard_map/all_gather | solution.py:89
  95.6 7.5 %all-gather.2.cloned.1.call-done = bf16[288,5376]{1,0:T(8,128)(2,1)} async-done(((bf16[24,5376]{1,0:T(8,128)(2,1)}), bf16[288,5376]{1,0:T(8,128)(2,1)}) %all-gather.2.cloned.1.call-update) | async-done | bytes 3096592 | tf_op jit(solution)/shard_map/all_gather | solution.py:88
  103.1 4.9 %fusion.2 = f32[288,384]{1,0:T(8,128)S(1)} fusion(bf16[288,5376]{1,0:T(8,128)(2,1)} %all-gather.2.cloned.1.call-done, bf16[7168,384]{0,1:T(8,128)(2,1)} %pad_maximum_fusion), kind=kOutput, calls=%fused_computation.9 | convolution fusion | flops 1189085184 | bytes 7667712 | tf_op jit(solution)/shard_map/dot_general | solution.py:92
  108.0 2.1 fusion.6
  110.4 6.9 %convolution_convert_fusion = bf16[288,7168]{1,0:T(8,128)(2,1)} fusion(bf16[7168,384]{0,1:T(8,128)(2,1)} %pad_maximum_fusion, bf16[288,128]{1,0:T(8,128)(2,1)S(1)} %fusion.43, bf16[288,128]{1,0:T(8,128)(2,1)S(1)} %get-tuple-element.37, bf16[288,128]{1,0:T(8,128)(2,1)S(1)} %get-tuple-element.36), kind=kOutput, calls=%fused_computation | convolution fusion | flops 1588174848 | bytes 9854976 | tf_op jit(solution)/shard_map/dot_general | solution.py:119
  117.4 1.1 convolution_convert_fusion.4
  119.3 3.0 %convolution_convert_fusion.1 = bf16[5376,384]{1,0:T(8,128)(2,1)S(1)} fusion(bf16[288,5376]{1,0:T(8,128)(2,1)S(1)} %copy-done.10, bf16[288,128]{1,0:T(8,128)(2,1)S(1)} %fusion.43, bf16[288,128]{1,0:T(8,128)(2,1)S(1)} %get-tuple-element.37, bf16[288,128]{1,0:T(8,128)(2,1)S(1)} %get-tuple-element.36), kind=kOutput, calls=%fused_computation.1 | convolution fusion | flops 1191813120 | bytes 7446528 | tf_op jit(solution)/shard_map/dot_general | solution.py:112
  123.2 1.1 pad_maximum_fusion.5
  124.4 3.0 %collective-permute-start.8 = (bf16[4,192,384]{2,1,0:T(8,128)(2,1)}, bf16[4,192,384]{2,1,0:T(8,128)(2,1)}, u32[]{:S(2)}, u32[]{:S(2)}) collective-permute-start(bf16[4,192,384]{2,1,0:T(8,128)(2,1)} %pad_maximum_fusion.5), channel_id=1, source_target_pairs={{0,48},{48,96},{96,144},{144,0},{1,49},{49,97},{97,145},{145,1},{2... | collective-permute-start | bytes 1769480 | tf_op jit(solution)/shard_map/ppermute | solution.py:29
  128.3 3.5 %collective-permute-start.7 = (bf16[4,192,384]{2,1,0:T(8,128)(2,1)}, bf16[4,192,384]{2,1,0:T(8,128)(2,1)}, u32[]{:S(2)}, u32[]{:S(2)}) collective-permute-start(bf16[4,192,384]{2,1,0:T(8,128)(2,1)} %pad_maximum_fusion.4), channel_id=1, source_target_pairs={{0,144},{48,0},{96,48},{144,96},{1,145},{49,1},{97,49},{145,97},{2... | collective-permute-start | bytes 1769480 | tf_op jit(solution)/shard_map/ppermute | solution.py:29
  132.3 1.0 pad_maximum_fusion.3
  133.3 1.9 collective-permute-start.1
  135.2 1.0 pad_maximum_fusion.2
  136.2 4.6 %collective-permute-start = (bf16[4,256,384]{2,1,0:T(8,128)(2,1)}, bf16[4,256,384]{2,1,0:T(8,128)(2,1)}, u32[]{:S(2)}, u32[]{:S(2)}) collective-permute-start(bf16[4,256,384]{2,1,0:T(8,128)(2,1)} %pad_maximum_fusion.2), channel_id=1, source_target_pairs={{0,144},{48,0},{96,48},{144,96},{1,145},{49,1},{97,49},{145,97},{2... | collective-permute-start | bytes 2359304 | tf_op jit(solution)/shard_map/ppermute | solution.py:29
  140.8 1.1 fusion.18
  142.0 1.1 fusion.17
  143.1 1.9 collective-permute-start.9
  145.1 4.6 %collective-permute-start.10 = (bf16[2,192,384]{2,1,0:T(8,128)(2,1)S(1)}, bf16[2,192,384]{2,1,0:T(8,128)(2,1)S(1)}, u32[]{:S(2)}, u32[]{:S(2)}) collective-permute-start(bf16[2,192,384]{2,1,0:T(8,128)(2,1)S(1)} %fusion.17), channel_id=1, source_target_pairs={{0,144},{48,0},{96,48},{144,96},{1,145},{49,1},{97,49},{145,97},{2... | collective-permute-start | bytes 884744 | tf_op jit(solution)/shard_map/ppermute | solution.py:29
  149.7 6.6 %collective-permute-done.1 = bf16[4,256,384]{2,1,0:T(8,128)(2,1)} collective-permute-done((bf16[4,256,384]{2,1,0:T(8,128)(2,1)}, bf16[4,256,384]{2,1,0:T(8,128)(2,1)}, u32[]{:S(2)}, u32[]{:S(2)}) %collective-permute-start.1) | collective-permute-done | bytes 786464 | tf_op jit(solution)/shard_map/ppermute | solution.py:29
  156.3 1.1 fusion.12
  157.4 1.0 collective-permute-done
  158.4 1.1 fusion.11
  159.5 2.5 %collective-permute-start.2 = (bf16[2,256,384]{2,1,0:T(8,128)(2,1)S(1)}, bf16[2,256,384]{2,1,0:T(8,128)(2,1)S(1)}, u32[]{:S(2)}, u32[]{:S(2)}) collective-permute-start(bf16[2,256,384]{2,1,0:T(8,128)(2,1)S(1)} %fusion.12), channel_id=1, source_target_pairs={{0,48},{48,96},{96,144},{144,0},{1,49},{49,97},{97,145},{145,1},{2... | collective-permute-start | bytes 1179656 | tf_op jit(solution)/shard_map/ppermute | solution.py:29
  162.1 4.9 %collective-permute-start.3 = (bf16[2,256,384]{2,1,0:T(8,128)(2,1)S(1)}, bf16[2,256,384]{2,1,0:T(8,128)(2,1)S(1)}, u32[]{:S(2)}, u32[]{:S(2)}) collective-permute-start(bf16[2,256,384]{2,1,0:T(8,128)(2,1)S(1)} %fusion.11), channel_id=1, source_target_pairs={{0,144},{48,0},{96,48},{144,96},{1,145},{49,1},{97,49},{145,97},{2... | collective-permute-start | bytes 1179656 | tf_op jit(solution)/shard_map/ppermute | solution.py:29
  167.0 1.2 fusion.20
  168.2 1.2 fusion.16
  169.4 0.9 fusion.40
  170.3 3.7 %collective-permute-start.13 = (bf16[192,384]{1,0:T(8,128)(2,1)}, bf16[192,384]{1,0:T(8,128)(2,1)}, u32[]{:S(2)}, u32[]{:S(2)}) collective-permute-start(bf16[192,384]{1,0:T(8,128)(2,1)} %get-tuple-element.40), channel_id=1, source_target_pairs={{0,576},{192,0},{384,192},{576,384},{1,577},{193,1},{385,193},{577... | collective-permute-start | bytes 442376 | tf_op jit(solution)/shard_map/ppermute | solution.py:29
  174.0 1.9 collective-permute-start.12
  175.9 3.6 %collective-permute-start.11 = (bf16[192,384]{1,0:T(8,128)(2,1)}, bf16[192,384]{1,0:T(8,128)(2,1)}, u32[]{:S(2)}, u32[]{:S(2)}) collective-permute-start(bf16[192,384]{1,0:T(8,128)(2,1)} %get-tuple-element.38), channel_id=1, source_target_pairs={{0,384},{192,576},{384,0},{576,192},{1,385},{193,577},{385,1},{577... | collective-permute-start | bytes 442376 | tf_op jit(solution)/shard_map/ppermute | solution.py:29
  179.6 1.2 fusion.14
  180.8 1.3 fusion.10
  182.4 3.6 %collective-permute-start.6 = (bf16[256,384]{1,0:T(8,128)(2,1)S(1)}, bf16[256,384]{1,0:T(8,128)(2,1)S(1)}, u32[]{:S(2)}, u32[]{:S(2)}) collective-permute-start(bf16[256,384]{1,0:T(8,128)(2,1)S(1)} %get-tuple-element.35), channel_id=1, source_target_pairs={{0,576},{192,0},{384,192},{576,384},{1,577},{193,1},{385,193},{577... | collective-permute-start | bytes 589832 | tf_op jit(solution)/shard_map/ppermute | solution.py:29
  186.0 2.2 collective-permute-start.5
  188.2 1.9 reshape.130
  190.1 13.8 %all-to-all-start.2 = ((bf16[4,6,7168]{2,1,0:T(8,128)(2,1)}), bf16[4,6,7168]{2,1,0:T(8,128)(2,1)S(1)}, u32[]{:S(2)}, u32[]{:S(2)}) async-start(bf16[4,6,7168]{2,1,0:T(8,128)(2,1)} %reshape.130), calls=%async_computation.3 | async-start | bytes 917504 | tf_op jit(solution)/shard_map/all_to_all | solution.py:84
  203.9 3.6 %collective-permute-start.4 = (bf16[256,384]{1,0:T(8,128)(2,1)S(1)}, bf16[256,384]{1,0:T(8,128)(2,1)S(1)}, u32[]{:S(2)}, u32[]{:S(2)}) collective-permute-start(bf16[256,384]{1,0:T(8,128)(2,1)S(1)} %get-tuple-element.33), channel_id=1, source_target_pairs={{0,384},{192,576},{384,0},{576,192},{1,385},{193,577},{385,1},{577... | collective-permute-start | bytes 589832 | tf_op jit(solution)/shard_map/ppermute | solution.py:29
  207.5 1.2 fusion.26
  208.7 18.4 %collective-permute-done.4 = bf16[256,384]{1,0:T(8,128)(2,1)S(1)} collective-permute-done((bf16[256,384]{1,0:T(8,128)(2,1)S(1)}, bf16[256,384]{1,0:T(8,128)(2,1)S(1)}, u32[]{:S(2)}, u32[]{:S(2)}) %collective-permute-start.4) | collective-permute-done | bytes 196640 | tf_op jit(solution)/shard_map/ppermute | solution.py:29
  228.2 0.9 convolution_convert_fusion.2
  229.1 0.9 convolution_convert_fusion.3
  (80 shorter events, 9.6 us)
Async XLA Ops:
  7.2 3.7 %copy-start = (bf16[6,7168]{1,0:T(8,128)(2,1)S(1)}, bf16[6,7168]{1,0:T(8,128)(2,1)}, u32[]{:S(2)}) copy-start(bf16[6,7168]{1,0:T(8,128)(2,1)} %param.7) | copy-start | bytes 258052
  7.2 96.0 %all-gather.2.cloned.1.call-start = ((), (), s32[]{:S(2)}) async-start(), calls=%async_computation.4 | async-start | bytes 3354624 | tf_op jit(solution)/shard_map/all_gather | solution.py:88
  10.1 1.2 copy-start.7
  36.9 16.9 %all-to-all-start = ((bf16[4,6,1792]{2,1,0:T(8,128)(2,1)}), bf16[4,6,1792]{2,1,0:T(8,128)(2,1)S(1)}, u32[]{:S(2)}, u32[]{:S(2)}) async-start(bf16[4,6,1792]{2,1,0:T(8,128)(2,1)} %reshape.126), calls=%async_computation | async-start | bytes 229376 | tf_op jit(solution)/shard_map/all_to_all | solution.py:84
  42.0 146.2 %reduce-scatter.2.cloned.1.call-start = ((), (), s32[]{:S(2)}) async-start(), calls=%async_computation.5 | async-start | bytes 4472832 | tf_op jit(solution)/shard_map/reduce_scatter | solution.py:122
  117.4 1.9 copy-start.10
  123.1 5.2 %copy-start.1 = (bf16[2,4,192,384]{3,2,1,0:T(8,128)(2,1)}, bf16[2,4,192,384]{3,2,1,0:T(8,128)(2,1)S(1)}, u32[]{:S(2)}) copy-start(bf16[2,4,192,384]{3,2,1,0:T(8,128)(2,1)S(1)} %get-tuple-element.22) | copy-start | bytes 3538948
  123.1 5.2 %copy-start.2 = (bf16[2,4,192,384]{3,2,1,0:T(8,128)(2,1)}, bf16[2,4,192,384]{3,2,1,0:T(8,128)(2,1)S(1)}, u32[]{:S(2)}) copy-start(bf16[2,4,192,384]{3,2,1,0:T(8,128)(2,1)S(1)} %get-tuple-element.21) | copy-start | bytes 3538948
  124.4 16.5 %collective-permute-start.8 = (bf16[4,192,384]{2,1,0:T(8,128)(2,1)}, bf16[4,192,384]{2,1,0:T(8,128)(2,1)}, u32[]{:S(2)}, u32[]{:S(2)}) collective-permute-start(bf16[4,192,384]{2,1,0:T(8,128)(2,1)} %pad_maximum_fusion.5), channel_id=1, source_target_pairs={{0,48},{48,96},{96,144},{144,0},{1,49},{49,97},{97,145},{145,1},{2... | collective-permute-start | bytes 1769480 | tf_op jit(solution)/shard_map/ppermute | solution.py:29
  128.3 13.7 %collective-permute-start.7 = (bf16[4,192,384]{2,1,0:T(8,128)(2,1)}, bf16[4,192,384]{2,1,0:T(8,128)(2,1)}, u32[]{:S(2)}, u32[]{:S(2)}) collective-permute-start(bf16[4,192,384]{2,1,0:T(8,128)(2,1)} %pad_maximum_fusion.4), channel_id=1, source_target_pairs={{0,144},{48,0},{96,48},{144,96},{1,145},{49,1},{97,49},{145,97},{2... | collective-permute-start | bytes 1769480 | tf_op jit(solution)/shard_map/ppermute | solution.py:29
  133.3 23.0 %collective-permute-start.1 = (bf16[4,256,384]{2,1,0:T(8,128)(2,1)}, bf16[4,256,384]{2,1,0:T(8,128)(2,1)}, u32[]{:S(2)}, u32[]{:S(2)}) collective-permute-start(bf16[4,256,384]{2,1,0:T(8,128)(2,1)} %pad_maximum_fusion.3), channel_id=1, source_target_pairs={{0,48},{48,96},{96,144},{144,0},{1,49},{49,97},{97,145},{145,1},{2... | collective-permute-start | bytes 2359304 | tf_op jit(solution)/shard_map/ppermute | solution.py:29
  136.2 22.2 %collective-permute-start = (bf16[4,256,384]{2,1,0:T(8,128)(2,1)}, bf16[4,256,384]{2,1,0:T(8,128)(2,1)}, u32[]{:S(2)}, u32[]{:S(2)}) collective-permute-start(bf16[4,256,384]{2,1,0:T(8,128)(2,1)} %pad_maximum_fusion.2), channel_id=1, source_target_pairs={{0,144},{48,0},{96,48},{144,96},{1,145},{49,1},{97,49},{145,97},{2... | collective-permute-start | bytes 2359304 | tf_op jit(solution)/shard_map/ppermute | solution.py:29
  143.1 23.8 %collective-permute-start.9 = (bf16[2,192,384]{2,1,0:T(8,128)(2,1)S(1)}, bf16[2,192,384]{2,1,0:T(8,128)(2,1)S(1)}, u32[]{:S(2)}, u32[]{:S(2)}) collective-permute-start(bf16[2,192,384]{2,1,0:T(8,128)(2,1)S(1)} %fusion.18), channel_id=1, source_target_pairs={{0,48},{48,96},{96,144},{144,0},{1,49},{49,97},{97,145},{145,1},{2... | collective-permute-start | bytes 884744 | tf_op jit(solution)/shard_map/ppermute | solution.py:29
  145.1 23.1 %collective-permute-start.10 = (bf16[2,192,384]{2,1,0:T(8,128)(2,1)S(1)}, bf16[2,192,384]{2,1,0:T(8,128)(2,1)S(1)}, u32[]{:S(2)}, u32[]{:S(2)}) collective-permute-start(bf16[2,192,384]{2,1,0:T(8,128)(2,1)S(1)} %fusion.17), channel_id=1, source_target_pairs={{0,144},{48,0},{96,48},{144,96},{1,145},{49,1},{97,49},{145,97},{2... | collective-permute-start | bytes 884744 | tf_op jit(solution)/shard_map/ppermute | solution.py:29
  159.5 20.0 %collective-permute-start.2 = (bf16[2,256,384]{2,1,0:T(8,128)(2,1)S(1)}, bf16[2,256,384]{2,1,0:T(8,128)(2,1)S(1)}, u32[]{:S(2)}, u32[]{:S(2)}) collective-permute-start(bf16[2,256,384]{2,1,0:T(8,128)(2,1)S(1)} %fusion.12), channel_id=1, source_target_pairs={{0,48},{48,96},{96,144},{144,0},{1,49},{49,97},{97,145},{145,1},{2... | collective-permute-start | bytes 1179656 | tf_op jit(solution)/shard_map/ppermute | solution.py:29
  162.1 18.7 %collective-permute-start.3 = (bf16[2,256,384]{2,1,0:T(8,128)(2,1)S(1)}, bf16[2,256,384]{2,1,0:T(8,128)(2,1)S(1)}, u32[]{:S(2)}, u32[]{:S(2)}) collective-permute-start(bf16[2,256,384]{2,1,0:T(8,128)(2,1)S(1)} %fusion.11), channel_id=1, source_target_pairs={{0,144},{48,0},{96,48},{144,96},{1,145},{49,1},{97,49},{145,97},{2... | collective-permute-start | bytes 1179656 | tf_op jit(solution)/shard_map/ppermute | solution.py:29
  169.3 10.2 %copy-start.5 = (bf16[2,192,384]{2,1,0:T(8,128)(2,1)}, bf16[2,192,384]{2,1,0:T(8,128)(2,1)S(1)}, u32[]{:S(2)}) copy-start(bf16[2,192,384]{2,1,0:T(8,128)(2,1)S(1)} %fusion.16) | copy-start | bytes 884740
  170.3 33.6 %collective-permute-start.13 = (bf16[192,384]{1,0:T(8,128)(2,1)}, bf16[192,384]{1,0:T(8,128)(2,1)}, u32[]{:S(2)}, u32[]{:S(2)}) collective-permute-start(bf16[192,384]{1,0:T(8,128)(2,1)} %get-tuple-element.40), channel_id=1, source_target_pairs={{0,576},{192,0},{384,192},{576,384},{1,577},{193,1},{385,193},{577... | collective-permute-start | bytes 442376 | tf_op jit(solution)/shard_map/ppermute | solution.py:29
  174.0 33.5 %collective-permute-start.12 = (bf16[192,384]{1,0:T(8,128)(2,1)}, bf16[192,384]{1,0:T(8,128)(2,1)}, u32[]{:S(2)}, u32[]{:S(2)}) collective-permute-start(bf16[192,384]{1,0:T(8,128)(2,1)} %get-tuple-element.39), channel_id=1, source_target_pairs={{0,192},{192,384},{384,576},{576,0},{1,193},{193,385},{385,577},{5... | collective-permute-start | bytes 442376 | tf_op jit(solution)/shard_map/ppermute | solution.py:29
  175.9 31.5 %collective-permute-start.11 = (bf16[192,384]{1,0:T(8,128)(2,1)}, bf16[192,384]{1,0:T(8,128)(2,1)}, u32[]{:S(2)}, u32[]{:S(2)}) collective-permute-start(bf16[192,384]{1,0:T(8,128)(2,1)} %get-tuple-element.38), channel_id=1, source_target_pairs={{0,384},{192,576},{384,0},{576,192},{1,385},{193,577},{385,1},{577... | collective-permute-start | bytes 442376 | tf_op jit(solution)/shard_map/ppermute | solution.py:29
  180.7 1.3 copy-start.3
  180.7 26.7 %copy-start.6 = (bf16[2,192,384]{2,1,0:T(8,128)(2,1)S(1)}, bf16[2,192,384]{2,1,0:T(8,128)(2,1)}, u32[]{:S(2)}) copy-start(bf16[2,192,384]{2,1,0:T(8,128)(2,1)} %copy-done.5) | copy-start | bytes 884740
  182.4 44.8 %copy-start.4 = (bf16[2,256,384]{2,1,0:T(8,128)(2,1)S(1)}, bf16[2,256,384]{2,1,0:T(8,128)(2,1)}, u32[]{:S(2)}) copy-start(bf16[2,256,384]{2,1,0:T(8,128)(2,1)} %copy-done.3) | copy-start | bytes 1179652
  182.4 45.8 %copy-start.8 = (f32[24,6]{0,1:T(8,128)S(1)}, f32[24,6]{0,1:T(8,128)}, u32[]{:S(2)}) copy-start(f32[24,6]{0,1:T(8,128)} %copy-done.7) | copy-start | bytes 1732
  182.4 26.3 %collective-permute-start.6 = (bf16[256,384]{1,0:T(8,128)(2,1)S(1)}, bf16[256,384]{1,0:T(8,128)(2,1)S(1)}, u32[]{:S(2)}, u32[]{:S(2)}) collective-permute-start(bf16[256,384]{1,0:T(8,128)(2,1)S(1)} %get-tuple-element.35), channel_id=1, source_target_pairs={{0,576},{192,0},{384,192},{576,384},{1,577},{193,1},{385,193},{577... | collective-permute-start | bytes 589832 | tf_op jit(solution)/shard_map/ppermute | solution.py:29
  186.0 43.1 %copy-start.9 = (f32[24,6]{0,1:T(8,128)S(1)}, f32[24,6]{0,1:T(8,128)}, u32[]{:S(2)}) copy-start(f32[24,6]{0,1:T(8,128)} %get-tuple-element.14) | copy-start | bytes 1732
  186.0 22.7 %collective-permute-start.5 = (bf16[256,384]{1,0:T(8,128)(2,1)S(1)}, bf16[256,384]{1,0:T(8,128)(2,1)S(1)}, u32[]{:S(2)}, u32[]{:S(2)}) collective-permute-start(bf16[256,384]{1,0:T(8,128)(2,1)S(1)} %get-tuple-element.34), channel_id=1, source_target_pairs={{0,192},{192,384},{384,576},{576,0},{1,193},{193,385},{385,577},{5... | collective-permute-start | bytes 589832 | tf_op jit(solution)/shard_map/ppermute | solution.py:29
  190.1 37.9 %all-to-all-start.2 = ((bf16[4,6,7168]{2,1,0:T(8,128)(2,1)}), bf16[4,6,7168]{2,1,0:T(8,128)(2,1)S(1)}, u32[]{:S(2)}, u32[]{:S(2)}) async-start(bf16[4,6,7168]{2,1,0:T(8,128)(2,1)} %reshape.130), calls=%async_computation.3 | async-start | bytes 917504 | tf_op jit(solution)/shard_map/all_to_all | solution.py:84
  203.9 23.3 %collective-permute-start.4 = (bf16[256,384]{1,0:T(8,128)(2,1)S(1)}, bf16[256,384]{1,0:T(8,128)(2,1)S(1)}, u32[]{:S(2)}, u32[]{:S(2)}) collective-permute-start(bf16[256,384]{1,0:T(8,128)(2,1)S(1)} %get-tuple-element.33), channel_id=1, source_target_pairs={{0,384},{192,576},{384,0},{576,192},{1,385},{193,577},{385,1},{577... | collective-permute-start | bytes 589832 | tf_op jit(solution)/shard_map/ppermute | solution.py:29
Sparse Core Ops, SparseCore 0:
  36.3 66.7 all-gather.1
  117.5 62.3 reduce-scatter.1

commit v5 on v2

--- a/solution.py
+++ b/solution.py
@@ -33,37 +33,37 @@
     return sum(term.astype(jnp.float32) for term in terms).astype(jnp.bfloat16)
 
 
-def scatter_shares(shares, pieces):
+def scatter_shares(shares, cuts):
     nx, ny = lax.axis_size("x"), lax.axis_size("yl")
     px, py = lax.axis_index("x"), lax.axis_index("yl")
     grid = shares.reshape(ny, nx, shares.shape[0] // (nx * ny), shares.shape[1])
-    rows = grid.shape[2] // pieces
     low, high = slice(0, ny // 2), slice(ny // 2, ny)
+    edges = (0,) + cuts + (grid.shape[2],)
     done = []
-    for piece in range(pieces):
-        part = grid[:, :, piece * rows : (piece + 1) * rows]
+    for piece in range(len(edges) - 1):
+        part = grid[:, :, edges[piece] : edges[piece + 1]]
 
         def chunk(step, half):
             return lax.dynamic_index_in_dim(part[half], (px + step) % nx, 1, keepdims=False)
 
-        far_low = shift(chunk(2, low), "x", 1)
-        far_high = shift(chunk(2, high), "x", -1)
-        near_high = shift(chunk(1, high), "x", 1)
-        near_low = shift(chunk(-1, low), "x", -1)
-        rest_low = shift(total(chunk(1, low), far_low), "x", 1)
-        rest_high = shift(total(chunk(-1, high), far_high), "x", -1)
+        right = shift(jnp.concatenate([chunk(2, low), chunk(1, high)], axis=0), "x", 1)
+        left = shift(jnp.concatenate([chunk(2, high), chunk(-1, low)], axis=0), "x", -1)
+        rests = lax.optimization_barrier((total(chunk(1, low), right[low]), total(chunk(-1, high), left[low])))
+        rest_low = shift(rests[0], "x", 1)
+        rest_high = shift(rests[1], "x", -1)
         mine = jnp.concatenate(
-            [total(chunk(0, low), near_low, rest_low), total(chunk(0, high), near_high, rest_high)], axis=0
+            [total(chunk(0, low), left[high], rest_low), total(chunk(0, high), right[high], rest_high)], axis=0
         )
 
         def target(step):
             return lax.dynamic_index_in_dim(mine, (py + step) % ny, 0, keepdims=False)
 
-        done.append(total(target(0), *[shift(target(step), "yl", step) for step in range(1, ny)]))
+        others = [shift(target(step), "yl", step) for step in (2, 1, 3)]
+        done.append(total(target(0), *others))
     return jnp.concatenate(done, axis=0)
 
 
-def local(hidden, grad_out, routes, combine, w_gate, w_up, w_down):
+def layer(hidden, grad_out, routes, combine, w_gate, w_up, w_down):
     experts = lax.axis_size("yh") * lax.axis_size("c")
     width = hidden.shape[1]
     f_dev = w_gate.shape[2]
@@ -72,7 +72,7 @@
     wts = lax.dynamic_index_in_dim(combine[0, :, 0], node, 0, keepdims=False)
     pick_tok, pick_cot, mix_out, cot_weight, slots = slot_plan(ids, wts, experts)
     bf16 = jnp.bfloat16
-    weights = jnp.concatenate([w_gate[0], w_up[0], w_down[0].T], axis=1)
+    weights = lax.optimization_barrier(jnp.concatenate([w_gate[0], w_up[0], w_down[0].T], axis=1))
 
     send_tok = jnp.dot(pick_tok.astype(bf16), hidden, preferred_element_type=jnp.float32)
     send_cot = jnp.dot(pick_cot.astype(bf16), grad_out, preferred_element_type=jnp.float32)
@@ -108,7 +108,7 @@
         mids, weights, (((1,), (1,)), ((), ())), preferred_element_type=jnp.float32
     ).astype(bf16)
     summed = lax.psum_scatter(parts, "z", scatter_dimension=0, tiled=True)
-    grads = scatter_shares(shares, 2)
+    grads = scatter_shares(shares, (144,))
     back = lax.all_to_all(
         summed.reshape(experts, own // experts, width), ("yh", "c"), split_axis=0, concat_axis=0, tiled=True
     ).reshape(own, width).astype(jnp.float32)
@@ -126,7 +126,7 @@
     dp, echip = ("yl", "x"), ("yh", "c")
     every = dp + ("z",) + echip
     return jax.shard_map(
-        local,
+        layer,
         mesh=fine,
         in_specs=(
             P(every, None),

time: 225 us -> 247 us (1.098)
  the two profiles are of different devices: /device:TPU:8 before, /device:TPU:1 now
where the time goes in v5:
time: 247 us; the launch traced here: 246 us
  waiting for transfers between devices  93.7 us (38%)
  starting transfers between devices  57.4 us (23%)
  blocking collectives  24.1 us (10%)
  other arithmetic  22.4 us (9%)
  matrix products  19.7 us (8%)
  between operations  14.6 us (6%)
  local copies, waits for them, and re-layouts  14.2 us (6%)
    all_gather x1, waiting for transfers between devices, layer(): rows = lax.all_gather(got, 'z', axis=0, tiled=True)  52.7 us
    ppermute x14, starting transfers between devices, shift(): lax.ppermute(value, axis, [(i, (i + step) % size) for i in range(size)])  44.6 us
    ppermute x14, waiting for transfers between devices, shift(): lax.ppermute(value, axis, [(i, (i + step) % size) for i in range(size)])  40.9 us
    all_to_all x1, blocking collectives, layer(): lax.all_to_all(send.reshape(experts, own // experts, width), ('yh', 'c'),...  24.1 us
    all_to_all x1, starting transfers between devices, layer(): lax.all_to_all(summed.reshape(experts, own // experts, width), ('yh', 'c'...  12.7 us
    convert_element_type x10, other arithmetic, total(): sum((term.astype(jnp.float32) for term in terms)).astype(jnp.bfloat16)  10.6 us
    unnamed x13, local copies, waits for them, and re-layouts  7.74 us
    dot_general x1, matrix products, layer(): pre = jnp.dot(rows, weights, preferred_element_type=jnp.float32)  6.26 us
  transfers between devices with their start and end apart: 17, of which 4 were waited for; matrix products, arithmetic and copies ran while one was open for 15% of the time, Pallas kernels for 0%

profile of v5, /device:TPU:1, one launch (start us, length us, event | category | flops | bytes accessed | tf_op | source)
XLA Modules:
  0.0 246.1 jit_solution(2035765639370103022)
XLA Ops:
  7.2 0.9 fusion.54
  8.8 0.9 fusion.53
  10.6 1.2 fusion.1
  12.0 24.1 %all_to_all.10 = bf16[4,6,7168]{2,1,0:T(8,128)(2,1)S(1)} all-to-all(bf16[4,6,7168]{2,1,0:T(8,128)(2,1)S(1)} %reshape.120), channel_id=1, replica_groups=mesh['yl'=4,'x'=4,'z'=12,'yh'=2,'c'=2] {'yh','c'}, dimensions={0} | all-to-all | bytes 688128 | tf_op jit(solution)/shard_map/all_to_all | solution.py:81
  36.1 0.9 reshape.121
  37.0 2.8 %copy.56 = bf16[1,7168,128]{1,2,0:T(8,128)(2,1)S(1)} copy(bf16[1,7168,128]{2,1,0:T(8,128)(2,1)} %param.12) | data formatting | bytes 3670016 | tf_op args[5]
  39.8 3.9 %copy.55 = bf16[1,7168,128]{1,2,0:T(8,128)(2,1)} copy(bf16[1,7168,128]{2,1,0:T(8,128)(2,1)} %param.11) | data formatting | bytes 3670016 | tf_op args[4]
  43.7 5.0 %pad_maximum_fusion = bf16[7168,384]{0,1:T(8,128)(2,1)} fusion(bf16[7168,128]{0,1:T(8,128)(2,1)} %bitcast.128, bf16[7168,128]{0,1:T(8,128)(2,1)S(1)} %bitcast.124, bf16[7168,128]{0,1:T(8,128)(2,1)} %bitcast.125), kind=kLoop, calls=%fused_computation.7 | loop fusion | flops 16515072 | bytes 11010048 | tf_op jit(solution)/shard_map/concatenate | solution.py:75
  48.8 52.7 %all-gather.2.cloned.1.call-done = bf16[288,7168]{1,0:T(8,128)(2,1)} async-done(((bf16[24,7168]{1,0:T(8,128)(2,1)}), bf16[288,7168]{1,0:T(8,128)(2,1)}) %all-gather.2.cloned.1.call-update) | async-done | bytes 4128784 | tf_op jit(solution)/shard_map/all_gather | solution.py:84
  101.5 6.3 %fusion.57 = f32[288,384]{1,0:T(8,128)S(1)} fusion(bf16[288,7168]{1,0:T(8,128)(2,1)} %all-gather.2.cloned.1.call-done, bf16[7168,384]{0,1:T(8,128)(2,1)} %pad_maximum_fusion), kind=kOutput, calls=%fused_computation.128 | convolution fusion | flops 1585446912 | bytes 10076160 | tf_op jit(solution)/shard_map/dot_general | solution.py:86
  108.1 4.3 %convolution_convert_fusion.1 = bf16[288,7168]{1,0:T(8,128)(2,1)} fusion(bf16[7168,384]{0,1:T(8,128)(2,1)S(1)} %copy-done.2, bf16[288,128]{1,0:T(8,128)(2,1)S(1)} %fusion.28, bf16[288,128]{1,0:T(8,128)(2,1)S(1)} %get-tuple-element.37, bf16[288,128]{1,0:T(8,128)(2,1)S(1)} %get-tuple-element.36), kind=kOutput, calls=%fused_computation.1 | convolution fusion | flops 1588174848 | bytes 9854976 | tf_op jit(solution)/shard_map/dot_general | solution.py:107
  112.5 5.7 %convolution_convert_fusion = bf16[7168,384]{1,0:T(8,128)(2,1)S(1)} fusion(bf16[288,7168]{1,0:T(8,128)(2,1)} %all-gather.2.cloned.1.call-done, bf16[288,128]{1,0:T(8,128)(2,1)S(1)} %fusion.28, bf16[288,128]{1,0:T(8,128)(2,1)S(1)} %get-tuple-element.37, bf16[288,128]{1,0:T(8,128)(2,1)S(1)} %get-tuple-element.36), kind=kOutput, calls=%fused_computation | convolution fusion | flops 1588862976 | bytes 9854976 | tf_op jit(solution)/shard_map/dot_general | solution.py:104
  118.9 1.4 pad_maximum_fusion.2
  120.3 3.1 %collective-permute-start.8 = (bf16[4,304,384]{2,1,0:T(8,128)(2,1)}, bf16[4,304,384]{2,1,0:T(8,128)(2,1)}, u32[]{:S(2)}, u32[]{:S(2)}) collective-permute-start(bf16[4,304,384]{2,1,0:T(8,128)(2,1)} %pad_maximum_fusion.2), channel_id=1, source_target_pairs={{0,48},{48,96},{96,144},{144,0},{1,49},{49,97},{97,145},{145,1},{2... | collective-permute-start | bytes 2801672 | tf_op jit(solution)/shard_map/ppermute | solution.py:29
  123.6 0.9 copy-done.3
  124.7 0.8 pad_maximum_fusion.4
  125.5 3.1 %collective-permute-start.1 = (bf16[4,144,384]{2,1,0:T(8,128)(2,1)}, bf16[4,144,384]{2,1,0:T(8,128)(2,1)S(1)}, u32[]{:S(2)}, u32[]{:S(2)}) collective-permute-start(bf16[4,144,384]{2,1,0:T(8,128)(2,1)} %pad_maximum_fusion.4), channel_id=1, source_target_pairs={{0,48},{48,96},{96,144},{144,0},{1,49},{49,97},{97,145},{145,1},{2... | collective-permute-start | bytes 1327112 | tf_op jit(solution)/shard_map/ppermute | solution.py:29
  128.6 1.1 pad_maximum_fusion.1
  129.7 3.4 %collective-permute-start.7 = (bf16[4,304,384]{2,1,0:T(8,128)(2,1)}, bf16[4,304,384]{2,1,0:T(8,128)(2,1)}, u32[]{:S(2)}, u32[]{:S(2)}) collective-permute-start(bf16[4,304,384]{2,1,0:T(8,128)(2,1)} %pad_maximum_fusion.1), channel_id=1, source_target_pairs={{0,144},{48,0},{96,48},{144,96},{1,145},{49,1},{97,49},{145,97},{2... | collective-permute-start | bytes 2801672 | tf_op jit(solution)/shard_map/ppermute | solution.py:29
  133.1 0.8 pad_maximum_fusion.3
  133.9 2.2 collective-permute-start
  136.1 14.3 %collective-permute-done.1 = bf16[4,144,384]{2,1,0:T(8,128)(2,1)S(1)} collective-permute-done((bf16[4,144,384]{2,1,0:T(8,128)(2,1)}, bf16[4,144,384]{2,1,0:T(8,128)(2,1)S(1)}, u32[]{:S(2)}, u32[]{:S(2)}) %collective-permute-start.1) | collective-permute-done | bytes 442400 | tf_op jit(solution)/shard_map/ppermute | solution.py:29
  150.4 1.2 fusion.14
  151.6 6.4 %collective-permute-done = bf16[4,144,384]{2,1,0:T(8,128)(2,1)} collective-permute-done((bf16[4,144,384]{2,1,0:T(8,128)(2,1)}, bf16[4,144,384]{2,1,0:T(8,128)(2,1)}, u32[]{:S(2)}, u32[]{:S(2)}) %collective-permute-start) | collective-permute-done | bytes 442400 | tf_op jit(solution)/shard_map/ppermute | solution.py:29
  158.0 1.0 fusion.13
  159.0 2.8 %collective-permute-start.2 = (bf16[2,144,384]{2,1,0:T(8,128)(2,1)S(1)}, bf16[2,144,384]{2,1,0:T(8,128)(2,1)S(1)}, u32[]{:S(2)}, u32[]{:S(2)}) collective-permute-start(bf16[2,144,384]{2,1,0:T(8,128)(2,1)S(1)} %fusion.14), channel_id=1, source_target_pairs={{0,48},{48,96},{96,144},{144,0},{1,49},{49,97},{97,145},{145,1},{2... | collective-permute-start | bytes 663560 | tf_op jit(solution)/shard_map/ppermute | solution.py:29
  161.8 3.9 %collective-permute-start.3 = (bf16[2,144,384]{2,1,0:T(8,128)(2,1)S(1)}, bf16[2,144,384]{2,1,0:T(8,128)(2,1)S(1)}, u32[]{:S(2)}, u32[]{:S(2)}) collective-permute-start(bf16[2,144,384]{2,1,0:T(8,128)(2,1)S(1)} %fusion.13), channel_id=1, source_target_pairs={{0,144},{48,0},{96,48},{144,96},{1,145},{49,1},{97,49},{145,97},{2... | collective-permute-start | bytes 663560 | tf_op jit(solution)/shard_map/ppermute | solution.py:29
  165.7 1.3 fusion.5
  167.1 1.1 fusion.4
  168.2 1.9 collective-permute-start.9
  170.2 1.2 fusion.16
  171.3 4.6 %collective-permute-start.10 = (bf16[2,304,384]{2,1,0:T(8,128)(2,1)S(1)}, bf16[2,304,384]{2,1,0:T(8,128)(2,1)S(1)}, u32[]{:S(2)}, u32[]{:S(2)}) collective-permute-start(bf16[2,304,384]{2,1,0:T(8,128)(2,1)S(1)} %fusion.4), channel_id=1, source_target_pairs={{0,144},{48,0},{96,48},{144,96},{1,145},{49,1},{97,49},{145,97},{2... | collective-permute-start | bytes 1400840 | tf_op jit(solution)/shard_map/ppermute | solution.py:29
  175.9 1.0 fusion.12
  176.9 0.8 fusion.39
  177.8 5.0 %collective-permute-start.6 = (bf16[144,384]{1,0:T(8,128)(2,1)}, bf16[144,384]{1,0:T(8,128)(2,1)S(1)}, u32[]{:S(2)}, u32[]{:S(2)}) collective-permute-start(bf16[144,384]{1,0:T(8,128)(2,1)} %get-tuple-element.40), channel_id=1, source_target_pairs={{0,576},{192,0},{384,192},{576,384},{1,577},{193,1},{385,193},{577... | collective-permute-start | bytes 331784 | tf_op jit(solution)/shard_map/ppermute | solution.py:29
  182.7 1.9 collective-permute-start.5
  184.7 2.4 collective-permute-start.4
  187.1 1.3 fusion.7
  188.5 1.2 fusion.3
  190.0 4.6 %collective-permute-start.13 = (bf16[304,384]{1,0:T(8,128)(2,1)S(1)}, bf16[304,384]{1,0:T(8,128)(2,1)S(1)}, u32[]{:S(2)}, u32[]{:S(2)}) collective-permute-start(bf16[304,384]{1,0:T(8,128)(2,1)S(1)} %get-tuple-element.31), channel_id=1, source_target_pairs={{0,576},{192,0},{384,192},{576,384},{1,577},{193,1},{385,193},{577... | collective-permute-start | bytes 700424 | tf_op jit(solution)/shard_map/ppermute | solution.py:29
  194.7 2.2 collective-permute-start.12
  196.9 1.9 reshape.122
  198.8 12.7 %all-to-all-start.1 = ((bf16[4,6,7168]{2,1,0:T(8,128)(2,1)}), bf16[4,6,7168]{2,1,0:T(8,128)(2,1)S(1)}, u32[]{:S(2)}, u32[]{:S(2)}) async-start(bf16[4,6,7168]{2,1,0:T(8,128)(2,1)} %reshape.122), calls=%async_computation.2 | async-start | bytes 917504 | tf_op jit(solution)/shard_map/all_to_all | solution.py:112
  211.5 3.6 %collective-permute-start.11 = (bf16[304,384]{1,0:T(8,128)(2,1)S(1)}, bf16[304,384]{1,0:T(8,128)(2,1)S(1)}, u32[]{:S(2)}, u32[]{:S(2)}) collective-permute-start(bf16[304,384]{1,0:T(8,128)(2,1)S(1)} %get-tuple-element.29), channel_id=1, source_target_pairs={{0,384},{192,576},{384,0},{576,192},{1,385},{193,577},{385,1},{577... | collective-permute-start | bytes 700424 | tf_op jit(solution)/shard_map/ppermute | solution.py:29
  215.1 1.1 fusion.27
  216.1 20.2 %collective-permute-done.11 = bf16[304,384]{1,0:T(8,128)(2,1)S(1)} collective-permute-done((bf16[304,384]{1,0:T(8,128)(2,1)S(1)}, bf16[304,384]{1,0:T(8,128)(2,1)S(1)}, u32[]{:S(2)}, u32[]{:S(2)}) %collective-permute-start.11) | collective-permute-done | bytes 233504 | tf_op jit(solution)/shard_map/ppermute | solution.py:29
  237.4 0.9 convolution_convert_fusion.2
  238.3 0.9 convolution_convert_fusion.3
  (58 shorter events, 4.5 us)
Async XLA Ops:
  7.2 3.1 %copy-start = (bf16[6,7168]{1,0:T(8,128)(2,1)S(1)}, bf16[6,7168]{1,0:T(8,128)(2,1)}, u32[]{:S(2)}) copy-start(bf16[6,7168]{1,0:T(8,128)(2,1)} %param.7) | copy-start | bytes 258052
  7.2 94.3 %all-gather.2.cloned.1.call-start = ((), (), s32[]{:S(2)}) async-start(), calls=%async_computation.3 | async-start | bytes 4472832 | tf_op jit(solution)/shard_map/all_gather | solution.py:84
  37.0 159.9 %reduce-scatter.2.cloned.1.call-start = ((), (), s32[]{:S(2)}) async-start(), calls=%async_computation.4 | async-start | bytes 4472832 | tf_op jit(solution)/shard_map/reduce_scatter | solution.py:110
  101.5 6.6 %copy-start.2 = (bf16[7168,384]{0,1:T(8,128)(2,1)S(1)}, bf16[7168,384]{0,1:T(8,128)(2,1)}, u32[]{:S(2)}) copy-start(bf16[7168,384]{0,1:T(8,128)(2,1)} %pad_maximum_fusion) | copy-start | bytes 16515076
  118.7 4.9 %copy-start.1 = (bf16[2,4,304,384]{3,2,1,0:T(8,128)(2,1)}, bf16[2,4,304,384]{3,2,1,0:T(8,128)(2,1)S(1)}, u32[]{:S(2)}) copy-start(bf16[2,4,304,384]{3,2,1,0:T(8,128)(2,1)S(1)} %get-tuple-element.23) | copy-start | bytes 5603332
  120.3 45.4 %collective-permute-start.8 = (bf16[4,304,384]{2,1,0:T(8,128)(2,1)}, bf16[4,304,384]{2,1,0:T(8,128)(2,1)}, u32[]{:S(2)}, u32[]{:S(2)}) collective-permute-start(bf16[4,304,384]{2,1,0:T(8,128)(2,1)} %pad_maximum_fusion.2), channel_id=1, source_target_pairs={{0,48},{48,96},{96,144},{144,0},{1,49},{49,97},{97,145},{145,1},{2... | collective-permute-start | bytes 2801672 | tf_op jit(solution)/shard_map/ppermute | solution.py:29
  123.6 0.9 copy-start.3
  125.5 24.9 %collective-permute-start.1 = (bf16[4,144,384]{2,1,0:T(8,128)(2,1)}, bf16[4,144,384]{2,1,0:T(8,128)(2,1)S(1)}, u32[]{:S(2)}, u32[]{:S(2)}) collective-permute-start(bf16[4,144,384]{2,1,0:T(8,128)(2,1)} %pad_maximum_fusion.4), channel_id=1, source_target_pairs={{0,48},{48,96},{96,144},{144,0},{1,49},{49,97},{97,145},{145,1},{2... | collective-permute-start | bytes 1327112 | tf_op jit(solution)/shard_map/ppermute | solution.py:29
  129.7 37.4 %collective-permute-start.7 = (bf16[4,304,384]{2,1,0:T(8,128)(2,1)}, bf16[4,304,384]{2,1,0:T(8,128)(2,1)}, u32[]{:S(2)}, u32[]{:S(2)}) collective-permute-start(bf16[4,304,384]{2,1,0:T(8,128)(2,1)} %pad_maximum_fusion.1), channel_id=1, source_target_pairs={{0,144},{48,0},{96,48},{144,96},{1,145},{49,1},{97,49},{145,97},{2... | collective-permute-start | bytes 2801672 | tf_op jit(solution)/shard_map/ppermute | solution.py:29
  133.9 24.1 %collective-permute-start = (bf16[4,144,384]{2,1,0:T(8,128)(2,1)}, bf16[4,144,384]{2,1,0:T(8,128)(2,1)}, u32[]{:S(2)}, u32[]{:S(2)}) collective-permute-start(bf16[4,144,384]{2,1,0:T(8,128)(2,1)} %pad_maximum_fusion.3), channel_id=1, source_target_pairs={{0,144},{48,0},{96,48},{144,96},{1,145},{49,1},{97,49},{145,97},{2... | collective-permute-start | bytes 1327112 | tf_op jit(solution)/shard_map/ppermute | solution.py:29
  150.4 19.7 %copy-start.4 = (bf16[4,144,384]{2,1,0:T(8,128)(2,1)}, bf16[4,144,384]{2,1,0:T(8,128)(2,1)S(1)}, u32[]{:S(2)}) copy-start(bf16[4,144,384]{2,1,0:T(8,128)(2,1)S(1)} %collective-permute-done.1) | copy-start | bytes 1327108
  159.0 11.1 %collective-permute-start.2 = (bf16[2,144,384]{2,1,0:T(8,128)(2,1)S(1)}, bf16[2,144,384]{2,1,0:T(8,128)(2,1)S(1)}, u32[]{:S(2)}, u32[]{:S(2)}) collective-permute-start(bf16[2,144,384]{2,1,0:T(8,128)(2,1)S(1)} %fusion.14), channel_id=1, source_target_pairs={{0,48},{48,96},{96,144},{144,0},{1,49},{49,97},{97,145},{145,1},{2... | collective-permute-start | bytes 663560 | tf_op jit(solution)/shard_map/ppermute | solution.py:29
  161.8 14.1 %collective-permute-start.3 = (bf16[2,144,384]{2,1,0:T(8,128)(2,1)S(1)}, bf16[2,144,384]{2,1,0:T(8,128)(2,1)S(1)}, u32[]{:S(2)}, u32[]{:S(2)}) collective-permute-start(bf16[2,144,384]{2,1,0:T(8,128)(2,1)S(1)} %fusion.13), channel_id=1, source_target_pairs={{0,144},{48,0},{96,48},{144,96},{1,145},{49,1},{97,49},{145,97},{2... | collective-permute-start | bytes 663560 | tf_op jit(solution)/shard_map/ppermute | solution.py:29
  168.2 18.9 %collective-permute-start.9 = (bf16[2,304,384]{2,1,0:T(8,128)(2,1)S(1)}, bf16[2,304,384]{2,1,0:T(8,128)(2,1)S(1)}, u32[]{:S(2)}, u32[]{:S(2)}) collective-permute-start(bf16[2,304,384]{2,1,0:T(8,128)(2,1)S(1)} %fusion.5), channel_id=1, source_target_pairs={{0,48},{48,96},{96,144},{144,0},{1,49},{49,97},{97,145},{145,1},{2... | collective-permute-start | bytes 1400840 | tf_op jit(solution)/shard_map/ppermute | solution.py:29
  171.3 17.2 %collective-permute-start.10 = (bf16[2,304,384]{2,1,0:T(8,128)(2,1)S(1)}, bf16[2,304,384]{2,1,0:T(8,128)(2,1)S(1)}, u32[]{:S(2)}, u32[]{:S(2)}) collective-permute-start(bf16[2,304,384]{2,1,0:T(8,128)(2,1)S(1)} %fusion.4), channel_id=1, source_target_pairs={{0,144},{48,0},{96,48},{144,96},{1,145},{49,1},{97,49},{145,97},{2... | collective-permute-start | bytes 1400840 | tf_op jit(solution)/shard_map/ppermute | solution.py:29
  177.8 33.7 %collective-permute-start.6 = (bf16[144,384]{1,0:T(8,128)(2,1)}, bf16[144,384]{1,0:T(8,128)(2,1)S(1)}, u32[]{:S(2)}, u32[]{:S(2)}) collective-permute-start(bf16[144,384]{1,0:T(8,128)(2,1)} %get-tuple-element.40), channel_id=1, source_target_pairs={{0,576},{192,0},{384,192},{576,384},{1,577},{193,1},{385,193},{577... | collective-permute-start | bytes 331784 | tf_op jit(solution)/shard_map/ppermute | solution.py:29
  182.7 32.3 %collective-permute-start.5 = (bf16[144,384]{1,0:T(8,128)(2,1)}, bf16[144,384]{1,0:T(8,128)(2,1)}, u32[]{:S(2)}, u32[]{:S(2)}) collective-permute-start(bf16[144,384]{1,0:T(8,128)(2,1)} %get-tuple-element.39), channel_id=1, source_target_pairs={{0,192},{192,384},{384,576},{576,0},{1,193},{193,385},{385,577},{5... | collective-permute-start | bytes 331784 | tf_op jit(solution)/shard_map/ppermute | solution.py:29
  184.7 30.4 %collective-permute-start.4 = (bf16[144,384]{1,0:T(8,128)(2,1)}, bf16[144,384]{1,0:T(8,128)(2,1)}, u32[]{:S(2)}, u32[]{:S(2)}) collective-permute-start(bf16[144,384]{1,0:T(8,128)(2,1)} %get-tuple-element.38), channel_id=1, source_target_pairs={{0,384},{192,576},{384,0},{576,192},{1,385},{193,577},{385,1},{577... | collective-permute-start | bytes 331784 | tf_op jit(solution)/shard_map/ppermute | solution.py:29
  190.0 26.1 %collective-permute-start.13 = (bf16[304,384]{1,0:T(8,128)(2,1)S(1)}, bf16[304,384]{1,0:T(8,128)(2,1)S(1)}, u32[]{:S(2)}, u32[]{:S(2)}) collective-permute-start(bf16[304,384]{1,0:T(8,128)(2,1)S(1)} %get-tuple-element.31), channel_id=1, source_target_pairs={{0,576},{192,0},{384,192},{576,384},{1,577},{193,1},{385,193},{577... | collective-permute-start | bytes 700424 | tf_op jit(solution)/shard_map/ppermute | solution.py:29
  194.7 21.4 %collective-permute-start.12 = (bf16[304,384]{1,0:T(8,128)(2,1)S(1)}, bf16[304,384]{1,0:T(8,128)(2,1)S(1)}, u32[]{:S(2)}, u32[]{:S(2)}) collective-permute-start(bf16[304,384]{1,0:T(8,128)(2,1)S(1)} %get-tuple-element.30), channel_id=1, source_target_pairs={{0,192},{192,384},{384,576},{576,0},{1,193},{193,385},{385,577},{5... | collective-permute-start | bytes 700424 | tf_op jit(solution)/shard_map/ppermute | solution.py:29
  198.8 38.5 %all-to-all-start.1 = ((bf16[4,6,7168]{2,1,0:T(8,128)(2,1)}), bf16[4,6,7168]{2,1,0:T(8,128)(2,1)S(1)}, u32[]{:S(2)}, u32[]{:S(2)}) async-start(bf16[4,6,7168]{2,1,0:T(8,128)(2,1)} %reshape.122), calls=%async_computation.2 | async-start | bytes 917504 | tf_op jit(solution)/shard_map/all_to_all | solution.py:112
  211.5 24.8 %collective-permute-start.11 = (bf16[304,384]{1,0:T(8,128)(2,1)S(1)}, bf16[304,384]{1,0:T(8,128)(2,1)S(1)}, u32[]{:S(2)}, u32[]{:S(2)}) collective-permute-start(bf16[304,384]{1,0:T(8,128)(2,1)S(1)} %get-tuple-element.29), channel_id=1, source_target_pairs={{0,384},{192,576},{384,0},{576,192},{1,385},{193,577},{385,1},{577... | collective-permute-start | bytes 700424 | tf_op jit(solution)/shard_map/ppermute | solution.py:29
Sparse Core Ops, SparseCore 0:
  37.1 64.3 all-gather.1
  112.6 64.0 reduce-scatter.1

commit v6 on v2

--- a/solution.py
+++ b/solution.py
@@ -59,11 +59,12 @@
         def target(step):
             return lax.dynamic_index_in_dim(mine, (py + step) % ny, 0, keepdims=False)
 
-        done.append(total(target(0), *[shift(target(step), "yl", step) for step in range(1, ny)]))
+        others = [shift(target(step), "yl", step) for step in range(1, ny)]
+        done.append(total(target(0), *others))
     return jnp.concatenate(done, axis=0)
 
 
-def local(hidden, grad_out, routes, combine, w_gate, w_up, w_down):
+def layer(hidden, grad_out, routes, combine, w_gate, w_up, w_down):
     experts = lax.axis_size("yh") * lax.axis_size("c")
     width = hidden.shape[1]
     f_dev = w_gate.shape[2]
@@ -111,7 +112,8 @@
     grads = scatter_shares(shares, 2)
     back = lax.all_to_all(
         summed.reshape(experts, own // experts, width), ("yh", "c"), split_axis=0, concat_axis=0, tiled=True
-    ).reshape(own, width).astype(jnp.float32)
+    )
+    back = back.reshape(own, width).astype(jnp.float32)
     high = lax.Precision.HIGHEST
     layer_out = jnp.dot(mix_out.T, back, precision=high).astype(bf16)
     grad_in = jnp.dot(pick_tok.T, back, precision=high).astype(bf16)
@@ -126,7 +128,7 @@
     dp, echip = ("yl", "x"), ("yh", "c")
     every = dp + ("z",) + echip
     return jax.shard_map(
-        local,
+        layer,
         mesh=fine,
         in_specs=(
             P(every, None),

time: 225 us -> 225 us (level)
  no operation moved by 1% of the time
where the time goes in v6:
time: 225 us; the launch traced here: 224 us
  waiting for transfers between devices  82.9 us (37%)
  starting transfers between devices  66.5 us (30%)
  blocking collectives  22.9 us (10%)
  matrix products  18.9 us (8%)
  between operations  14.7 us (7%)
  local copies, waits for them, and re-layouts  13.9 us (6%)
  other arithmetic  3.94 us (2%)
    all_gather x1, waiting for transfers between devices, layer(): rows = lax.all_gather(got, 'z', axis=0, tiled=True)  62.1 us
    ppermute x18, starting transfers between devices, shift(): lax.ppermute(value, axis, [(i, (i + step) % size) for i in range(size)])  61.2 us
    all_to_all x1, blocking collectives, layer(): lax.all_to_all(send.reshape(experts, own // experts, width), ('yh', 'c'),...  22.9 us
    ppermute x18, waiting for transfers between devices, shift(): lax.ppermute(value, axis, [(i, (i + step) % size) for i in range(size)])  12.8 us
    all_to_all x1, waiting for transfers between devices, layer(): lax.all_to_all(summed.reshape(experts, own // experts, width), ('yh', 'c'...  7.94 us
    unnamed x13, local copies, waits for them, and re-layouts  7.09 us
    dot_general x1, matrix products, layer(): lax.dot_general(rows, mids, (((0,), (0,)), ((), ())), preferred_element_t...  5.74 us
    dot_general x1, matrix products, layer(): pre = jnp.dot(rows, weights, preferred_element_type=jnp.float32)  5.73 us
  transfers between devices with their start and end apart: 21, of which 6 were waited for; matrix products, arithmetic and copies ran while one was open for 8% of the time, Pallas kernels for 0%

profile of v6, /device:TPU:8, one launch (start us, length us, event | category | flops | bytes accessed | tf_op | source)
XLA Modules:
  0.0 223.6 jit_solution(13615890083432252139)
XLA Ops:
  7.2 0.9 fusion.56
  8.3 0.2 convert_reduce_fusion
  8.8 0.9 fusion.55
  10.3 0.3 fusion.47
  10.7 1.3 fusion.1
  12.1 22.9 %all_to_all.10 = bf16[4,6,7168]{2,1,0:T(8,128)(2,1)S(1)} all-to-all(bf16[4,6,7168]{2,1,0:T(8,128)(2,1)S(1)} %reshape.120), channel_id=1, replica_groups=mesh['yl'=4,'x'=4,'z'=12,'yh'=2,'c'=2] {'yh','c'}, dimensions={0} | all-to-all | bytes 688128 | tf_op jit(solution)/shard_map/all_to_all | solution.py:82
  35.0 0.9 reshape.121
  36.0 2.9 %copy.56 = bf16[1,7168,128]{1,2,0:T(8,128)(2,1)} copy(bf16[1,7168,128]{2,1,0:T(8,128)(2,1)S(1)} %copy-done.1) | data formatting | bytes 3670016 | tf_op args[5]
  39.0 4.0 %copy.55 = bf16[1,7168,128]{1,2,0:T(8,128)(2,1)} copy(bf16[1,7168,128]{2,1,0:T(8,128)(2,1)} %param.11) | data formatting | bytes 3670016 | tf_op args[4]
  43.0 62.1 %all-gather.2.cloned.1.call-done = bf16[288,7168]{1,0:T(8,128)(2,1)} async-done(((bf16[24,7168]{1,0:T(8,128)(2,1)}), bf16[288,7168]{1,0:T(8,128)(2,1)}) %all-gather.2.cloned.1.call-update) | async-done | bytes 4128784 | tf_op jit(solution)/shard_map/all_gather | solution.py:85
  105.2 5.7 %fusion.2 = f32[288,384]{1,0:T(8,128)S(1)} fusion(bf16[288,7168]{1,0:T(8,128)(2,1)} %all-gather.2.cloned.1.call-done, bf16[7168,128]{0,1:T(8,128)(2,1)} %bitcast.129, bf16[7168,128]{0,1:T(8,128)(2,1)S(1)} %bitcast.123, bf16[7168,128]{0,1:T(8,128)(2,1)} %bitcast.125), kind=kOutput, calls=%fused_computation.8 | convolution fusion | flops 1601961984 | bytes 10076160 | tf_op jit(solution)/shard_map/dot_general | solution.py:87
  111.2 3.9 %convolution_convert_fusion.1 = bf16[288,7168]{1,0:T(8,128)(2,1)} fusion(bf16[7168,128]{0,1:T(8,128)(2,1)S(1)} %bitcast.130, bf16[7168,128]{0,1:T(8,128)(2,1)S(1)} %bitcast.124, bf16[7168,128]{0,1:T(8,128)(2,1)S(1)} %bitcast.126, bf16[288,128]{1,0:T(8,128)(2,1)S(1)} %fusion.37, bf16[288,128]{1,0:T(8,128)(2,1)S(1)} %get-tuple-element.32, ...), kind=kOutput, calls=%fused_computation.1 | convolution fusion | flops 1604689920 | bytes 9854976 | tf_op jit(solution)/shard_map/dot_general | solution.py:108
  115.3 5.7 %convolution_convert_fusion = bf16[7168,384]{1,0:T(8,128)(2,1)S(1)} fusion(bf16[288,7168]{1,0:T(8,128)(2,1)} %all-gather.2.cloned.1.call-done, bf16[288,128]{1,0:T(8,128)(2,1)S(1)} %fusion.37, bf16[288,128]{1,0:T(8,128)(2,1)S(1)} %get-tuple-element.32, bf16[288,128]{1,0:T(8,128)(2,1)S(1)} %get-tuple-element.31), kind=kOutput, calls=%fused_computation | convolution fusion | flops 1588862976 | bytes 9854976 | tf_op jit(solution)/shard_map/dot_general | solution.py:105
  121.0 0.8 fusion.57
  121.9 3.4 %collective-permute-start.10 = (bf16[2,224,384]{2,1,0:T(8,128)(2,1)S(1)}, bf16[2,224,384]{2,1,0:T(8,128)(2,1)S(1)}, u32[]{:S(2)}, u32[]{:S(2)}) collective-permute-start(bf16[2,224,384]{2,1,0:T(8,128)(2,1)S(1)} %get-tuple-element.20), channel_id=1, source_target_pairs={{0,48},{48,96},{96,144},{144,0},{1,49},{49,97},{97,145},{145,1},{2... | collective-permute-start | bytes 1032200 | tf_op jit(solution)/shard_map/ppermute | solution.py:29
  125.3 3.7 %collective-permute-start.9 = (bf16[2,224,384]{2,1,0:T(8,128)(2,1)S(1)}, bf16[2,224,384]{2,1,0:T(8,128)(2,1)S(1)}, u32[]{:S(2)}, u32[]{:S(2)}) collective-permute-start(bf16[2,224,384]{2,1,0:T(8,128)(2,1)S(1)} %get-tuple-element.19), channel_id=1, source_target_pairs={{0,144},{48,0},{96,48},{144,96},{1,145},{49,1},{97,49},{145,97},{2... | collective-permute-start | bytes 1032200 | tf_op jit(solution)/shard_map/ppermute | solution.py:29
  129.1 3.4 %collective-permute-start.13 = (bf16[2,224,384]{2,1,0:T(8,128)(2,1)S(1)}, bf16[2,224,384]{2,1,0:T(8,128)(2,1)S(1)}, u32[]{:S(2)}, u32[]{:S(2)}) collective-permute-start(bf16[2,224,384]{2,1,0:T(8,128)(2,1)S(1)} %get-tuple-element.18), channel_id=1, source_target_pairs={{0,144},{48,0},{96,48},{144,96},{1,145},{49,1},{97,49},{145,97},{2... | collective-permute-start | bytes 1032200 | tf_op jit(solution)/shard_map/ppermute | solution.py:29
  132.5 2.5 %collective-permute-start.12 = (bf16[2,224,384]{2,1,0:T(8,128)(2,1)S(1)}, bf16[2,224,384]{2,1,0:T(8,128)(2,1)S(1)}, u32[]{:S(2)}, u32[]{:S(2)}) collective-permute-start(bf16[2,224,384]{2,1,0:T(8,128)(2,1)S(1)} %get-tuple-element.17), channel_id=1, source_target_pairs={{0,48},{48,96},{96,144},{144,0},{1,49},{49,97},{97,145},{145,1},{2... | collective-permute-start | bytes 1032200 | tf_op jit(solution)/shard_map/ppermute | solution.py:29
  135.1 2.2 collective-permute-start.1
  137.4 4.9 %collective-permute-start = (bf16[2,224,384]{2,1,0:T(8,128)(2,1)S(1)}, bf16[2,224,384]{2,1,0:T(8,128)(2,1)S(1)}, u32[]{:S(2)}, u32[]{:S(2)}) collective-permute-start(bf16[2,224,384]{2,1,0:T(8,128)(2,1)S(1)} %get-tuple-element.23), channel_id=1, source_target_pairs={{0,144},{48,0},{96,48},{144,96},{1,145},{49,1},{97,49},{145,97},{2... | collective-permute-start | bytes 1032200 | tf_op jit(solution)/shard_map/ppermute | solution.py:29
  142.4 1.1 collective-permute-done.13
  143.5 3.7 %collective-permute-start.4 = (bf16[2,224,384]{2,1,0:T(8,128)(2,1)S(1)}, bf16[2,224,384]{2,1,0:T(8,128)(2,1)S(1)}, u32[]{:S(2)}, u32[]{:S(2)}) collective-permute-start(bf16[2,224,384]{2,1,0:T(8,128)(2,1)S(1)} %get-tuple-element.22), channel_id=1, source_target_pairs={{0,144},{48,0},{96,48},{144,96},{1,145},{49,1},{97,49},{145,97},{2... | collective-permute-start | bytes 1032200 | tf_op jit(solution)/shard_map/ppermute | solution.py:29
  147.3 0.7 collective-permute-done.1
  148.0 2.2 collective-permute-start.11
  150.3 4.1 %collective-permute-done.4 = bf16[2,224,384]{2,1,0:T(8,128)(2,1)S(1)} collective-permute-done((bf16[2,224,384]{2,1,0:T(8,128)(2,1)S(1)}, bf16[2,224,384]{2,1,0:T(8,128)(2,1)S(1)}, u32[]{:S(2)}, u32[]{:S(2)}) %collective-permute-start.4) | collective-permute-done | bytes 344096 | tf_op jit(solution)/shard_map/ppermute | solution.py:29
  154.5 4.9 %collective-permute-start.14 = (bf16[2,224,384]{2,1,0:T(8,128)(2,1)S(1)}, bf16[2,224,384]{2,1,0:T(8,128)(2,1)S(1)}, u32[]{:S(2)}, u32[]{:S(2)}) collective-permute-start(bf16[2,224,384]{2,1,0:T(8,128)(2,1)S(1)} %fusion.3), channel_id=1, source_target_pairs={{0,144},{48,0},{96,48},{144,96},{1,145},{49,1},{97,49},{145,97},{2... | collective-permute-start | bytes 1032200 | tf_op jit(solution)/shard_map/ppermute | solution.py:29
  159.5 1.9 collective-permute-start.3
  161.4 2.4 %collective-permute-start.2 = (bf16[2,224,384]{2,1,0:T(8,128)(2,1)S(1)}, bf16[2,224,384]{2,1,0:T(8,128)(2,1)S(1)}, u32[]{:S(2)}, u32[]{:S(2)}) collective-permute-start(bf16[2,224,384]{2,1,0:T(8,128)(2,1)S(1)} %fusion.12), channel_id=1, source_target_pairs={{0,48},{48,96},{96,144},{144,0},{1,49},{49,97},{97,145},{145,1},{2... | collective-permute-start | bytes 1032200 | tf_op jit(solution)/shard_map/ppermute | solution.py:29
  163.8 0.1 fusion.8
  164.0 4.6 %collective-permute-start.5 = (bf16[2,224,384]{2,1,0:T(8,128)(2,1)S(1)}, bf16[2,224,384]{2,1,0:T(8,128)(2,1)S(1)}, u32[]{:S(2)}, u32[]{:S(2)}) collective-permute-start(bf16[2,224,384]{2,1,0:T(8,128)(2,1)S(1)} %fusion.9), channel_id=1, source_target_pairs={{0,144},{48,0},{96,48},{144,96},{1,145},{49,1},{97,49},{145,97},{2... | collective-permute-start | bytes 1032200 | tf_op jit(solution)/shard_map/ppermute | solution.py:29
  168.6 0.1 fusion.5
  168.8 0.2 fusion.26
  169.0 2.4 %collective-permute-start.17 = (bf16[224,384]{1,0:T(8,128)(2,1)S(1)}, bf16[224,384]{1,0:T(8,128)(2,1)S(1)}, u32[]{:S(2)}, u32[]{:S(2)}) collective-permute-start(bf16[224,384]{1,0:T(8,128)(2,1)S(1)} %get-tuple-element.27), channel_id=1, source_target_pairs={{0,576},{192,0},{384,192},{576,384},{1,577},{193,1},{385,193},{577... | collective-permute-start | bytes 516104 | tf_op jit(solution)/shard_map/ppermute | solution.py:29
  171.5 4.3 %collective-permute-start.16 = (bf16[224,384]{1,0:T(8,128)(2,1)S(1)}, bf16[224,384]{1,0:T(8,128)(2,1)S(1)}, u32[]{:S(2)}, u32[]{:S(2)}) collective-permute-start(bf16[224,384]{1,0:T(8,128)(2,1)S(1)} %get-tuple-element.26), channel_id=1, source_target_pairs={{0,384},{192,576},{384,0},{576,192},{1,385},{193,577},{385,1},{577... | collective-permute-start | bytes 516104 | tf_op jit(solution)/shard_map/ppermute | solution.py:29
  175.8 4.3 %collective-permute-start.15 = (bf16[224,384]{1,0:T(8,128)(2,1)S(1)}, bf16[224,384]{1,0:T(8,128)(2,1)S(1)}, u32[]{:S(2)}, u32[]{:S(2)}) collective-permute-start(bf16[224,384]{1,0:T(8,128)(2,1)S(1)} %get-tuple-element.25), channel_id=1, source_target_pairs={{0,192},{192,384},{384,576},{576,0},{1,193},{193,385},{385,577},{5... | collective-permute-start | bytes 516104 | tf_op jit(solution)/shard_map/ppermute | solution.py:29
  180.4 1.0 fusion.34
  181.4 1.9 collective-permute-start.8
  183.3 3.6 %collective-permute-start.7 = (bf16[224,384]{1,0:T(8,128)(2,1)}, bf16[224,384]{1,0:T(8,128)(2,1)S(1)}, u32[]{:S(2)}, u32[]{:S(2)}) collective-permute-start(bf16[224,384]{1,0:T(8,128)(2,1)} %get-tuple-element.29), channel_id=1, source_target_pairs={{0,384},{192,576},{384,0},{576,192},{1,385},{193,577},{385,1},{577... | collective-permute-start | bytes 516104 | tf_op jit(solution)/shard_map/ppermute | solution.py:29
  187.0 1.9 reshape.122
  188.9 5.2 %all-to-all-start.1 = ((bf16[4,6,7168]{2,1,0:T(8,128)(2,1)}), bf16[4,6,7168]{2,1,0:T(8,128)(2,1)S(1)}, u32[]{:S(2)}, u32[]{:S(2)}) async-start(bf16[4,6,7168]{2,1,0:T(8,128)(2,1)} %reshape.122), calls=%async_computation.2 | async-start | bytes 917504 | tf_op jit(solution)/shard_map/all_to_all | solution.py:113
  194.1 4.8 %collective-permute-start.6 = (bf16[224,384]{1,0:T(8,128)(2,1)S(1)}, bf16[224,384]{1,0:T(8,128)(2,1)S(1)}, u32[]{:S(2)}, u32[]{:S(2)}) collective-permute-start(bf16[224,384]{1,0:T(8,128)(2,1)S(1)} %get-tuple-element.28), channel_id=1, source_target_pairs={{0,192},{192,384},{384,576},{576,0},{1,193},{193,385},{385,577},{5... | collective-permute-start | bytes 516104 | tf_op jit(solution)/shard_map/ppermute | solution.py:29
  199.0 0.2 fusion.17
  199.1 6.8 %collective-permute-done.6 = bf16[224,384]{1,0:T(8,128)(2,1)S(1)} collective-permute-done((bf16[224,384]{1,0:T(8,128)(2,1)S(1)}, bf16[224,384]{1,0:T(8,128)(2,1)S(1)}, u32[]{:S(2)}, u32[]{:S(2)}) %collective-permute-start.6) | collective-permute-done | bytes 172064 | tf_op jit(solution)/shard_map/ppermute | solution.py:29
  205.9 0.1 fusion.20
  206.1 0.7 fusion.42
  206.8 7.9 %all-to-all-done.1 = bf16[4,6,7168]{2,1,0:T(8,128)(2,1)S(1)} async-done(((bf16[4,6,7168]{2,1,0:T(8,128)(2,1)}), bf16[4,6,7168]{2,1,0:T(8,128)(2,1)S(1)}, u32[]{:S(2)}, u32[]{:S(2)}) %all-to-all-start.1) | async-done | bytes 344096 | tf_op jit(solution)/shard_map/all_to_all | solution.py:113
  214.9 0.9 convolution_convert_fusion.2
  215.8 0.9 convolution_convert_fusion.3
  (62 shorter events, 2.9 us)
Async XLA Ops:
  7.2 3.1 %copy-start = (bf16[6,7168]{1,0:T(8,128)(2,1)S(1)}, bf16[6,7168]{1,0:T(8,128)(2,1)}, u32[]{:S(2)}) copy-start(bf16[6,7168]{1,0:T(8,128)(2,1)} %param.7) | copy-start | bytes 258052
  7.2 98.0 %all-gather.2.cloned.1.call-start = ((), (), s32[]{:S(2)}) async-start(), calls=%async_computation.3 | async-start | bytes 4472832 | tf_op jit(solution)/shard_map/all_gather | solution.py:85
  10.6 25.4 %copy-start.1 = (bf16[1,7168,128]{2,1,0:T(8,128)(2,1)S(1)}, bf16[1,7168,128]{2,1,0:T(8,128)(2,1)}, u32[]{:S(2)}) copy-start(bf16[1,7168,128]{2,1,0:T(8,128)(2,1)} %param.12) | copy-start | bytes 5505028
  36.0 151.0 %reduce-scatter.2.cloned.1.call-start = ((), (), s32[]{:S(2)}) async-start(), calls=%async_computation.4 | async-start | bytes 4472832 | tf_op jit(solution)/shard_map/reduce_scatter | solution.py:111
  39.0 66.2 %copy-start.2 = (bf16[1,7168,128]{1,2,0:T(8,128)(2,1)S(1)}, bf16[1,7168,128]{1,2,0:T(8,128)(2,1)}, u32[]{:S(2)}) copy-start(bf16[1,7168,128]{1,2,0:T(8,128)(2,1)} %copy.56) | copy-start | bytes 5505028
  105.2 6.1 %copy-start.3 = (bf16[1,7168,128]{1,2,0:T(8,128)(2,1)S(1)}, bf16[1,7168,128]{1,2,0:T(8,128)(2,1)}, u32[]{:S(2)}) copy-start(bf16[1,7168,128]{1,2,0:T(8,128)(2,1)} %copy.55) | copy-start | bytes 5505028
  105.2 6.1 %copy-start.4 = (bf16[1,128,7168]{2,1,0:T(8,128)(2,1)S(1)}, bf16[1,128,7168]{2,1,0:T(8,128)(2,1)}, u32[]{:S(2)}) copy-start(bf16[1,128,7168]{2,1,0:T(8,128)(2,1)} %param.13) | copy-start | bytes 5505028
  121.9 15.4 %collective-permute-start.10 = (bf16[2,224,384]{2,1,0:T(8,128)(2,1)S(1)}, bf16[2,224,384]{2,1,0:T(8,128)(2,1)S(1)}, u32[]{:S(2)}, u32[]{:S(2)}) collective-permute-start(bf16[2,224,384]{2,1,0:T(8,128)(2,1)S(1)} %get-tuple-element.20), channel_id=1, source_target_pairs={{0,48},{48,96},{96,144},{144,0},{1,49},{49,97},{97,145},{145,1},{2... | collective-permute-start | bytes 1032200 | tf_op jit(solution)/shard_map/ppermute | solution.py:29
  125.3 34.2 %collective-permute-start.9 = (bf16[2,224,384]{2,1,0:T(8,128)(2,1)S(1)}, bf16[2,224,384]{2,1,0:T(8,128)(2,1)S(1)}, u32[]{:S(2)}, u32[]{:S(2)}) collective-permute-start(bf16[2,224,384]{2,1,0:T(8,128)(2,1)S(1)} %get-tuple-element.19), channel_id=1, source_target_pairs={{0,144},{48,0},{96,48},{144,96},{1,145},{49,1},{97,49},{145,97},{2... | collective-permute-start | bytes 1032200 | tf_op jit(solution)/shard_map/ppermute | solution.py:29
  129.1 14.4 %collective-permute-start.13 = (bf16[2,224,384]{2,1,0:T(8,128)(2,1)S(1)}, bf16[2,224,384]{2,1,0:T(8,128)(2,1)S(1)}, u32[]{:S(2)}, u32[]{:S(2)}) collective-permute-start(bf16[2,224,384]{2,1,0:T(8,128)(2,1)S(1)} %get-tuple-element.18), channel_id=1, source_target_pairs={{0,144},{48,0},{96,48},{144,96},{1,145},{49,1},{97,49},{145,97},{2... | collective-permute-start | bytes 1032200 | tf_op jit(solution)/shard_map/ppermute | solution.py:29
  132.5 31.5 %collective-permute-start.12 = (bf16[2,224,384]{2,1,0:T(8,128)(2,1)S(1)}, bf16[2,224,384]{2,1,0:T(8,128)(2,1)S(1)}, u32[]{:S(2)}, u32[]{:S(2)}) collective-permute-start(bf16[2,224,384]{2,1,0:T(8,128)(2,1)S(1)} %get-tuple-element.17), channel_id=1, source_target_pairs={{0,48},{48,96},{96,144},{144,0},{1,49},{49,97},{97,145},{145,1},{2... | collective-permute-start | bytes 1032200 | tf_op jit(solution)/shard_map/ppermute | solution.py:29
  135.1 12.9 %collective-permute-start.1 = (bf16[2,224,384]{2,1,0:T(8,128)(2,1)S(1)}, bf16[2,224,384]{2,1,0:T(8,128)(2,1)S(1)}, u32[]{:S(2)}, u32[]{:S(2)}) collective-permute-start(bf16[2,224,384]{2,1,0:T(8,128)(2,1)S(1)} %get-tuple-element.24), channel_id=1, source_target_pairs={{0,48},{48,96},{96,144},{144,0},{1,49},{49,97},{97,145},{145,1},{2... | collective-permute-start | bytes 1032200 | tf_op jit(solution)/shard_map/ppermute | solution.py:29
  137.4 34.1 %collective-permute-start = (bf16[2,224,384]{2,1,0:T(8,128)(2,1)S(1)}, bf16[2,224,384]{2,1,0:T(8,128)(2,1)S(1)}, u32[]{:S(2)}, u32[]{:S(2)}) collective-permute-start(bf16[2,224,384]{2,1,0:T(8,128)(2,1)S(1)} %get-tuple-element.23), channel_id=1, source_target_pairs={{0,144},{48,0},{96,48},{144,96},{1,145},{49,1},{97,49},{145,97},{2... | collective-permute-start | bytes 1032200 | tf_op jit(solution)/shard_map/ppermute | solution.py:29
  143.5 11.0 %collective-permute-start.4 = (bf16[2,224,384]{2,1,0:T(8,128)(2,1)S(1)}, bf16[2,224,384]{2,1,0:T(8,128)(2,1)S(1)}, u32[]{:S(2)}, u32[]{:S(2)}) collective-permute-start(bf16[2,224,384]{2,1,0:T(8,128)(2,1)S(1)} %get-tuple-element.22), channel_id=1, source_target_pairs={{0,144},{48,0},{96,48},{144,96},{1,145},{49,1},{97,49},{145,97},{2... | collective-permute-start | bytes 1032200 | tf_op jit(solution)/shard_map/ppermute | solution.py:29
  148.0 13.4 %collective-permute-start.11 = (bf16[2,224,384]{2,1,0:T(8,128)(2,1)S(1)}, bf16[2,224,384]{2,1,0:T(8,128)(2,1)S(1)}, u32[]{:S(2)}, u32[]{:S(2)}) collective-permute-start(bf16[2,224,384]{2,1,0:T(8,128)(2,1)S(1)} %fusion.6), channel_id=1, source_target_pairs={{0,48},{48,96},{96,144},{144,0},{1,49},{49,97},{97,145},{145,1},{2... | collective-permute-start | bytes 1032200 | tf_op jit(solution)/shard_map/ppermute | solution.py:29
  154.5 14.2 %collective-permute-start.14 = (bf16[2,224,384]{2,1,0:T(8,128)(2,1)S(1)}, bf16[2,224,384]{2,1,0:T(8,128)(2,1)S(1)}, u32[]{:S(2)}, u32[]{:S(2)}) collective-permute-start(bf16[2,224,384]{2,1,0:T(8,128)(2,1)S(1)} %fusion.3), channel_id=1, source_target_pairs={{0,144},{48,0},{96,48},{144,96},{1,145},{49,1},{97,49},{145,97},{2... | collective-permute-start | bytes 1032200 | tf_op jit(solution)/shard_map/ppermute | solution.py:29
  159.5 20.8 %collective-permute-start.3 = (bf16[2,224,384]{2,1,0:T(8,128)(2,1)S(1)}, bf16[2,224,384]{2,1,0:T(8,128)(2,1)S(1)}, u32[]{:S(2)}, u32[]{:S(2)}) collective-permute-start(bf16[2,224,384]{2,1,0:T(8,128)(2,1)S(1)} %get-tuple-element.21), channel_id=1, source_target_pairs={{0,48},{48,96},{96,144},{144,0},{1,49},{49,97},{97,145},{145,1},{2... | collective-permute-start | bytes 1032200 | tf_op jit(solution)/shard_map/ppermute | solution.py:29
  161.4 14.4 %collective-permute-start.2 = (bf16[2,224,384]{2,1,0:T(8,128)(2,1)S(1)}, bf16[2,224,384]{2,1,0:T(8,128)(2,1)S(1)}, u32[]{:S(2)}, u32[]{:S(2)}) collective-permute-start(bf16[2,224,384]{2,1,0:T(8,128)(2,1)S(1)} %fusion.12), channel_id=1, source_target_pairs={{0,48},{48,96},{96,144},{144,0},{1,49},{49,97},{97,145},{145,1},{2... | collective-permute-start | bytes 1032200 | tf_op jit(solution)/shard_map/ppermute | solution.py:29
  164.0 16.3 %collective-permute-start.5 = (bf16[2,224,384]{2,1,0:T(8,128)(2,1)S(1)}, bf16[2,224,384]{2,1,0:T(8,128)(2,1)S(1)}, u32[]{:S(2)}, u32[]{:S(2)}) collective-permute-start(bf16[2,224,384]{2,1,0:T(8,128)(2,1)S(1)} %fusion.9), channel_id=1, source_target_pairs={{0,144},{48,0},{96,48},{144,96},{1,145},{49,1},{97,49},{145,97},{2... | collective-permute-start | bytes 1032200 | tf_op jit(solution)/shard_map/ppermute | solution.py:29
  169.0 25.1 %collective-permute-start.17 = (bf16[224,384]{1,0:T(8,128)(2,1)S(1)}, bf16[224,384]{1,0:T(8,128)(2,1)S(1)}, u32[]{:S(2)}, u32[]{:S(2)}) collective-permute-start(bf16[224,384]{1,0:T(8,128)(2,1)S(1)} %get-tuple-element.27), channel_id=1, source_target_pairs={{0,576},{192,0},{384,192},{576,384},{1,577},{193,1},{385,193},{577... | collective-permute-start | bytes 516104 | tf_op jit(solution)/shard_map/ppermute | solution.py:29
  171.5 27.4 %collective-permute-start.16 = (bf16[224,384]{1,0:T(8,128)(2,1)S(1)}, bf16[224,384]{1,0:T(8,128)(2,1)S(1)}, u32[]{:S(2)}, u32[]{:S(2)}) collective-permute-start(bf16[224,384]{1,0:T(8,128)(2,1)S(1)} %get-tuple-element.26), channel_id=1, source_target_pairs={{0,384},{192,576},{384,0},{576,192},{1,385},{193,577},{385,1},{577... | collective-permute-start | bytes 516104 | tf_op jit(solution)/shard_map/ppermute | solution.py:29
  175.8 23.1 %collective-permute-start.15 = (bf16[224,384]{1,0:T(8,128)(2,1)S(1)}, bf16[224,384]{1,0:T(8,128)(2,1)S(1)}, u32[]{:S(2)}, u32[]{:S(2)}) collective-permute-start(bf16[224,384]{1,0:T(8,128)(2,1)S(1)} %get-tuple-element.25), channel_id=1, source_target_pairs={{0,192},{192,384},{384,576},{576,0},{1,193},{193,385},{385,577},{5... | collective-permute-start | bytes 516104 | tf_op jit(solution)/shard_map/ppermute | solution.py:29
  181.4 17.7 %collective-permute-start.8 = (bf16[224,384]{1,0:T(8,128)(2,1)}, bf16[224,384]{1,0:T(8,128)(2,1)S(1)}, u32[]{:S(2)}, u32[]{:S(2)}) collective-permute-start(bf16[224,384]{1,0:T(8,128)(2,1)} %get-tuple-element.30), channel_id=1, source_target_pairs={{0,576},{192,0},{384,192},{576,384},{1,577},{193,1},{385,193},{577... | collective-permute-start | bytes 516104 | tf_op jit(solution)/shard_map/ppermute | solution.py:29
  183.3 15.8 %collective-permute-start.7 = (bf16[224,384]{1,0:T(8,128)(2,1)}, bf16[224,384]{1,0:T(8,128)(2,1)S(1)}, u32[]{:S(2)}, u32[]{:S(2)}) collective-permute-start(bf16[224,384]{1,0:T(8,128)(2,1)} %get-tuple-element.29), channel_id=1, source_target_pairs={{0,384},{192,576},{384,0},{576,192},{1,385},{193,577},{385,1},{577... | collective-permute-start | bytes 516104 | tf_op jit(solution)/shard_map/ppermute | solution.py:29
  188.9 25.9 %all-to-all-start.1 = ((bf16[4,6,7168]{2,1,0:T(8,128)(2,1)}), bf16[4,6,7168]{2,1,0:T(8,128)(2,1)S(1)}, u32[]{:S(2)}, u32[]{:S(2)}) async-start(bf16[4,6,7168]{2,1,0:T(8,128)(2,1)} %reshape.122), calls=%async_computation.2 | async-start | bytes 917504 | tf_op jit(solution)/shard_map/all_to_all | solution.py:113
  194.1 11.8 %collective-permute-start.6 = (bf16[224,384]{1,0:T(8,128)(2,1)S(1)}, bf16[224,384]{1,0:T(8,128)(2,1)S(1)}, u32[]{:S(2)}, u32[]{:S(2)}) collective-permute-start(bf16[224,384]{1,0:T(8,128)(2,1)S(1)} %get-tuple-element.28), channel_id=1, source_target_pairs={{0,192},{192,384},{384,576},{576,0},{1,193},{193,385},{385,577},{5... | collective-permute-start | bytes 516104 | tf_op jit(solution)/shard_map/ppermute | solution.py:29
Sparse Core Ops, SparseCore 0:
  36.1 69.0 all-gather.1
  115.3 65.8 reduce-scatter.1
